TPU v7x, 128 devices: a whole 4x4x4 slice. The times are simulated.
128 devices in a mesh: row: 16 (over z, x_lo, core), col: 8 (over y, x_hi).
Axes of the slice: x: 4 (x_hi: 2, x_lo: 2; x = x_hi * 2 + x_lo), y: 4, z: 4, core: 2. Of those that a mesh axis runs over, the one named last changes fastest.
Arguments:
- genotypes: bfloat16 [5120, 16384], P(None, ('row', 'col')), may hold values from -5 to 5
- running: float32 [16384, 16, 8, 128], P('row', None, 'col'), as said below
- grid_map: int32 [16], replicated, may hold values from 0 to 15, each once
Outputs:
- factored: float32 [16, 16, 64, 16, 8, 128], P(None, 'row', None, None, 'col')
Inputs may be any that keep to these rules, and one draw needn't show every extreme that they name: running is symmetric, and in its first 128 rows each diagonal entry exceeds the sum of the magnitudes of the row's other entries among the first 128 columns. grid_map holds each of its values once.
All inputs are finite; a program needn't handle non-finite values.
Results may differ from a plain program's by a relative error of at most 0.0003.
Values may be sent and summed in bfloat16 or wider, within the bound.
No kernel may reach another device: no remote copies, remote signals or barrier semaphores. Data moves between devices by JAX's collectives and lax.ppermute only.
A program may use at most 128 MiB of HBM per device.

v0:
```python
import jax
import jax.numpy as jnp
from jax import lax
from jax.experimental import pallas as pl
from jax.experimental.pallas import tpu as pltpu
from jax.sharding import PartitionSpec as P


NB = 128
NZ, NX, NC = 4, 2, 2
NY, NH = 4, 2
STEP_OF_SLOT = (0, 3, 1, 2)
HALVES = 2
TILE_ROWS = 64 // HALVES
LEVELS = 32767.0
LOG_STEP = 0.6931471805599453 / 64.0


def row_perm(dz=0, fx=0, fc=0):
    return [
        ((z * NX + x) * NC + k, (((z + dz) % NZ) * NX + (x ^ fx)) * NC + (k ^ fc))
        for z in range(NZ)
        for x in range(NX)
        for k in range(NC)
    ]


def col_perm(dy=0, fh=0):
    return [(y * NH + h, ((y + dy) % NY) * NH + (h ^ fh)) for y in range(NY) for h in range(NH)]


def ring_sides(shard, axis, perm):
    return lax.ppermute(shard, axis, perm(1)), lax.ppermute(shard, axis, perm(-1))


def ring_relay(up, down, axis, perm):
    half = up.shape[0] // 2
    top = lax.ppermute(up[:half], axis, perm(1))
    bottom = lax.ppermute(down[half:], axis, perm(-1))
    return top, bottom


def ring_direct(shard, axis, perm):
    return [shard] + [lax.ppermute(shard, axis, perm(d)) for d in (1, -1, 2)]


def split_bf16(value):
    high = lax.reduce_precision(value, exponent_bits=8, mantissa_bits=7)
    return high.astype(jnp.bfloat16), (value - high).astype(jnp.bfloat16)


def epilogue_kernel(table, running, *refs, part, inv_snp):
    prods, (row_factor, col_factor, out, values) = refs[:4], refs[4:]
    step = pl.program_id(0)
    row_start = table[32 + step] + part * TILE_ROWS
    mine = row_factor[...]
    high = mine.astype(jnp.bfloat16)
    low = (mine - high.astype(jnp.float32)).astype(jnp.bfloat16)
    left = jnp.concatenate([high, high, low], axis=1)
    for group in range(4):
        outer = jnp.dot(
            left,
            col_factor[:, group * 512 : (group + 1) * 512],
            preferred_element_type=jnp.float32,
        )
        for side in range(4):
            place = table[48 + group * 4 + side]
            lanes = slice(side * 128, (side + 1) * 128)
            old = running[pl.ds(place, TILE_ROWS, stride=16), :]
            values[pl.ds(place, TILE_ROWS, stride=16), :] = (
                old + prods[group][:, lanes] * inv_snp - outer[:, lanes]
            )

    @pl.when(row_start < NB)
    def _():
        values[...] = jnp.zeros_like(values)

    @pl.when(table[64] == 1)
    def _():
        row_pos = row_start + lax.broadcasted_iota(jnp.int32, (TILE_ROWS, NB), 0)
        lane = lax.broadcasted_iota(jnp.int32, (TILE_ROWS, NB), 1)
        values[pl.ds(0, TILE_ROWS, stride=16), :] = jnp.where(row_pos >= lane, mine, 0.0)

    peak = jnp.full((16, 128), 1e-30, jnp.float32)
    for a in range(TILE_ROWS):
        peak = jnp.maximum(peak, jnp.abs(values[a * 16 : (a + 1) * 16, :]))
    code = jnp.minimum(jnp.ceil(jnp.log(peak) * (1.0 / LOG_STEP)) + 1.0, 8190.0)
    gain = LEVELS / jnp.exp(code * LOG_STEP)
    for a in range(TILE_ROWS):
        scaled = jnp.round(values[a * 16 : (a + 1) * 16, :] * gain)
        out[a * 16 : (a + 1) * 16, :] = scaled.astype(jnp.int32).astype(jnp.int16)
    out[TILE_ROWS * 16 :, :] = code.astype(jnp.int32).astype(jnp.int16)


def epilogue(part, table, running, prods, row_factor, col_factor, snp_count):
    block = pl.BlockSpec((TILE_ROWS, 512), lambda i, t: (t[16 + i] * HALVES + part, 0))
    return pl.pallas_call(
        lambda *refs: epilogue_kernel(*refs, part=part, inv_snp=1.0 / snp_count),
        grid_spec=pltpu.PrefetchScalarGridSpec(
            num_scalar_prefetch=1,
            grid=(16,),
            in_specs=[
                pl.BlockSpec((TILE_ROWS * 16, 128), lambda i, t: (t[i] * HALVES + part, 0)),
                *[block] * 4,
                pl.BlockSpec((TILE_ROWS, NB), lambda i, t: (t[16 + i] * HALVES + part, 0)),
                pl.BlockSpec((3 * NB, 2048), lambda i, t: (0, 0)),
            ],
            out_specs=pl.BlockSpec(((TILE_ROWS + 1) * 16, 128), lambda i, t: (i, 0)),
            scratch_shapes=[pltpu.VMEM((TILE_ROWS * 16, 128), jnp.float32)],
        ),
        out_shape=jax.ShapeDtypeStruct((16 * (TILE_ROWS + 1) * 16, 128), jnp.int16),
        name="epilogue",
    )(table, running, *prods, row_factor, col_factor)


ROW_STEP = 256
ROW_PLACES = ((0, 0, 0), (0, 1, 128), (1, 2, 0), (1, 3, 128), (2, 4, 0), (2, 5, 128))
ROW_PLACES += ((3, 6, 0), (3, 7, 64), (3, 8, 128), (3, 9, 192))


def fetch_rows(parts, rows, sems, others=()):
    step = pl.program_id(0)

    def copies(n):
        places = [(part, row) for where, part, row in ROW_PLACES if where == n]
        return [
            pltpu.make_async_copy(
                parts[part],
                rows.at[n % 2, row : row + parts[part].shape[0], :],
                sems.at[n % 2, number],
            )
            for number, (part, row) in enumerate(places)
        ]

    for n in range(4):

        @pl.when(step == n)
        def _():
            if n == 0:
                for copy in list(others) + copies(0):
                    copy.start()
            if n < 3:
                for copy in copies(n + 1):
                    copy.start()
            for copy in copies(n) + (list(others) if n == 0 else []):
                copy.wait()


def product_kernel(*refs):
    parts, shards, (out, rows, cols, row_sems, col_sems) = refs[:10], refs[10:14], refs[14:]
    others = [
        pltpu.make_async_copy(
            shards[n], cols.at[:, n * 128 : (n + 1) * 128], col_sems.at[n]
        )
        for n in range(4)
    ]
    fetch_rows(parts, rows, row_sems, others)
    out[...] = jnp.dot(
        rows[pl.program_id(0) % 2], cols[...], preferred_element_type=jnp.float32
    )


def product(parts, shards):
    count = shards[0].shape[0]
    return pl.pallas_call(
        product_kernel,
        grid=(4,),
        in_specs=[pl.BlockSpec(memory_space=pl.ANY)] * 14,
        out_specs=pl.BlockSpec((ROW_STEP, 512), lambda i: (i, 0)),
        scratch_shapes=[
            pltpu.VMEM((2, ROW_STEP, count), jnp.bfloat16),
            pltpu.VMEM((count, 512), jnp.bfloat16),
            pltpu.SemaphoreType.DMA((2, 4)),
            pltpu.SemaphoreType.DMA((4,)),
        ],
        out_shape=jax.ShapeDtypeStruct((4 * ROW_STEP, 512), jnp.float32),
        name="product",
    )(*parts, *shards)


def panel_kernel(pick, old, inverse, *refs, inv_snp):
    parts, shards, (out, rows, first, row_sems, sem) = refs[:10], refs[10:26], refs[26:]

    @pl.when(pl.program_id(0) == 0)
    def _():
        for n in range(16):

            @pl.when(pick[0] == n)
            def _():
                copy = pltpu.make_async_copy(shards[n], first, sem)
                copy.start()
                copy.wait()

    fetch_rows(parts, rows, row_sems)
    product_rows = jnp.dot(
        rows[pl.program_id(0) % 2], first[...], preferred_element_type=jnp.float32
    )
    out[...] = lax.dot_general(
        old[...] + product_rows * inv_snp,
        inverse[...],
        (((1,), (1,)), ((), ())),
        precision=lax.Precision.HIGHEST,
        preferred_element_type=jnp.float32,
    )


def panel(pick, old, inverse, parts, shards):
    count = shards[0].shape[0]
    block = pl.BlockSpec((ROW_STEP, NB), lambda i, t: (t[1 + i], 0))
    return pl.pallas_call(
        lambda *refs: panel_kernel(*refs, inv_snp=1.0 / count),
        grid_spec=pltpu.PrefetchScalarGridSpec(
            num_scalar_prefetch=1,
            grid=(4,),
            in_specs=[
                block,
                pl.BlockSpec((NB, NB), lambda i, t: (0, 0)),
                *[pl.BlockSpec(memory_space=pl.ANY)] * 26,
            ],
            out_specs=block,
            scratch_shapes=[
                pltpu.VMEM((2, ROW_STEP, count), jnp.bfloat16),
                pltpu.VMEM((count, NB), jnp.bfloat16),
                pltpu.SemaphoreType.DMA((2, 4)),
                pltpu.SemaphoreType.DMA(()),
            ],
        ),
        out_shape=jax.ShapeDtypeStruct((4 * ROW_STEP, NB), jnp.float32),
        name="panel",
    )(pick, old, inverse, *parts, *shards)


def unpack_kernel(coded, *refs):
    out = refs[-1]
    for source in range(2):
        code = coded[source, TILE_ROWS * 16 :, :].astype(jnp.float32)
        scale = jnp.exp(code * LOG_STEP) * (1.0 / LEVELS)
        for a in range(TILE_ROWS):
            values = coded[source, a * 16 : (a + 1) * 16, :].astype(jnp.float32)
            out[source, 0, a * 16 : (a + 1) * 16, :] = values * scale


def unpack(part, coded, before):
    begun = [] if before is None else [before]
    return pl.pallas_call(
        unpack_kernel,
        grid=(8,),
        in_specs=[
            pl.BlockSpec((2, (TILE_ROWS + 1) * 16, 128), lambda i: (i, 0, 0)),
            *[pl.BlockSpec(memory_space=pl.ANY)] * len(begun),
        ],
        out_specs=pl.BlockSpec((2, 1, TILE_ROWS * 16, 128), lambda i: (i, part, 0, 0)),
        out_shape=jax.ShapeDtypeStruct((16, HALVES, TILE_ROWS * 16, 128), jnp.float32),
        input_output_aliases={1: 0} if begun else {},
        name="unpack",
    )(coded, *begun)


def compute(genotypes, running, grid_map):
    row_index = lax.axis_index("row").astype(jnp.uint32)
    col_index = lax.axis_index("col").astype(jnp.uint32)
    z, x_lo, core = row_index >> 2, (row_index >> 1) & 1, row_index & 1
    y, x_hi = col_index >> 1, col_index & 1
    snp_count = genotypes.shape[0]
    inv_snp = 1.0 / snp_count

    def dot0(a, b):
        return lax.dot_general(a, b, (((0,), (0,)), ((), ())), preferred_element_type=jnp.float32)

    def twin(value):
        return lax.ppermute(value, "row", row_perm(0, 0, 1))

    z_up, z_down = ring_sides(genotypes, "row", row_perm)
    turned = genotypes.T
    across = lax.ppermute(turned, "col", col_perm(0, 1))
    y_up, y_down = ring_sides(turned, "col", col_perm)
    own_twin = twin(genotypes)

    leading = running[:NB, 0, 0, :] + dot0(genotypes, genotypes) * inv_snp
    lower = jnp.linalg.cholesky(leading)

    late, across, lower = lax.optimization_barrier((genotypes, across, lower))
    beside = lax.ppermute(late, "row", row_perm(0, 1, 0))
    y_up_across, y_down_across = ring_sides(across, "col", col_perm)
    z_opposite = jnp.concatenate(ring_relay(z_up, z_down, "row", row_perm), axis=0)
    y_opposite = ring_relay(y_up, y_down, "col", col_perm)
    z_up_twin, z_down_twin = twin(z_up), twin(z_down)
    inverse = lax.linalg.triangular_solve(
        lower, jnp.eye(NB, dtype=jnp.float32), left_side=True, lower=True
    )

    heard = sum(lax.ppermute(inverse, "row", [(0, d * NX * NC)]) for d in range(1, NZ))
    inverse = jnp.where(z == 0, inverse, heard)
    z_up_side, z_down_side = ring_sides(beside, "row", row_perm)
    heard = lax.ppermute(inverse, "row", [(d * NX * NC, d * NX * NC + NC) for d in range(NZ)])
    inverse = jnp.where(x_lo == 0, inverse, heard)
    z_opposite_side = lax.ppermute(z_opposite, "row", row_perm(0, 1, 0))
    y_opposite_across = ring_relay(y_up_across, y_down_across, "col", col_perm)
    heard = lax.ppermute(inverse, "row", [(d * NC, d * NC + 1) for d in range(NZ * NX)])
    inverse = jnp.where(core == 0, inverse, heard)

    row_parts = [turned, across, y_up, y_up_across, y_down, y_down_across]
    row_parts += [*y_opposite, *y_opposite_across]
    col_shards = [
        (genotypes, beside, own_twin, twin(beside)),
        (z_up, z_up_side, z_up_twin, twin(z_up_side)),
        (z_down, z_down_side, z_down_twin, twin(z_down_side)),
        (z_opposite, z_opposite_side, twin(z_opposite), twin(z_opposite_side)),
    ]

    away = (0 - z) & 3
    slot0 = jnp.where(away == 0, 0, jnp.where(away == 1, 2, jnp.where(away == 2, 3, 1)))
    pick = ((slot0.astype(jnp.uint32) * 2 + core) * 2 + x_lo).astype(jnp.int32)
    pick = jnp.stack([pick, *[jnp.int32(step) for step in STEP_OF_SLOT]])
    factor = panel(
        pick, running[:, 0, 0, :], inverse, row_parts, [s for group in col_shards for s in group]
    )
    pieces = factor.reshape(NY, NH, 128, NB)
    heard = lax.ppermute(pieces[:, 1], "col", [(0, 1)])
    pieces = jnp.where(x_hi == 0, pieces[:, 0], heard)
    heard = sum(
        lax.ppermute(pieces[d], "col", [(h, d * NH + h) for h in range(NH)]) for d in range(1, NY)
    )
    own_factor = jnp.where(y == 0, pieces[0], heard)
    pair = jnp.stack([own_factor, lax.ppermute(own_factor, "col", col_perm(0, 1))])
    row_factor = jnp.concatenate(ring_direct(pair, "col", col_perm), axis=0).reshape(1024, NB)
    pair = jnp.stack([own_factor, lax.ppermute(own_factor, "row", row_perm(0, 1, 0))])
    half = jnp.stack(ring_direct(pair, "row", row_perm))
    half_twin = lax.ppermute(half, "row", row_perm(0, 0, 1))
    high, low = split_bf16(jnp.stack([half, half_twin], axis=1).reshape(2048, NB).T)
    col_factor = jnp.concatenate([high, low, high], axis=0)

    late_rows, _ = lax.optimization_barrier((row_parts, factor))
    prods = []
    for g in range(4):
        prods.append(product(late_rows, col_shards[g]))

    tiles = jnp.arange(16, dtype=jnp.uint32)
    hit = grid_map[None, :] == jnp.arange(16, dtype=jnp.int32)[:, None]
    inverse_map = jnp.sum(jnp.where(hit, tiles[None, :], 0), axis=1).astype(jnp.uint32)
    step_y = ((inverse_map >> 2) - y) & 3
    slot = jnp.where(step_y == 0, 0, jnp.where(step_y == 1, 2, jnp.where(step_y == 2, 3, 1)))
    tile = ((slot.astype(jnp.uint32) * 2) + (((inverse_map >> 1) & 1) ^ x_hi)) * 2 + (inverse_map & 1)
    row_start = row_index * 1024 + inverse_map * 64
    slot_z = tiles >> 2
    step_z = jnp.where(slot_z == 0, 0, jnp.where(slot_z == 1, 3, slot_z - 1)).astype(jnp.uint32)
    place = (((step_z + z) & 3) << 2) + (((tiles & 1) ^ x_lo) << 1) + (((tiles >> 1) & 1) ^ core)
    is_col0 = jnp.where(col_index == 0, 1, 0).astype(jnp.uint32)
    table = jnp.concatenate([inverse_map, tile, row_start, place, is_col0[None]]).astype(jnp.int32)

    result = None
    running = running.reshape(1024 * 16, 128)
    for part in range(HALVES):
        packed = epilogue(part, table, running, prods, row_factor, col_factor, snp_count)
        packed = packed.reshape(16, (TILE_ROWS + 1) * 16, 128)
        coded = lax.all_to_all(packed, "row", split_axis=0, concat_axis=0, tiled=True)
        result = unpack(part, coded, result)
    return result.reshape(16, 1, 64, 16, 1, 128)


def solution(mesh):
    in_specs = (P(None, ("row", "col")), P("row", None, "col", None), P())
    out_specs = P(None, "row", None, None, "col", None)
    return jax.shard_map(
        compute, mesh=mesh, in_specs=in_specs, out_specs=out_specs, check_vma=False
    )
```

profile of v0, /device:TPU:1, one launch (start us, length us, event | category | flops | bytes accessed | tf_op | source)
XLA Modules:
  0.0 338.2 jit_solution(15503565375243009293)
XLA Ops:
  0.0 1.6 copy.19
  1.6 3.6 %collective-permute-start = (bf16[128,5120]{1,0:T(8,128)(2,1)S(1)}, bf16[128,5120]{1,0:T(8,128)(2,1)}, u32[]{:S(2)}, u32[]{:S(2)}) collective-permute-start(bf16[128,5120]{1,0:T(8,128)(2,1)S(1)} %bitcast.69), channel_id=1, source_target_pairs={{0,1},{1,0},{2,3},{3,2},{4,5},{5,4},{6,7},{7,6},{8,9},{9,8},{10,11... | collective-permute-start | bytes 3932168 | tf_op jit(solution)/shard_map/ppermute | solution.py:275
  5.3 2.7 collective-permute-start.3
  8.9 2.3 fusion
  11.4 11.7 %cholesky.20 = f32[128,128]{1,0:T(8,128)S(1)} custom-call(f32[128,128]{1,0:T(8,128)S(1)} %fusion.5), custom_call_target="Cholesky" | custom-call | tf_op jit(solution)/shard_map/jit(cholesky)/cholesky | solution.py:280
  24.5 9.0 %collective-permute-done.refs_4_.refs_1_ = bf16[128,5120]{1,0:T(8,128)(2,1)} collective-permute-done((bf16[128,5120]{1,0:T(8,128)(2,1)S(1)}, bf16[128,5120]{1,0:T(8,128)(2,1)}, u32[]{:S(2)}, u32[]{:S(2)}) %collective-permute-start) | collective-permute-done | bytes 1310752 | tf_op jit(solution)/shard_map/ppermute | solution.py:275
  33.5 9.8 %custom-call.6 = f32[1,128,128]{1,2,0:T(8,128)S(1)} custom-call(f32[1,128,128]{2,1,0:T(8,128)S(1)} %select_bitcast_fusion), custom_call_target="InvertDiagBlocksLowerTriangular" | custom-call | tf_op jit(solution)/shard_map/triangular_solve | solution.py:288
  45.6 4.2 %collective-permute-start.21 = (bf16[5120,128]{1,0:T(8,128)(2,1)}, bf16[5120,128]{1,0:T(8,128)(2,1)}, u32[]{:S(2)}, u32[]{:S(2)}) collective-permute-start(bf16[5120,128]{1,0:T(8,128)(2,1)} %refs_10_.1), channel_id=1, source_target_pairs={{0,96},{8,104},{16,112},{24,120},{32,0},{40,8},{48,16},{56,24},{64... | collective-permute-start | bytes 3932168 | tf_op jit(solution)/shard_map/ppermute | solution.py:33
  49.7 7.9 %collective-permute-start.15 = (bf16[5120,128]{1,0:T(8,128)(2,1)}, bf16[5120,128]{1,0:T(8,128)(2,1)}, u32[]{:S(2)}, u32[]{:S(2)}) collective-permute-start(bf16[5120,128]{1,0:T(8,128)(2,1)} %refs_10_.1), channel_id=1, source_target_pairs={{0,8},{8,0},{16,24},{24,16},{32,40},{40,32},{48,56},{56,48},{64,72... | collective-permute-start | bytes 3932168 | tf_op jit(solution)/shard_map/ppermute | solution.py:271
  58.4 2.8 collective-permute-start.6
  61.2 2.0 slice.66
  63.2 8.8 %collective-permute-done.21.refs_21_.refs_10_ = bf16[5120,128]{1,0:T(8,128)(2,1)} collective-permute-done((bf16[5120,128]{1,0:T(8,128)(2,1)}, bf16[5120,128]{1,0:T(8,128)(2,1)}, u32[]{:S(2)}, u32[]{:S(2)}) %collective-permute-start.21) | collective-permute-done | bytes 1310752 | tf_op jit(solution)/shard_map/ppermute | solution.py:33
  72.1 1.3 collective-permute-start.13
  73.4 1.1 slice.71
  74.5 3.5 %collective-permute-start.26 = (bf16[2560,128]{1,0:T(8,128)(2,1)S(1)}, bf16[2560,128]{1,0:T(8,128)(2,1)S(1)}, u32[]{:S(2)}, u32[]{:S(2)}) collective-permute-start(bf16[2560,128]{1,0:T(8,128)(2,1)S(1)} %slice.71), channel_id=1, source_target_pairs={{0,96},{8,104},{16,112},{24,120},{32,0},{40,8},{48,16},{56,24},{64... | collective-permute-start | bytes 1966088 | tf_op jit(solution)/shard_map/ppermute | solution.py:39
  78.0 1.1 slice.70
  79.1 1.1 collective-permute-start.25
  80.2 2.3 collective-permute-done.13
  82.5 2.6 collective-permute-start.14
  85.1 2.7 collective-permute-start.4
  88.3 6.4 %collective-permute-start.23 = (bf16[5120,128]{1,0:T(8,128)(2,1)}, bf16[5120,128]{1,0:T(8,128)(2,1)S(1)}, u32[]{:S(2)}, u32[]{:S(2)}) collective-permute-start(bf16[5120,128]{1,0:T(8,128)(2,1)} %collective-permute-done.21.refs_21_.refs_10_), channel_id=1, source_target_pairs={{0,8},{8,0},{16,24},{24,16},{32,40},{40,32},{48,56},{56,48},{64,72... | collective-permute-start | bytes 3932168 | tf_op jit(solution)/shard_map/ppermute | solution.py:271
  94.8 4.9 %collective-permute-start.19 = (bf16[5120,128]{1,0:T(8,128)(2,1)}, bf16[5120,128]{1,0:T(8,128)(2,1)S(1)}, u32[]{:S(2)}, u32[]{:S(2)}) collective-permute-start(bf16[5120,128]{1,0:T(8,128)(2,1)} %collective-permute-done.17.refs_17_.refs_10_), channel_id=1, source_target_pairs={{0,8},{8,0},{16,24},{24,16},{32,40},{40,32},{48,56},{56,48},{64,72... | collective-permute-start | bytes 3932168 | tf_op jit(solution)/shard_map/ppermute | solution.py:271
  99.8 10.7 %collective-permute-done.14.refs_14_.refs_11_ = bf16[5120,128]{1,0:T(8,128)(2,1)} collective-permute-done((bf16[5120,128]{1,0:T(8,128)(2,1)S(1)}, bf16[5120,128]{1,0:T(8,128)(2,1)}, u32[]{:S(2)}, u32[]{:S(2)}) %collective-permute-start.14) | collective-permute-done | bytes 1310752 | tf_op jit(solution)/shard_map/ppermute | solution.py:283
  110.6 2.3 collective-permute-start.27
  113.1 2.3 collective-permute-start.22
  116.3 0.9 copy-done.3
  117.2 2.6 collective-permute-start.8
  119.8 9.5 %collective-permute-done.8.refs_12_.refs_9_ = bf16[64,5120]{1,0:T(8,128)(2,1)S(1)} collective-permute-done((bf16[64,5120]{1,0:T(8,128)(2,1)S(1)}, bf16[64,5120]{1,0:T(8,128)(2,1)S(1)}, u32[]{:S(2)}, u32[]{:S(2)}) %collective-permute-start.8) | collective-permute-done | bytes 655392 | tf_op jit(solution)/shard_map/ppermute | solution.py:39
  129.3 5.4 %collective-permute-start.28 = (bf16[5120,128]{1,0:T(8,128)(2,1)S(1)}, bf16[5120,128]{1,0:T(8,128)(2,1)}, u32[]{:S(2)}, u32[]{:S(2)}) collective-permute-start(bf16[5120,128]{1,0:T(8,128)(2,1)S(1)} %constant_dynamic-update-slice_fusion.refs_25_.refs_10_), channel_id=1, source_target_pairs={{0,8},{8,0},{16,24},{24,16},{32,40},{40,32},{48,56},{56,48},{64,72... | collective-permute-start | bytes 3932168 | tf_op jit(solution)/shard_map/ppermute | solution.py:271
  134.8 3.4 %collective-permute-start.16 = (bf16[5120,128]{1,0:T(8,128)(2,1)}, bf16[5120,128]{1,0:T(8,128)(2,1)}, u32[]{:S(2)}, u32[]{:S(2)}) collective-permute-start(bf16[5120,128]{1,0:T(8,128)(2,1)} %collective-permute-done.14.refs_14_.refs_11_), channel_id=1, source_target_pairs={{0,8},{8,0},{16,24},{24,16},{32,40},{40,32},{48,56},{56,48},{64,72... | collective-permute-start | bytes 3932168 | tf_op jit(solution)/shard_map/ppermute | solution.py:271
  138.6 4.4 %collective-permute-start.29 = (bf16[5120,128]{1,0:T(8,128)(2,1)}, bf16[5120,128]{1,0:T(8,128)(2,1)}, u32[]{:S(2)}, u32[]{:S(2)}) collective-permute-start(bf16[5120,128]{1,0:T(8,128)(2,1)} %collective-permute-done.27.refs_26_.refs_11_), channel_id=1, source_target_pairs={{0,8},{8,0},{16,24},{24,16},{32,40},{40,32},{48,56},{56,48},{64,72... | collective-permute-start | bytes 3932168 | tf_op jit(solution)/shard_map/ppermute | solution.py:271
  143.0 1.7 collective-permute-start.24
  144.7 4.1 %collective-permute-start.20 = (bf16[5120,128]{1,0:T(8,128)(2,1)}, bf16[5120,128]{1,0:T(8,128)(2,1)}, u32[]{:S(2)}, u32[]{:S(2)}) collective-permute-start(bf16[5120,128]{1,0:T(8,128)(2,1)} %collective-permute-done.18.refs_18_.refs_11_), channel_id=1, source_target_pairs={{0,8},{8,0},{16,24},{24,16},{32,40},{40,32},{48,56},{56,48},{64,72... | collective-permute-start | bytes 3932168 | tf_op jit(solution)/shard_map/ppermute | solution.py:271
  148.9 1.9 slice.57
  152.0 11.1 %panel.1 = f32[1024,128]{1,0:T(8,128)} custom-call(s32[5]{0:T(128)} %stack.47.refs_0_, f32[1024,128]{1,0:T(8,128)} %bitcast.83, f32[128,128]{1,0:T(8,128)} %broadcast_select_fusion.1.refs_2_, bf16[128,5120]{1,0:T(8,128)(2,1)} %bitcast.72, bf16[128,5120]{1,0:T(8,128)(2,1)} %collective-permute-done.refs_4_.refs_1_, ...), custom_call_target="tpu_custom_call" | custom-call | tf_op jit(solution)/shard_map/panel/pallas_call | solution.py:210
  163.2 1.1 fusion.12
  164.4 4.1 %collective-permute-start.30 = (f32[4,128,128]{1,2,0:T(8,128)S(1)}, f32[4,128,128]{1,2,0:T(8,128)S(1)}, u32[]{:S(2)}, u32[]{:S(2)}) collective-permute-start(f32[4,128,128]{1,2,0:T(8,128)S(1)} %bitcast.94), channel_id=1, source_target_pairs={{0,1},{8,9},{16,17},{24,25},{32,33},{40,41},{48,49},{56,57},{64,65... | collective-permute-start | bytes 786440 | tf_op jit(solution)/shard_map/ppermute | solution.py:319
  168.6 5.3 %collective-permute-done.30 = f32[4,128,128]{1,2,0:T(8,128)S(1)} collective-permute-done((f32[4,128,128]{1,2,0:T(8,128)S(1)}, f32[4,128,128]{1,2,0:T(8,128)S(1)}, u32[]{:S(2)}, u32[]{:S(2)}) %collective-permute-start.30) | collective-permute-done | bytes 262176 | tf_op jit(solution)/shard_map/ppermute | solution.py:319
  173.9 1.3 collective-permute-start.32
  175.2 1.3 collective-permute-start.33
  176.5 1.3 collective-permute-start.31
  177.9 1.3 collective-permute-done.31
  179.4 3.8 %collective-permute-start.34 = (f32[128,128]{0,1:T(8,128)S(1)}, f32[128,128]{0,1:T(8,128)S(1)}, u32[]{:S(2)}, u32[]{:S(2)}) collective-permute-start(f32[128,128]{0,1:T(8,128)S(1)} %get-tuple-element.32), channel_id=1, source_target_pairs={{0,1},{1,0},{2,3},{3,2},{4,5},{5,4},{6,7},{7,6},{8,9},{9,8},{10,11... | collective-permute-start | bytes 196616 | tf_op jit(solution)/shard_map/ppermute | solution.py:325
  183.3 1.9 collective-permute-start.40
  185.2 1.3 collective-permute-start.41
  187.1 11.1 %product.7.refs_5_ = f32[1024,512]{1,0:T(8,128)} custom-call(bf16[128,5120]{1,0:T(8,128)(2,1)} %bitcast.73, bf16[128,5120]{1,0:T(8,128)(2,1)} %collective-permute-done.refs_4_.refs_1_, bf16[128,5120]{1,0:T(8,128)(2,1)} %collective-permute-done.1.refs_5_.refs_2_, bf16[128,5120]{1,0:T(8,128)(2,1)} %copy-done.3, bf16[128,5120]{1,0:T(8,128)(2,1)} %copy-done.1, ...), custom_call_target="tpu_custom_call" | custom-call | tf_op jit(solution)/shard_map/product/pallas_call | solution.py:165
  198.2 11.2 %product.6.refs_4_ = f32[1024,512]{1,0:T(8,128)} custom-call(bf16[128,5120]{1,0:T(8,128)(2,1)} %bitcast.74, bf16[128,5120]{1,0:T(8,128)(2,1)} %collective-permute-done.refs_4_.refs_1_, bf16[128,5120]{1,0:T(8,128)(2,1)} %collective-permute-done.1.refs_5_.refs_2_, bf16[128,5120]{1,0:T(8,128)(2,1)} %copy-done.3, bf16[128,5120]{1,0:T(8,128)(2,1)} %copy-done.1, ...), custom_call_target="tpu_custom_call" | custom-call | tf_op jit(solution)/shard_map/product/pallas_call | solution.py:165
  209.3 11.1 %product.5.refs_3_ = f32[1024,512]{1,0:T(8,128)} custom-call(bf16[128,5120]{1,0:T(8,128)(2,1)} %bitcast.75, bf16[128,5120]{1,0:T(8,128)(2,1)} %collective-permute-done.refs_4_.refs_1_, bf16[128,5120]{1,0:T(8,128)(2,1)} %collective-permute-done.1.refs_5_.refs_2_, bf16[128,5120]{1,0:T(8,128)(2,1)} %copy-done.3, bf16[128,5120]{1,0:T(8,128)(2,1)} %copy-done.1, ...), custom_call_target="tpu_custom_call" | custom-call | tf_op jit(solution)/shard_map/product/pallas_call | solution.py:165
  220.5 11.1 %product.4.refs_2_ = f32[1024,512]{1,0:T(8,128)} custom-call(bf16[128,5120]{1,0:T(8,128)(2,1)} %bitcast.76, bf16[128,5120]{1,0:T(8,128)(2,1)} %collective-permute-done.refs_4_.refs_1_, bf16[128,5120]{1,0:T(8,128)(2,1)} %collective-permute-done.1.refs_5_.refs_2_, bf16[128,5120]{1,0:T(8,128)(2,1)} %copy-done.3, bf16[128,5120]{1,0:T(8,128)(2,1)} %copy-done.1, ...), custom_call_target="tpu_custom_call" | custom-call | tf_op jit(solution)/shard_map/product/pallas_call | solution.py:165
  231.6 1.0 collective-permute-start.37
  232.6 3.5 %collective-permute-start.36 = (f32[2,128,128]{1,2,0:T(8,128)S(1)}, f32[2,128,128]{1,2,0:T(8,128)S(1)}, u32[]{:S(2)}, u32[]{:S(2)}) collective-permute-start(f32[2,128,128]{1,2,0:T(8,128)S(1)} %pad_maximum_fusion.3), channel_id=1, source_target_pairs={{0,6},{1,7},{2,0},{3,1},{4,2},{5,3},{6,4},{7,5},{8,14},{9,15},{10,... | collective-permute-start | bytes 393224 | tf_op jit(solution)/shard_map/ppermute | solution.py:44
  236.4 3.9 %collective-permute-start.42 = (f32[4,2,128,128]{2,1,0,3:T(2,128)S(1)}, f32[4,2,128,128]{2,1,0,3:T(2,128)S(1)}, u32[]{:S(2)}, u32[]{:S(2)}) collective-permute-start(f32[4,2,128,128]{2,1,0,3:T(2,128)S(1)} %pad_maximum_fusion.2), channel_id=1, source_target_pairs={{0,8},{8,0},{16,24},{24,16},{32,40},{40,32},{48,56},{56,48},{64,72... | collective-permute-start | bytes 1572872 | tf_op jit(solution)/shard_map/ppermute | solution.py:329
  240.3 2.0 collective-permute-done.35
  242.4 1.0 copy.26
  245.1 1.4 pad_maximum_fusion.refs_7_
  246.5 16.0 %epilogue.3 = s16[8448,128]{1,0:T(8,128)(2,1)} custom-call(s32[65]{0:T(128)} %convert_element_type.37.refs_0_, f32[16384,128]{1,0:T(8,128)} %bitcast.77, f32[1024,512]{1,0:T(8,128)} %product.4.refs_2_, f32[1024,512]{1,0:T(8,128)} %product.5.refs_3_, f32[1024,512]{1,0:T(8,128)} %product.6.refs_4_, f32[1024,512]{1,0:T(8,128)} %product.7.refs_5_, ...), custom_call_target="tpu_custom_call" | custom-call | tf_op jit(solution)/shard_map/epilogue/pallas_call | solution.py:97
  262.5 7.6 %all-to-all-start.1 = ((s16[16,528,128]{2,1,0:T(8,128)(2,1)}), s16[16,528,128]{2,1,0:T(8,128)(2,1)S(1)}, u32[]{:S(2)}, u32[]{:S(2)}) async-start(s16[16,528,128]{2,1,0:T(8,128)(2,1)} %bitcast.80), calls=%async_computation.1 | async-start | bytes 4325376 | tf_op jit(solution)/shard_map/all_to_all | solution.py:356
  270.1 16.0 %epilogue.2 = s16[8448,128]{1,0:T(8,128)(2,1)} custom-call(s32[65]{0:T(128)} %convert_element_type.37.refs_0_, f32[16384,128]{1,0:T(8,128)} %bitcast.78, f32[1024,512]{1,0:T(8,128)} %product.4.refs_2_, f32[1024,512]{1,0:T(8,128)} %product.5.refs_3_, f32[1024,512]{1,0:T(8,128)} %product.6.refs_4_, f32[1024,512]{1,0:T(8,128)} %product.7.refs_5_, ...), custom_call_target="tpu_custom_call" | custom-call | tf_op jit(solution)/shard_map/epilogue/pallas_call | solution.py:97
  286.1 11.6 %all-to-all-done.1.coded = s16[16,528,128]{2,1,0:T(8,128)(2,1)S(1)} async-done(((s16[16,528,128]{2,1,0:T(8,128)(2,1)}), s16[16,528,128]{2,1,0:T(8,128)(2,1)S(1)}, u32[]{:S(2)}, u32[]{:S(2)}) %all-to-all-start.1) | async-done | bytes 2162720 | tf_op jit(solution)/shard_map/all_to_all | solution.py:356
  297.7 1.4 copy-done.9
  299.1 5.1 %all-to-all-start = ((s16[16,528,128]{2,1,0:T(8,128)(2,1)}), s16[16,528,128]{2,1,0:T(8,128)(2,1)}, u32[]{:S(2)}, u32[]{:S(2)}) async-start(s16[16,528,128]{2,1,0:T(8,128)(2,1)} %bitcast.79), calls=%async_computation | async-start | bytes 4325376 | tf_op jit(solution)/shard_map/all_to_all | solution.py:356
  304.3 6.1 %unpack.2.refs_0_ = f32[16,2,512,128]{3,2,1,0:T(8,128)} custom-call(s16[16,528,128]{2,1,0:T(8,128)(2,1)} %copy-done.9), custom_call_target="tpu_custom_call" | custom-call | tf_op jit(solution)/shard_map/unpack/pallas_call | solution.py:245
  310.3 21.8 %all-to-all-done.coded = s16[16,528,128]{2,1,0:T(8,128)(2,1)} async-done(((s16[16,528,128]{2,1,0:T(8,128)(2,1)}), s16[16,528,128]{2,1,0:T(8,128)(2,1)}, u32[]{:S(2)}, u32[]{:S(2)}) %all-to-all-start) | async-done | bytes 2162720 | tf_op jit(solution)/shard_map/all_to_all | solution.py:356
  332.1 6.1 %unpack.3 = f32[16,2,512,128]{3,2,1,0:T(8,128)} custom-call(s16[16,528,128]{2,1,0:T(8,128)(2,1)} %all-to-all-done.coded, f32[16,2,512,128]{3,2,1,0:T(8,128)} %unpack.2.refs_0_), custom_call_target="tpu_custom_call", output_to_operand_aliasing={{}: (1, {})} | custom-call | tf_op jit(solution)/shard_map/unpack/pallas_call | solution.py:245
  (112 shorter events, 12.1 us)
Async XLA Ops:
  1.6 9.7 %copy-start = (bf16[5120,128]{0,1:T(8,128)(2,1)}, bf16[5120,128]{0,1:T(8,128)(2,1)S(1)}, u32[]{:S(2)}) copy-start(bf16[5120,128]{0,1:T(8,128)(2,1)S(1)} %copy.19) | copy-start | bytes 3932164
  1.6 31.8 %collective-permute-start = (bf16[128,5120]{1,0:T(8,128)(2,1)S(1)}, bf16[128,5120]{1,0:T(8,128)(2,1)}, u32[]{:S(2)}, u32[]{:S(2)}) collective-permute-start(bf16[128,5120]{1,0:T(8,128)(2,1)S(1)} %bitcast.69), channel_id=1, source_target_pairs={{0,1},{1,0},{2,3},{3,2},{4,5},{5,4},{6,7},{7,6},{8,9},{9,8},{10,11... | collective-permute-start | bytes 3932168 | tf_op jit(solution)/shard_map/ppermute | solution.py:275
  5.3 52.4 %collective-permute-start.3 = (bf16[128,5120]{1,0:T(8,128)(2,1)S(1)}, bf16[128,5120]{1,0:T(8,128)(2,1)S(1)}, u32[]{:S(2)}, u32[]{:S(2)}) collective-permute-start(bf16[128,5120]{1,0:T(8,128)(2,1)S(1)} %bitcast.70), channel_id=1, source_target_pairs={{0,6},{1,7},{2,0},{3,1},{4,2},{5,3},{6,4},{7,5},{8,14},{9,15},{10,... | collective-permute-start | bytes 3932168 | tf_op jit(solution)/shard_map/ppermute | solution.py:33
  8.0 50.4 %collective-permute-start.1 = (bf16[128,5120]{1,0:T(8,128)(2,1)S(1)}, bf16[128,5120]{1,0:T(8,128)(2,1)}, u32[]{:S(2)}, u32[]{:S(2)}) collective-permute-start(bf16[128,5120]{1,0:T(8,128)(2,1)S(1)} %bitcast.71), channel_id=1, source_target_pairs={{0,2},{1,3},{2,4},{3,5},{4,6},{5,7},{6,0},{7,1},{8,10},{9,11},{10,... | collective-permute-start | bytes 3932168 | tf_op jit(solution)/shard_map/ppermute | solution.py:33
  43.5 2.0 collective-permute-start.11
  44.2 5.5 %collective-permute-start.10 = (f32[128,128]{1,0:T(8,128)S(1)}, f32[128,128]{1,0:T(8,128)S(1)}, u32[]{:S(2)}, u32[]{:S(2)}) collective-permute-start(f32[128,128]{1,0:T(8,128)S(1)} %fusion.3), channel_id=1, source_target_pairs={{0,64},{1,65},{2,66},{3,67},{4,68},{5,69},{6,70},{7,71}} | collective-permute-start | bytes 196616 | tf_op jit(solution)/shard_map/ppermute | solution.py:292
  44.9 4.8 %collective-permute-start.9 = (f32[128,128]{1,0:T(8,128)S(1)}, f32[128,128]{1,0:T(8,128)S(1)}, u32[]{:S(2)}, u32[]{:S(2)}) collective-permute-start(f32[128,128]{1,0:T(8,128)S(1)} %fusion.3), channel_id=1, source_target_pairs={{0,32},{1,33},{2,34},{3,35},{4,36},{5,37},{6,38},{7,39}} | collective-permute-start | bytes 196616 | tf_op jit(solution)/shard_map/ppermute | solution.py:292
  45.6 26.5 %collective-permute-start.21 = (bf16[5120,128]{1,0:T(8,128)(2,1)}, bf16[5120,128]{1,0:T(8,128)(2,1)}, u32[]{:S(2)}, u32[]{:S(2)}) collective-permute-start(bf16[5120,128]{1,0:T(8,128)(2,1)} %refs_10_.1), channel_id=1, source_target_pairs={{0,96},{8,104},{16,112},{24,120},{32,0},{40,8},{48,16},{56,24},{64... | collective-permute-start | bytes 3932168 | tf_op jit(solution)/shard_map/ppermute | solution.py:33
  49.7 24.8 %collective-permute-start.17 = (bf16[5120,128]{1,0:T(8,128)(2,1)}, bf16[5120,128]{1,0:T(8,128)(2,1)}, u32[]{:S(2)}, u32[]{:S(2)}) collective-permute-start(bf16[5120,128]{1,0:T(8,128)(2,1)} %refs_10_.1), channel_id=1, source_target_pairs={{0,32},{8,40},{16,48},{24,56},{32,64},{40,72},{48,80},{56,88},{64,... | collective-permute-start | bytes 3932168 | tf_op jit(solution)/shard_map/ppermute | solution.py:33
  49.7 29.4 %collective-permute-start.15 = (bf16[5120,128]{1,0:T(8,128)(2,1)}, bf16[5120,128]{1,0:T(8,128)(2,1)}, u32[]{:S(2)}, u32[]{:S(2)}) collective-permute-start(bf16[5120,128]{1,0:T(8,128)(2,1)} %refs_10_.1), channel_id=1, source_target_pairs={{0,8},{8,0},{16,24},{24,16},{32,40},{40,32},{48,56},{56,48},{64,72... | collective-permute-start | bytes 3932168 | tf_op jit(solution)/shard_map/ppermute | solution.py:271
  57.6 5.6 %copy-start.1 = (bf16[128,5120]{1,0:T(8,128)(2,1)}, bf16[128,5120]{1,0:T(8,128)(2,1)S(1)}, u32[]{:S(2)}) copy-start(bf16[128,5120]{1,0:T(8,128)(2,1)S(1)} %collective-permute-done.3.refs_7_.refs_4_) | copy-start | bytes 3932164
  57.6 5.5 %collective-permute-start.12 = (f32[128,128]{1,0:T(8,128)S(1)}, f32[128,128]{1,0:T(8,128)S(1)}, u32[]{:S(2)}, u32[]{:S(2)}) collective-permute-start(f32[128,128]{1,0:T(8,128)S(1)} %add_select_fusion), channel_id=1, source_target_pairs={{0,16},{32,48},{64,80},{96,112},{1,17},{33,49},{65,81},{97,113},{2... | collective-permute-start | bytes 196616 | tf_op jit(solution)/shard_map/ppermute | solution.py:295
  58.4 26.7 %collective-permute-start.6 = (bf16[64,5120]{1,0:T(8,128)(2,1)S(1)}, bf16[64,5120]{1,0:T(8,128)(2,1)S(1)}, u32[]{:S(2)}, u32[]{:S(2)}) collective-permute-start(bf16[64,5120]{1,0:T(8,128)(2,1)S(1)} %slice.67), channel_id=1, source_target_pairs={{0,6},{1,7},{2,0},{3,1},{4,2},{5,3},{6,4},{7,5},{8,14},{9,15},{10,... | collective-permute-start | bytes 1966088 | tf_op jit(solution)/shard_map/ppermute | solution.py:39
  63.2 24.7 %collective-permute-start.5 = (bf16[64,5120]{1,0:T(8,128)(2,1)}, bf16[64,5120]{1,0:T(8,128)(2,1)S(1)}, u32[]{:S(2)}, u32[]{:S(2)}) collective-permute-start(bf16[64,5120]{1,0:T(8,128)(2,1)} %slice.66), channel_id=1, source_target_pairs={{0,2},{1,3},{2,4},{3,5},{4,6},{5,7},{6,0},{7,1},{8,10},{9,11},{10,... | collective-permute-start | bytes 1966088 | tf_op jit(solution)/shard_map/ppermute | solution.py:38
  63.2 19.3 %copy-start.4 = (bf16[5120,128]{1,0:T(8,128)(2,1)S(1)}, bf16[5120,128]{1,0:T(8,128)(2,1)}, u32[]{:S(2)}) copy-start(bf16[5120,128]{1,0:T(8,128)(2,1)} %refs_10_.1) | copy-start | bytes 3932164
  72.1 10.4 %collective-permute-start.13 = (f32[128,128]{1,0:T(8,128)S(1)}, f32[128,128]{1,0:T(8,128)S(1)}, u32[]{:S(2)}, u32[]{:S(2)}) collective-permute-start(f32[128,128]{1,0:T(8,128)S(1)} %broadcast_select_fusion), channel_id=1, source_target_pairs={{0,8},{16,24},{32,40},{48,56},{64,72},{80,88},{96,104},{112,120},{... | collective-permute-start | bytes 196616 | tf_op jit(solution)/shard_map/ppermute | solution.py:299
  74.5 13.8 %collective-permute-start.26 = (bf16[2560,128]{1,0:T(8,128)(2,1)S(1)}, bf16[2560,128]{1,0:T(8,128)(2,1)S(1)}, u32[]{:S(2)}, u32[]{:S(2)}) collective-permute-start(bf16[2560,128]{1,0:T(8,128)(2,1)S(1)} %slice.71), channel_id=1, source_target_pairs={{0,96},{8,104},{16,112},{24,120},{32,0},{40,8},{48,16},{56,24},{64... | collective-permute-start | bytes 1966088 | tf_op jit(solution)/shard_map/ppermute | solution.py:39
  79.1 15.6 %collective-permute-start.25 = (bf16[2560,128]{1,0:T(8,128)(2,1)S(1)}, bf16[2560,128]{1,0:T(8,128)(2,1)S(1)}, u32[]{:S(2)}, u32[]{:S(2)}) collective-permute-start(bf16[2560,128]{1,0:T(8,128)(2,1)S(1)} %slice.70), channel_id=1, source_target_pairs={{0,32},{8,40},{16,48},{24,56},{32,64},{40,72},{48,80},{56,88},{64,... | collective-permute-start | bytes 1966088 | tf_op jit(solution)/shard_map/ppermute | solution.py:38
  82.5 28.1 %collective-permute-start.14 = (bf16[5120,128]{1,0:T(8,128)(2,1)S(1)}, bf16[5120,128]{1,0:T(8,128)(2,1)}, u32[]{:S(2)}, u32[]{:S(2)}) collective-permute-start(bf16[5120,128]{1,0:T(8,128)(2,1)S(1)} %copy-done.4), channel_id=1, source_target_pairs={{0,16},{8,24},{16,0},{24,8},{32,48},{40,56},{48,32},{56,40},{64,80... | collective-permute-start | bytes 3932168 | tf_op jit(solution)/shard_map/ppermute | solution.py:283
  85.1 31.1 %copy-start.5 = (bf16[64,5120]{1,0:T(8,128)(2,1)}, bf16[64,5120]{1,0:T(8,128)(2,1)S(1)}, u32[]{:S(2)}) copy-start(bf16[64,5120]{1,0:T(8,128)(2,1)S(1)} %collective-permute-done.6.refs_10_.refs_7_) | copy-start | bytes 1966084
  85.1 28.0 %collective-permute-start.4 = (bf16[128,5120]{1,0:T(8,128)(2,1)}, bf16[128,5120]{1,0:T(8,128)(2,1)S(1)}, u32[]{:S(2)}, u32[]{:S(2)}) collective-permute-start(bf16[128,5120]{1,0:T(8,128)(2,1)} %collective-permute-done.refs_4_.refs_1_), channel_id=1, source_target_pairs={{0,6},{1,7},{2,0},{3,1},{4,2},{5,3},{6,4},{7,5},{8,14},{9,15},{10,... | collective-permute-start | bytes 3932168 | tf_op jit(solution)/shard_map/ppermute | solution.py:33
  87.8 28.4 %copy-start.6 = (bf16[64,5120]{1,0:T(8,128)(2,1)}, bf16[64,5120]{1,0:T(8,128)(2,1)S(1)}, u32[]{:S(2)}) copy-start(bf16[64,5120]{1,0:T(8,128)(2,1)S(1)} %collective-permute-done.5.refs_9_.refs_6_) | copy-start | bytes 1966084
  87.8 28.3 %collective-permute-start.2 = (bf16[128,5120]{1,0:T(8,128)(2,1)}, bf16[128,5120]{1,0:T(8,128)(2,1)S(1)}, u32[]{:S(2)}, u32[]{:S(2)}) collective-permute-start(bf16[128,5120]{1,0:T(8,128)(2,1)} %collective-permute-done.refs_4_.refs_1_), channel_id=1, source_target_pairs={{0,2},{1,3},{2,4},{3,5},{4,6},{5,7},{6,0},{7,1},{8,10},{9,11},{10,... | collective-permute-start | bytes 3932168 | tf_op jit(solution)/shard_map/ppermute | solution.py:33
  88.3 28.9 %collective-permute-start.23 = (bf16[5120,128]{1,0:T(8,128)(2,1)}, bf16[5120,128]{1,0:T(8,128)(2,1)S(1)}, u32[]{:S(2)}, u32[]{:S(2)}) collective-permute-start(bf16[5120,128]{1,0:T(8,128)(2,1)} %collective-permute-done.21.refs_21_.refs_10_), channel_id=1, source_target_pairs={{0,8},{8,0},{16,24},{24,16},{32,40},{40,32},{48,56},{56,48},{64,72... | collective-permute-start | bytes 3932168 | tf_op jit(solution)/shard_map/ppermute | solution.py:271
  94.8 25.0 %collective-permute-start.19 = (bf16[5120,128]{1,0:T(8,128)(2,1)}, bf16[5120,128]{1,0:T(8,128)(2,1)S(1)}, u32[]{:S(2)}, u32[]{:S(2)}) collective-permute-start(bf16[5120,128]{1,0:T(8,128)(2,1)} %collective-permute-done.17.refs_17_.refs_10_), channel_id=1, source_target_pairs={{0,8},{8,0},{16,24},{24,16},{32,40},{40,32},{48,56},{56,48},{64,72... | collective-permute-start | bytes 3932168 | tf_op jit(solution)/shard_map/ppermute | solution.py:271
  99.8 52.2 %copy-start.10 = (bf16[5120,128]{1,0:T(8,128)(2,1)}, bf16[5120,128]{1,0:T(8,128)(2,1)S(1)}, u32[]{:S(2)}) copy-start(bf16[5120,128]{1,0:T(8,128)(2,1)S(1)} %constant_dynamic-update-slice_fusion.refs_25_.refs_10_) | copy-start | bytes 3932164
  110.6 28.1 %collective-permute-start.27 = (bf16[5120,128]{1,0:T(8,128)(2,1)S(1)}, bf16[5120,128]{1,0:T(8,128)(2,1)}, u32[]{:S(2)}, u32[]{:S(2)}) collective-permute-start(bf16[5120,128]{1,0:T(8,128)(2,1)S(1)} %constant_dynamic-update-slice_fusion.refs_25_.refs_10_), channel_id=1, source_target_pairs={{0,16},{8,24},{16,0},{24,8},{32,48},{40,56},{48,32},{56,40},{64,80... | collective-permute-start | bytes 3932168 | tf_op jit(solution)/shard_map/ppermute | solution.py:297
  113.1 3.2 copy-start.2
  113.1 29.9 %collective-permute-start.22 = (bf16[5120,128]{1,0:T(8,128)(2,1)}, bf16[5120,128]{1,0:T(8,128)(2,1)}, u32[]{:S(2)}, u32[]{:S(2)}) collective-permute-start(bf16[5120,128]{1,0:T(8,128)(2,1)} %collective-permute-done.14.refs_14_.refs_11_), channel_id=1, source_target_pairs={{0,96},{8,104},{16,112},{24,120},{32,0},{40,8},{48,16},{56,24},{64... | collective-permute-start | bytes 3932168 | tf_op jit(solution)/shard_map/ppermute | solution.py:33
  116.1 1.1 copy-start.3
  116.1 28.6 %collective-permute-start.18 = (bf16[5120,128]{1,0:T(8,128)(2,1)}, bf16[5120,128]{1,0:T(8,128)(2,1)}, u32[]{:S(2)}, u32[]{:S(2)}) collective-permute-start(bf16[5120,128]{1,0:T(8,128)(2,1)} %collective-permute-done.14.refs_14_.refs_11_), channel_id=1, source_target_pairs={{0,32},{8,40},{16,48},{24,56},{32,64},{40,72},{48,80},{56,88},{64,... | collective-permute-start | bytes 3932168 | tf_op jit(solution)/shard_map/ppermute | solution.py:33
  117.2 21.4 %copy-start.11 = (bf16[5120,128]{1,0:T(8,128)(2,1)}, bf16[5120,128]{1,0:T(8,128)(2,1)S(1)}, u32[]{:S(2)}) copy-start(bf16[5120,128]{1,0:T(8,128)(2,1)S(1)} %collective-permute-done.23.refs_23_.refs_12_) | copy-start | bytes 3932164
  117.2 12.1 %collective-permute-start.8 = (bf16[64,5120]{1,0:T(8,128)(2,1)S(1)}, bf16[64,5120]{1,0:T(8,128)(2,1)S(1)}, u32[]{:S(2)}, u32[]{:S(2)}) collective-permute-start(bf16[64,5120]{1,0:T(8,128)(2,1)S(1)} %slice.69), channel_id=1, source_target_pairs={{0,6},{1,7},{2,0},{3,1},{4,2},{5,3},{6,4},{7,5},{8,14},{9,15},{10,... | collective-permute-start | bytes 1966088 | tf_op jit(solution)/shard_map/ppermute | solution.py:39
  119.8 23.2 %copy-start.12 = (bf16[5120,128]{1,0:T(8,128)(2,1)}, bf16[5120,128]{1,0:T(8,128)(2,1)S(1)}, u32[]{:S(2)}) copy-start(bf16[5120,128]{1,0:T(8,128)(2,1)S(1)} %collective-permute-done.19.refs_19_.refs_12_) | copy-start | bytes 3932164
  119.8 14.9 %collective-permute-start.7 = (bf16[64,5120]{1,0:T(8,128)(2,1)S(1)}, bf16[64,5120]{1,0:T(8,128)(2,1)S(1)}, u32[]{:S(2)}, u32[]{:S(2)}) collective-permute-start(bf16[64,5120]{1,0:T(8,128)(2,1)S(1)} %slice.68), channel_id=1, source_target_pairs={{0,2},{1,3},{2,4},{3,5},{4,6},{5,7},{6,0},{7,1},{8,10},{9,11},{10,... | collective-permute-start | bytes 1966088 | tf_op jit(solution)/shard_map/ppermute | solution.py:38
  129.3 22.7 %copy-start.7 = (bf16[64,5120]{1,0:T(8,128)(2,1)}, bf16[64,5120]{1,0:T(8,128)(2,1)S(1)}, u32[]{:S(2)}) copy-start(bf16[64,5120]{1,0:T(8,128)(2,1)S(1)} %collective-permute-done.8.refs_12_.refs_9_) | copy-start | bytes 1966084
  129.3 22.7 %collective-permute-start.28 = (bf16[5120,128]{1,0:T(8,128)(2,1)S(1)}, bf16[5120,128]{1,0:T(8,128)(2,1)}, u32[]{:S(2)}, u32[]{:S(2)}) collective-permute-start(bf16[5120,128]{1,0:T(8,128)(2,1)S(1)} %constant_dynamic-update-slice_fusion.refs_25_.refs_10_), channel_id=1, source_target_pairs={{0,8},{8,0},{16,24},{24,16},{32,40},{40,32},{48,56},{56,48},{64,72... | collective-permute-start | bytes 3932168 | tf_op jit(solution)/shard_map/ppermute | solution.py:271
  134.8 17.3 %copy-start.8 = (bf16[64,5120]{1,0:T(8,128)(2,1)}, bf16[64,5120]{1,0:T(8,128)(2,1)S(1)}, u32[]{:S(2)}) copy-start(bf16[64,5120]{1,0:T(8,128)(2,1)S(1)} %collective-permute-done.7.refs_11_.refs_8_) | copy-start | bytes 1966084
  134.8 17.2 %collective-permute-start.16 = (bf16[5120,128]{1,0:T(8,128)(2,1)}, bf16[5120,128]{1,0:T(8,128)(2,1)}, u32[]{:S(2)}, u32[]{:S(2)}) collective-permute-start(bf16[5120,128]{1,0:T(8,128)(2,1)} %collective-permute-done.14.refs_14_.refs_11_), channel_id=1, source_target_pairs={{0,8},{8,0},{16,24},{24,16},{32,40},{40,32},{48,56},{56,48},{64,72... | collective-permute-start | bytes 3932168 | tf_op jit(solution)/shard_map/ppermute | solution.py:271
  138.6 13.3 %collective-permute-start.29 = (bf16[5120,128]{1,0:T(8,128)(2,1)}, bf16[5120,128]{1,0:T(8,128)(2,1)}, u32[]{:S(2)}, u32[]{:S(2)}) collective-permute-start(bf16[5120,128]{1,0:T(8,128)(2,1)} %collective-permute-done.27.refs_26_.refs_11_), channel_id=1, source_target_pairs={{0,8},{8,0},{16,24},{24,16},{32,40},{40,32},{48,56},{56,48},{64,72... | collective-permute-start | bytes 3932168 | tf_op jit(solution)/shard_map/ppermute | solution.py:271
  143.0 9.0 %collective-permute-start.24 = (bf16[5120,128]{1,0:T(8,128)(2,1)}, bf16[5120,128]{1,0:T(8,128)(2,1)}, u32[]{:S(2)}, u32[]{:S(2)}) collective-permute-start(bf16[5120,128]{1,0:T(8,128)(2,1)} %collective-permute-done.22.refs_22_.refs_11_), channel_id=1, source_target_pairs={{0,8},{8,0},{16,24},{24,16},{32,40},{40,32},{48,56},{56,48},{64,72... | collective-permute-start | bytes 3932168 | tf_op jit(solution)/shard_map/ppermute | solution.py:271
  144.7 7.3 %collective-permute-start.20 = (bf16[5120,128]{1,0:T(8,128)(2,1)}, bf16[5120,128]{1,0:T(8,128)(2,1)}, u32[]{:S(2)}, u32[]{:S(2)}) collective-permute-start(bf16[5120,128]{1,0:T(8,128)(2,1)} %collective-permute-done.18.refs_18_.refs_11_), channel_id=1, source_target_pairs={{0,8},{8,0},{16,24},{24,16},{32,40},{40,32},{48,56},{56,48},{64,72... | collective-permute-start | bytes 3932168 | tf_op jit(solution)/shard_map/ppermute | solution.py:271
  164.2 15.0 %copy-start.13 = (s32[16]{0:T(128)S(1)}, s32[16]{0:T(128)}, u32[]{:S(2)}) copy-start(s32[16]{0:T(128)} %param.5) | copy-start | bytes 196
  164.4 9.5 %collective-permute-start.30 = (f32[4,128,128]{1,2,0:T(8,128)S(1)}, f32[4,128,128]{1,2,0:T(8,128)S(1)}, u32[]{:S(2)}, u32[]{:S(2)}) collective-permute-start(f32[4,128,128]{1,2,0:T(8,128)S(1)} %bitcast.94), channel_id=1, source_target_pairs={{0,1},{8,9},{16,17},{24,25},{32,33},{40,41},{48,49},{56,57},{64,65... | collective-permute-start | bytes 786440 | tf_op jit(solution)/shard_map/ppermute | solution.py:319
  173.9 3.9 %collective-permute-start.32 = (f32[128,128]{0,1:T(8,128)S(1)}, f32[128,128]{0,1:T(8,128)S(1)}, u32[]{:S(2)}, u32[]{:S(2)}) collective-permute-start(f32[128,128]{0,1:T(8,128)S(1)} %get-tuple-element.37), channel_id=1, source_target_pairs={{0,4},{1,5},{8,12},{9,13},{16,20},{17,21},{24,28},{25,29},{32,36},... | collective-permute-start | bytes 196616 | tf_op jit(solution)/shard_map/ppermute | solution.py:322
  175.2 2.6 collective-permute-start.33
  176.5 2.6 collective-permute-start.31
  179.2 4.0 %collective-permute-start.38 = (f32[128,128]{0,1:T(8,128)S(1)}, f32[128,128]{0,1:T(8,128)S(1)}, u32[]{:S(2)}, u32[]{:S(2)}) collective-permute-start(f32[128,128]{0,1:T(8,128)S(1)} %get-tuple-element.32), channel_id=1, source_target_pairs={{0,16},{8,24},{16,0},{24,8},{32,48},{40,56},{48,32},{56,40},{64,80... | collective-permute-start | bytes 196616 | tf_op jit(solution)/shard_map/ppermute | solution.py:327
  179.4 52.2 %collective-permute-start.34 = (f32[128,128]{0,1:T(8,128)S(1)}, f32[128,128]{0,1:T(8,128)S(1)}, u32[]{:S(2)}, u32[]{:S(2)}) collective-permute-start(f32[128,128]{0,1:T(8,128)S(1)} %get-tuple-element.32), channel_id=1, source_target_pairs={{0,1},{1,0},{2,3},{3,2},{4,5},{5,4},{6,7},{7,6},{8,9},{9,8},{10,11... | collective-permute-start | bytes 196616 | tf_op jit(solution)/shard_map/ppermute | solution.py:325
  183.3 52.8 %collective-permute-start.40 = (f32[2,128,128]{1,0,2:T(2,128)S(1)}, f32[2,128,128]{1,0,2:T(2,128)S(1)}, u32[]{:S(2)}, u32[]{:S(2)}) collective-permute-start(f32[2,128,128]{1,0,2:T(2,128)S(1)} %get-tuple-element.41), channel_id=1, source_target_pairs={{0,96},{8,104},{16,112},{24,120},{32,0},{40,8},{48,16},{56,24},{64... | collective-permute-start | bytes 393224 | tf_op jit(solution)/shard_map/ppermute | solution.py:44
  185.2 50.9 %collective-permute-start.39 = (f32[2,128,128]{1,0,2:T(2,128)S(1)}, f32[2,128,128]{1,0,2:T(2,128)S(1)}, u32[]{:S(2)}, u32[]{:S(2)}) collective-permute-start(f32[2,128,128]{1,0,2:T(2,128)S(1)} %get-tuple-element.41), channel_id=1, source_target_pairs={{0,32},{8,40},{16,48},{24,56},{32,64},{40,72},{48,80},{56,88},{64,... | collective-permute-start | bytes 393224 | tf_op jit(solution)/shard_map/ppermute | solution.py:44
  185.2 50.9 %collective-permute-start.41 = (f32[2,128,128]{1,0,2:T(2,128)S(1)}, f32[2,128,128]{1,0,2:T(2,128)S(1)}, u32[]{:S(2)}, u32[]{:S(2)}) collective-permute-start(f32[2,128,128]{1,0,2:T(2,128)S(1)} %get-tuple-element.41), channel_id=1, source_target_pairs={{0,64},{8,72},{16,80},{24,88},{32,96},{40,104},{48,112},{56,120},{... | collective-permute-start | bytes 393224 | tf_op jit(solution)/shard_map/ppermute | solution.py:44
  231.6 10.7 %collective-permute-start.37 = (f32[2,128,128]{1,2,0:T(8,128)S(1)}, f32[2,128,128]{1,2,0:T(8,128)S(1)}, u32[]{:S(2)}, u32[]{:S(2)}) collective-permute-start(f32[2,128,128]{1,2,0:T(8,128)S(1)} %pad_maximum_fusion.3), channel_id=1, source_target_pairs={{0,4},{1,5},{2,6},{3,7},{4,0},{5,1},{6,2},{7,3},{8,12},{9,13},{10,... | collective-permute-start | bytes 393224 | tf_op jit(solution)/shard_map/ppermute | solution.py:44
  232.6 9.7 %collective-permute-start.36 = (f32[2,128,128]{1,2,0:T(8,128)S(1)}, f32[2,128,128]{1,2,0:T(8,128)S(1)}, u32[]{:S(2)}, u32[]{:S(2)}) collective-permute-start(f32[2,128,128]{1,2,0:T(8,128)S(1)} %pad_maximum_fusion.3), channel_id=1, source_target_pairs={{0,6},{1,7},{2,0},{3,1},{4,2},{5,3},{6,4},{7,5},{8,14},{9,15},{10,... | collective-permute-start | bytes 393224 | tf_op jit(solution)/shard_map/ppermute | solution.py:44
  236.1 6.2 %collective-permute-start.35 = (f32[2,128,128]{1,2,0:T(8,128)S(1)}, f32[2,128,128]{1,2,0:T(8,128)S(1)}, u32[]{:S(2)}, u32[]{:S(2)}) collective-permute-start(f32[2,128,128]{1,2,0:T(8,128)S(1)} %pad_maximum_fusion.3), channel_id=1, source_target_pairs={{0,2},{1,3},{2,4},{3,5},{4,6},{5,7},{6,0},{7,1},{8,10},{9,11},{10,... | collective-permute-start | bytes 393224 | tf_op jit(solution)/shard_map/ppermute | solution.py:44
  236.4 7.3 %collective-permute-start.42 = (f32[4,2,128,128]{2,1,0,3:T(2,128)S(1)}, f32[4,2,128,128]{2,1,0,3:T(2,128)S(1)}, u32[]{:S(2)}, u32[]{:S(2)}) collective-permute-start(f32[4,2,128,128]{2,1,0,3:T(2,128)S(1)} %pad_maximum_fusion.2), channel_id=1, source_target_pairs={{0,8},{8,0},{16,24},{24,16},{32,40},{40,32},{48,56},{56,48},{64,72... | collective-permute-start | bytes 1572872 | tf_op jit(solution)/shard_map/ppermute | solution.py:329
  262.5 35.3 %all-to-all-start.1 = ((s16[16,528,128]{2,1,0:T(8,128)(2,1)}), s16[16,528,128]{2,1,0:T(8,128)(2,1)S(1)}, u32[]{:S(2)}, u32[]{:S(2)}) async-start(s16[16,528,128]{2,1,0:T(8,128)(2,1)} %bitcast.80), calls=%async_computation.1 | async-start | bytes 4325376 | tf_op jit(solution)/shard_map/all_to_all | solution.py:356
  297.7 1.4 copy-start.9
  299.1 33.0 %all-to-all-start = ((s16[16,528,128]{2,1,0:T(8,128)(2,1)}), s16[16,528,128]{2,1,0:T(8,128)(2,1)}, u32[]{:S(2)}, u32[]{:S(2)}) async-start(s16[16,528,128]{2,1,0:T(8,128)(2,1)} %bitcast.79), calls=%async_computation | async-start | bytes 4325376 | tf_op jit(solution)/shard_map/all_to_all | solution.py:356
where the time goes:
time: 340 us; the launch traced here: 338 us
  starting transfers between devices  109 us (32%)
  Pallas kernels  99.7 us (29%)
  waiting for transfers between devices  84.4 us (25%)
  other arithmetic  26.8 us (8%)
  local copies, waits for them, and re-layouts  15.3 us (4%)
    pallas_call x4, Pallas kernels, product(): pl.pallas_call(product_kernel, grid=(4,), in_specs=[pl.BlockSpec(memory_s...  44.5 us
    ppermute x8, starting transfers between devices, twin(): return lax.ppermute(value, 'row', row_perm(0, 0, 1))  38.3 us
    all_to_all x2, waiting for transfers between devices, compute(): lax.all_to_all(packed, 'row', split_axis=0, concat_axis=0, tiled=True)  33.4 us
    pallas_call x2, Pallas kernels, epilogue(): pl.pallas_call(lambda *refs: epilogue_kernel(*refs, part=part, inv_snp=1....  32 us
    all_to_all x2, starting transfers between devices, compute(): lax.all_to_all(packed, 'row', split_axis=0, concat_axis=0, tiled=True)  12.8 us
    another operation x3, other arithmetic, compute(): lower = jnp.linalg.cholesky(leading)  12.4 us
    pallas_call x2, Pallas kernels, unpack(): pl.pallas_call(unpack_kernel, grid=(8,), in_specs=[pl.BlockSpec((2, (TILE...  12.1 us
    ppermute x4, starting transfers between devices, ring_sides(): lax.ppermute(shard, axis, perm(-1))  11.9 us
  transfers between devices with their start and end apart: 45, of which 14 were waited for; matrix products, arithmetic and copies ran while one was open for 11% of the time, Pallas kernels for 20%

commit v1 on v0

--- a/solution.py
+++ b/solution.py
@@ -10,8 +10,10 @@
 NZ, NX, NC = 4, 2, 2
 NY, NH = 4, 2
 STEP_OF_SLOT = (0, 3, 1, 2)
-HALVES = 2
-TILE_ROWS = 64 // HALVES
+TILE_ROWS = 64
+HALF = 8
+PAIRS = TILE_ROWS * HALF // 16
+CODED_ROWS = TILE_ROWS * HALF + 16
 LEVELS = 32767.0
 LOG_STEP = 0.6931471805599453 / 64.0
 
@@ -50,67 +52,70 @@
 
 
 def epilogue_kernel(table, running, *refs, part, inv_snp):
-    prods, (row_factor, col_factor, out, values) = refs[:4], refs[4:]
+    prods, col_factors, (row_factor, out, values) = refs[:2], refs[2:4], refs[4:]
     step = pl.program_id(0)
-    row_start = table[32 + step] + part * TILE_ROWS
+    row_start = table[32 + step]
+    old_rows = running.reshape(TILE_ROWS * HALF, 128)
     mine = row_factor[...]
     high = mine.astype(jnp.bfloat16)
     low = (mine - high.astype(jnp.float32)).astype(jnp.bfloat16)
     left = jnp.concatenate([high, high, low], axis=1)
-    for group in range(4):
-        outer = jnp.dot(
-            left,
-            col_factor[:, group * 512 : (group + 1) * 512],
-            preferred_element_type=jnp.float32,
-        )
+    for plane in range(2):
+        outer = jnp.dot(left, col_factors[plane][...], preferred_element_type=jnp.float32)
         for side in range(4):
-            place = table[48 + group * 4 + side]
+            place = table[48 + side] + plane * 4
             lanes = slice(side * 128, (side + 1) * 128)
-            old = running[pl.ds(place, TILE_ROWS, stride=16), :]
-            values[pl.ds(place, TILE_ROWS, stride=16), :] = (
-                old + prods[group][:, lanes] * inv_snp - outer[:, lanes]
+            old = old_rows[pl.ds(place, TILE_ROWS, stride=HALF), :]
+            values[pl.ds(place, TILE_ROWS, stride=HALF), :] = (
+                old + prods[plane][:, lanes] * inv_snp - outer[:, lanes]
             )
 
     @pl.when(row_start < NB)
     def _():
         values[...] = jnp.zeros_like(values)
 
-    @pl.when(table[64] == 1)
-    def _():
-        row_pos = row_start + lax.broadcasted_iota(jnp.int32, (TILE_ROWS, NB), 0)
-        lane = lax.broadcasted_iota(jnp.int32, (TILE_ROWS, NB), 1)
-        values[pl.ds(0, TILE_ROWS, stride=16), :] = jnp.where(row_pos >= lane, mine, 0.0)
+    if part == 0:
+
+        @pl.when(table[56] == 1)
+        def _():
+            row_pos = row_start + lax.broadcasted_iota(jnp.int32, (TILE_ROWS, NB), 0)
+            lane = lax.broadcasted_iota(jnp.int32, (TILE_ROWS, NB), 1)
+            values[pl.ds(0, TILE_ROWS, stride=HALF), :] = jnp.where(row_pos >= lane, mine, 0.0)
 
     peak = jnp.full((16, 128), 1e-30, jnp.float32)
-    for a in range(TILE_ROWS):
+    for a in range(PAIRS):
         peak = jnp.maximum(peak, jnp.abs(values[a * 16 : (a + 1) * 16, :]))
+    peak = jnp.maximum(peak[:8], peak[8:])
     code = jnp.minimum(jnp.ceil(jnp.log(peak) * (1.0 / LOG_STEP)) + 1.0, 8190.0)
+    code = jnp.concatenate([code, code], axis=0)
     gain = LEVELS / jnp.exp(code * LOG_STEP)
-    for a in range(TILE_ROWS):
+    for a in range(PAIRS):
         scaled = jnp.round(values[a * 16 : (a + 1) * 16, :] * gain)
         out[a * 16 : (a + 1) * 16, :] = scaled.astype(jnp.int32).astype(jnp.int16)
-    out[TILE_ROWS * 16 :, :] = code.astype(jnp.int32).astype(jnp.int16)
+    out[TILE_ROWS * HALF :, :] = code.astype(jnp.int32).astype(jnp.int16)
 
 
 def epilogue(part, table, running, prods, row_factor, col_factor, snp_count):
-    block = pl.BlockSpec((TILE_ROWS, 512), lambda i, t: (t[16 + i] * HALVES + part, 0))
+    block = pl.BlockSpec((TILE_ROWS, 512), lambda i, t: (t[16 + i], 0))
     return pl.pallas_call(
         lambda *refs: epilogue_kernel(*refs, part=part, inv_snp=1.0 / snp_count),
         grid_spec=pltpu.PrefetchScalarGridSpec(
             num_scalar_prefetch=1,
             grid=(16,),
             in_specs=[
-                pl.BlockSpec((TILE_ROWS * 16, 128), lambda i, t: (t[i] * HALVES + part, 0)),
-                *[block] * 4,
-                pl.BlockSpec((TILE_ROWS, NB), lambda i, t: (t[16 + i] * HALVES + part, 0)),
-                pl.BlockSpec((3 * NB, 2048), lambda i, t: (0, 0)),
+                pl.BlockSpec((TILE_ROWS, HALF, 128), lambda i, t: (t[i], part, 0)),
+                block,
+                block,
+                pl.BlockSpec((3 * NB, 512), lambda i, t: (0, t[52 + part * 2])),
+                pl.BlockSpec((3 * NB, 512), lambda i, t: (0, t[53 + part * 2])),
+                pl.BlockSpec((TILE_ROWS, NB), lambda i, t: (t[16 + i], 0)),
             ],
-            out_specs=pl.BlockSpec(((TILE_ROWS + 1) * 16, 128), lambda i, t: (i, 0)),
-            scratch_shapes=[pltpu.VMEM((TILE_ROWS * 16, 128), jnp.float32)],
+            out_specs=pl.BlockSpec((CODED_ROWS, 128), lambda i, t: (i, 0)),
+            scratch_shapes=[pltpu.VMEM((TILE_ROWS * HALF, 128), jnp.float32)],
         ),
-        out_shape=jax.ShapeDtypeStruct((16 * (TILE_ROWS + 1) * 16, 128), jnp.int16),
+        out_shape=jax.ShapeDtypeStruct((16 * CODED_ROWS, 128), jnp.int16),
         name="epilogue",
-    )(table, running, *prods, row_factor, col_factor)
+    )(table, running, *prods, col_factor, col_factor, row_factor)
 
 
 ROW_STEP = 256
@@ -118,7 +123,7 @@
 ROW_PLACES += ((3, 6, 0), (3, 7, 64), (3, 8, 128), (3, 9, 192))
 
 
-def fetch_rows(parts, rows, sems, others=()):
+def fetch_rows(parts, rows, sems):
     step = pl.program_id(0)
 
     def copies(n):
@@ -137,45 +142,62 @@
         @pl.when(step == n)
         def _():
             if n == 0:
-                for copy in list(others) + copies(0):
+                for copy in copies(0):
                     copy.start()
             if n < 3:
                 for copy in copies(n + 1):
                     copy.start()
-            for copy in copies(n) + (list(others) if n == 0 else []):
+            for copy in copies(n):
                 copy.wait()
 
 
-def product_kernel(*refs):
-    parts, shards, (out, rows, cols, row_sems, col_sems) = refs[:10], refs[10:14], refs[14:]
-    others = [
-        pltpu.make_async_copy(
-            shards[n], cols.at[:, n * 128 : (n + 1) * 128], col_sems.at[n]
+def product_kernel(slots, *refs, plane):
+    parts, shards, (out, rows, cols, row_sems, col_sems) = refs[:10], refs[10:26], refs[26:]
+    first = pl.program_id(0) == 0
+
+    def copy(slot, side):
+        return pltpu.make_async_copy(
+            shards[slot * 4 + side], cols.at[:, side * 128 : (side + 1) * 128], col_sems.at[side]
         )
-        for n in range(4)
-    ]
-    fetch_rows(parts, rows, row_sems, others)
+
+    for slot in range(4):
+
+        @pl.when(jnp.logical_and(first, slots[plane] == slot))
+        def _():
+            for side in range(4):
+                copy(slot, side).start()
+
+    fetch_rows(parts, rows, row_sems)
+
+    @pl.when(first)
+    def _():
+        for side in range(4):
+            copy(0, side).wait()
+
     out[...] = jnp.dot(
         rows[pl.program_id(0) % 2], cols[...], preferred_element_type=jnp.float32
     )
 
 
-def product(parts, shards):
+def product(plane, slots, parts, shards):
     count = shards[0].shape[0]
     return pl.pallas_call(
-        product_kernel,
-        grid=(4,),
-        in_specs=[pl.BlockSpec(memory_space=pl.ANY)] * 14,
-        out_specs=pl.BlockSpec((ROW_STEP, 512), lambda i: (i, 0)),
-        scratch_shapes=[
-            pltpu.VMEM((2, ROW_STEP, count), jnp.bfloat16),
-            pltpu.VMEM((count, 512), jnp.bfloat16),
-            pltpu.SemaphoreType.DMA((2, 4)),
-            pltpu.SemaphoreType.DMA((4,)),
-        ],
+        lambda *refs: product_kernel(*refs, plane=plane),
+        grid_spec=pltpu.PrefetchScalarGridSpec(
+            num_scalar_prefetch=1,
+            grid=(4,),
+            in_specs=[pl.BlockSpec(memory_space=pl.ANY)] * 26,
+            out_specs=pl.BlockSpec((ROW_STEP, 512), lambda i, t: (i, 0)),
+            scratch_shapes=[
+                pltpu.VMEM((2, ROW_STEP, count), jnp.bfloat16),
+                pltpu.VMEM((count, 512), jnp.bfloat16),
+                pltpu.SemaphoreType.DMA((2, 4)),
+                pltpu.SemaphoreType.DMA((4,)),
+            ],
+        ),
         out_shape=jax.ShapeDtypeStruct((4 * ROW_STEP, 512), jnp.float32),
         name="product",
-    )(*parts, *shards)
+    )(slots, *parts, *shards)
 
 
 def panel_kernel(pick, old, inverse, *refs, inv_snp):
@@ -233,11 +255,12 @@
 def unpack_kernel(coded, *refs):
     out = refs[-1]
     for source in range(2):
-        code = coded[source, TILE_ROWS * 16 :, :].astype(jnp.float32)
+        code = coded[source, TILE_ROWS * HALF :, :].astype(jnp.float32)
         scale = jnp.exp(code * LOG_STEP) * (1.0 / LEVELS)
-        for a in range(TILE_ROWS):
-            values = coded[source, a * 16 : (a + 1) * 16, :].astype(jnp.float32)
-            out[source, 0, a * 16 : (a + 1) * 16, :] = values * scale
+        for a in range(PAIRS):
+            values = coded[source, a * 16 : (a + 1) * 16, :].astype(jnp.float32) * scale
+            row = source * TILE_ROWS + a * 2
+            out[row : row + 2] = values.reshape(2, HALF, 128)
 
 
 def unpack(part, coded, before):
@@ -246,11 +269,11 @@
         unpack_kernel,
         grid=(8,),
         in_specs=[
-            pl.BlockSpec((2, (TILE_ROWS + 1) * 16, 128), lambda i: (i, 0, 0)),
+            pl.BlockSpec((2, CODED_ROWS, 128), lambda i: (i, 0, 0)),
             *[pl.BlockSpec(memory_space=pl.ANY)] * len(begun),
         ],
-        out_specs=pl.BlockSpec((2, 1, TILE_ROWS * 16, 128), lambda i: (i, part, 0, 0)),
-        out_shape=jax.ShapeDtypeStruct((16, HALVES, TILE_ROWS * 16, 128), jnp.float32),
+        out_specs=pl.BlockSpec((2 * TILE_ROWS, HALF, 128), lambda i: (i, part, 0)),
+        out_shape=jax.ShapeDtypeStruct((16 * TILE_ROWS, 2 * HALF, 128), jnp.float32),
         input_output_aliases={1: 0} if begun else {},
         name="unpack",
     )(coded, *begun)
@@ -308,13 +331,13 @@
         (z_opposite, z_opposite_side, twin(z_opposite), twin(z_opposite_side)),
     ]
 
-    away = (0 - z) & 3
-    slot0 = jnp.where(away == 0, 0, jnp.where(away == 1, 2, jnp.where(away == 2, 3, 1)))
-    pick = ((slot0.astype(jnp.uint32) * 2 + core) * 2 + x_lo).astype(jnp.int32)
+    away = (jnp.arange(4, dtype=jnp.uint32) - z) & 3
+    slots = jnp.where(away == 0, 0, jnp.where(away == 1, 2, jnp.where(away == 2, 3, 1)))
+    slots = slots.astype(jnp.int32)
+    pick = slots[0] * 4 + (core * 2 + x_lo).astype(jnp.int32)
     pick = jnp.stack([pick, *[jnp.int32(step) for step in STEP_OF_SLOT]])
-    factor = panel(
-        pick, running[:, 0, 0, :], inverse, row_parts, [s for group in col_shards for s in group]
-    )
+    flat_shards = [shard for group in col_shards for shard in group]
+    factor = panel(pick, running[:, 0, 0, :], inverse, row_parts, flat_shards)
     pieces = factor.reshape(NY, NH, 128, NB)
     heard = lax.ppermute(pieces[:, 1], "col", [(0, 1)])
     pieces = jnp.where(x_hi == 0, pieces[:, 0], heard)
@@ -330,11 +353,6 @@
     high, low = split_bf16(jnp.stack([half, half_twin], axis=1).reshape(2048, NB).T)
     col_factor = jnp.concatenate([high, low, high], axis=0)
 
-    late_rows, _ = lax.optimization_barrier((row_parts, factor))
-    prods = []
-    for g in range(4):
-        prods.append(product(late_rows, col_shards[g]))
-
     tiles = jnp.arange(16, dtype=jnp.uint32)
     hit = grid_map[None, :] == jnp.arange(16, dtype=jnp.int32)[:, None]
     inverse_map = jnp.sum(jnp.where(hit, tiles[None, :], 0), axis=1).astype(jnp.uint32)
@@ -342,18 +360,24 @@
     slot = jnp.where(step_y == 0, 0, jnp.where(step_y == 1, 2, jnp.where(step_y == 2, 3, 1)))
     tile = ((slot.astype(jnp.uint32) * 2) + (((inverse_map >> 1) & 1) ^ x_hi)) * 2 + (inverse_map & 1)
     row_start = row_index * 1024 + inverse_map * 64
-    slot_z = tiles >> 2
-    step_z = jnp.where(slot_z == 0, 0, jnp.where(slot_z == 1, 3, slot_z - 1)).astype(jnp.uint32)
-    place = (((step_z + z) & 3) << 2) + (((tiles & 1) ^ x_lo) << 1) + (((tiles >> 1) & 1) ^ core)
+    side = jnp.arange(4, dtype=jnp.uint32)
+    place = (((side & 1) ^ x_lo) << 1) + ((side >> 1) ^ core)
     is_col0 = jnp.where(col_index == 0, 1, 0).astype(jnp.uint32)
-    table = jnp.concatenate([inverse_map, tile, row_start, place, is_col0[None]]).astype(jnp.int32)
-
-    result = None
-    running = running.reshape(1024 * 16, 128)
-    for part in range(HALVES):
+    table = jnp.concatenate(
+        [inverse_map, tile, row_start, place, slots.astype(jnp.uint32), is_col0[None]]
+    ).astype(jnp.int32)
+
+    result, packed = None, factor
+    running = running.reshape(1024, 16, 128)
+    for part in range(2):
+        late_rows, packed = lax.optimization_barrier((row_parts, packed))
+        prods = []
+        for plane in (2 * part, 2 * part + 1):
+            prods.append(product(plane, slots, late_rows, flat_shards))
         packed = epilogue(part, table, running, prods, row_factor, col_factor, snp_count)
-        packed = packed.reshape(16, (TILE_ROWS + 1) * 16, 128)
-        coded = lax.all_to_all(packed, "row", split_axis=0, concat_axis=0, tiled=True)
+        coded = lax.all_to_all(
+            packed.reshape(16, CODED_ROWS, 128), "row", split_axis=0, concat_axis=0, tiled=True
+        )
         result = unpack(part, coded, result)
     return result.reshape(16, 1, 64, 16, 1, 128)
 

time: 340 us -> 330 us (0.971)
  waiting for transfers between devices: 84.4 us -> 73.9 us
    all_to_all x2, waiting for transfers between devices: 33.4 us -> 21.7 us  [compute(): lax.all_to_all(packed.reshape(16, CODED_ROWS, 128), 'row', split_axis=0,...]
  transfers between devices with their start and end apart: 45 -> 45, of which waited for: 14 -> 15; matrix products, arithmetic and copies ran while one was open for 11% -> 11% of each run, Pallas kernels for 20% -> 20%
where the time goes in v1:
time: 330 us; the launch traced here: 328 us
  starting transfers between devices  109 us (33%)
  Pallas kernels  98.2 us (30%)
  waiting for transfers between devices  73.9 us (22%)
  other arithmetic  26.8 us (8%)
  local copies, waits for them, and re-layouts  18.4 us (6%)
    pallas_call x4, Pallas kernels, product(): pl.pallas_call(lambda *refs: product_kernel(*refs, plane=plane), grid_spe...  46.2 us
    ppermute x8, starting transfers between devices, twin(): return lax.ppermute(value, 'row', row_perm(0, 0, 1))  38 us
    pallas_call x2, Pallas kernels, epilogue(): pl.pallas_call(lambda *refs: epilogue_kernel(*refs, part=part, inv_snp=1....  28.8 us
    all_to_all x2, waiting for transfers between devices, compute(): lax.all_to_all(packed.reshape(16, CODED_ROWS, 128), 'row', split_axis=0,...  21.7 us
    all_to_all x2, starting transfers between devices, compute(): lax.all_to_all(packed.reshape(16, CODED_ROWS, 128), 'row', split_axis=0,...  13.8 us
    another operation x3, other arithmetic, compute(): lower = jnp.linalg.cholesky(leading)  12.4 us
    pallas_call x2, Pallas kernels, unpack(): pl.pallas_call(unpack_kernel, grid=(8,), in_specs=[pl.BlockSpec((2, CODED...  12.1 us
    ppermute x4, starting transfers between devices, ring_sides(): lax.ppermute(shard, axis, perm(-1))  11.9 us
  transfers between devices with their start and end apart: 45, of which 15 were waited for; matrix products, arithmetic and copies ran while one was open for 11% of the time, Pallas kernels for 20%

profile of v1, /device:TPU:1, one launch (start us, length us, event | category | flops | bytes accessed | tf_op | source)
XLA Modules:
  0.0 328.0 jit_solution(17902041892451630339)
XLA Ops:
  0.0 1.7 copy.14
  1.7 3.6 %collective-permute-start = (bf16[128,5120]{1,0:T(8,128)(2,1)S(1)}, bf16[128,5120]{1,0:T(8,128)(2,1)}, u32[]{:S(2)}, u32[]{:S(2)}) collective-permute-start(bf16[128,5120]{1,0:T(8,128)(2,1)S(1)} %bitcast.68), channel_id=1, source_target_pairs={{0,1},{1,0},{2,3},{3,2},{4,5},{5,4},{6,7},{7,6},{8,9},{9,8},{10,11... | collective-permute-start | bytes 3932168 | tf_op jit(solution)/shard_map/ppermute | solution.py:298
  5.4 2.7 collective-permute-start.3
  9.7 11.7 %cholesky.20 = f32[128,128]{1,0:T(8,128)S(1)} custom-call(f32[128,128]{1,0:T(8,128)S(1)} %fusion.6), custom_call_target="Cholesky" | custom-call | tf_op jit(solution)/shard_map/jit(cholesky)/cholesky | solution.py:303
  22.8 10.8 %collective-permute-done.refs_4_.refs_2_ = bf16[128,5120]{1,0:T(8,128)(2,1)} collective-permute-done((bf16[128,5120]{1,0:T(8,128)(2,1)S(1)}, bf16[128,5120]{1,0:T(8,128)(2,1)}, u32[]{:S(2)}, u32[]{:S(2)}) %collective-permute-start) | collective-permute-done | bytes 1310752 | tf_op jit(solution)/shard_map/ppermute | solution.py:298
  33.6 9.8 %custom-call.6 = f32[1,128,128]{1,2,0:T(8,128)S(1)} custom-call(f32[1,128,128]{2,1,0:T(8,128)S(1)} %select_bitcast_fusion), custom_call_target="InvertDiagBlocksLowerTriangular" | custom-call | tf_op jit(solution)/shard_map/triangular_solve | solution.py:311
  45.7 4.2 %collective-permute-start.21 = (bf16[5120,128]{1,0:T(8,128)(2,1)S(1)}, bf16[5120,128]{1,0:T(8,128)(2,1)}, u32[]{:S(2)}, u32[]{:S(2)}) collective-permute-start(bf16[5120,128]{1,0:T(8,128)(2,1)S(1)} %copy-done), channel_id=1, source_target_pairs={{0,96},{8,104},{16,112},{24,120},{32,0},{40,8},{48,16},{56,24},{64... | collective-permute-start | bytes 3932168 | tf_op jit(solution)/shard_map/ppermute | solution.py:35
  49.8 7.9 %collective-permute-start.15 = (bf16[5120,128]{1,0:T(8,128)(2,1)S(1)}, bf16[5120,128]{1,0:T(8,128)(2,1)}, u32[]{:S(2)}, u32[]{:S(2)}) collective-permute-start(bf16[5120,128]{1,0:T(8,128)(2,1)S(1)} %copy-done), channel_id=1, source_target_pairs={{0,8},{8,0},{16,24},{24,16},{32,40},{40,32},{48,56},{56,48},{64,72... | collective-permute-start | bytes 3932168 | tf_op jit(solution)/shard_map/ppermute | solution.py:294
  58.4 2.0 slice.71
  60.4 2.7 collective-permute-start.6
  63.1 2.0 slice.70
  65.1 6.8 %collective-permute-done.21.refs_21_.refs_19_ = bf16[5120,128]{1,0:T(8,128)(2,1)} collective-permute-done((bf16[5120,128]{1,0:T(8,128)(2,1)S(1)}, bf16[5120,128]{1,0:T(8,128)(2,1)}, u32[]{:S(2)}, u32[]{:S(2)}) %collective-permute-start.21) | collective-permute-done | bytes 1310752 | tf_op jit(solution)/shard_map/ppermute | solution.py:35
  71.9 1.3 collective-permute-start.13
  73.1 1.1 slice.75
  74.3 3.6 %collective-permute-start.26 = (bf16[2560,128]{1,0:T(8,128)(2,1)S(1)}, bf16[2560,128]{1,0:T(8,128)(2,1)S(1)}, u32[]{:S(2)}, u32[]{:S(2)}) collective-permute-start(bf16[2560,128]{1,0:T(8,128)(2,1)S(1)} %slice.75), channel_id=1, source_target_pairs={{0,96},{8,104},{16,112},{24,120},{32,0},{40,8},{48,16},{56,24},{64... | collective-permute-start | bytes 1966088 | tf_op jit(solution)/shard_map/ppermute | solution.py:41
  77.9 1.1 slice.74
  79.0 1.1 collective-permute-start.25
  80.1 2.2 collective-permute-done.13
  82.3 2.7 collective-permute-start.14
  85.0 2.7 collective-permute-start.4
  88.3 6.3 %collective-permute-start.23 = (bf16[5120,128]{1,0:T(8,128)(2,1)}, bf16[5120,128]{1,0:T(8,128)(2,1)S(1)}, u32[]{:S(2)}, u32[]{:S(2)}) collective-permute-start(bf16[5120,128]{1,0:T(8,128)(2,1)} %collective-permute-done.21.refs_21_.refs_19_), channel_id=1, source_target_pairs={{0,8},{8,0},{16,24},{24,16},{32,40},{40,32},{48,56},{56,48},{64,72... | collective-permute-start | bytes 3932168 | tf_op jit(solution)/shard_map/ppermute | solution.py:294
  94.7 4.9 %collective-permute-start.19 = (bf16[5120,128]{1,0:T(8,128)(2,1)}, bf16[5120,128]{1,0:T(8,128)(2,1)S(1)}, u32[]{:S(2)}, u32[]{:S(2)}) collective-permute-start(bf16[5120,128]{1,0:T(8,128)(2,1)} %collective-permute-done.17.refs_17_.refs_15_), channel_id=1, source_target_pairs={{0,8},{8,0},{16,24},{24,16},{32,40},{40,32},{48,56},{56,48},{64,72... | collective-permute-start | bytes 3932168 | tf_op jit(solution)/shard_map/ppermute | solution.py:294
  101.3 9.1 %collective-permute-done.14.refs_14_.refs_12_ = bf16[5120,128]{1,0:T(8,128)(2,1)S(1)} collective-permute-done((bf16[5120,128]{1,0:T(8,128)(2,1)S(1)}, bf16[5120,128]{1,0:T(8,128)(2,1)S(1)}, u32[]{:S(2)}, u32[]{:S(2)}) %collective-permute-start.14) | collective-permute-done | bytes 1310752 | tf_op jit(solution)/shard_map/ppermute | solution.py:306
  110.4 2.2 collective-permute-start.27
  113.0 2.3 collective-permute-start.22
  116.1 1.0 copy-done.3
  117.2 2.6 collective-permute-start.8
  119.8 9.5 %collective-permute-done.8.refs_12_.refs_10_ = bf16[64,5120]{1,0:T(8,128)(2,1)S(1)} collective-permute-done((bf16[64,5120]{1,0:T(8,128)(2,1)S(1)}, bf16[64,5120]{1,0:T(8,128)(2,1)S(1)}, u32[]{:S(2)}, u32[]{:S(2)}) %collective-permute-start.8) | collective-permute-done | bytes 655392 | tf_op jit(solution)/shard_map/ppermute | solution.py:41
  129.3 5.4 %collective-permute-start.28 = (bf16[5120,128]{1,0:T(8,128)(2,1)}, bf16[5120,128]{1,0:T(8,128)(2,1)}, u32[]{:S(2)}, u32[]{:S(2)}) collective-permute-start(bf16[5120,128]{1,0:T(8,128)(2,1)} %constant_dynamic-update-slice_fusion.refs_25_.refs_23_), channel_id=1, source_target_pairs={{0,8},{8,0},{16,24},{24,16},{32,40},{40,32},{48,56},{56,48},{64,72... | collective-permute-start | bytes 3932168 | tf_op jit(solution)/shard_map/ppermute | solution.py:294
  134.7 3.4 %collective-permute-start.16 = (bf16[5120,128]{1,0:T(8,128)(2,1)S(1)}, bf16[5120,128]{1,0:T(8,128)(2,1)}, u32[]{:S(2)}, u32[]{:S(2)}) collective-permute-start(bf16[5120,128]{1,0:T(8,128)(2,1)S(1)} %collective-permute-done.14.refs_14_.refs_12_), channel_id=1, source_target_pairs={{0,8},{8,0},{16,24},{24,16},{32,40},{40,32},{48,56},{56,48},{64,72... | collective-permute-start | bytes 3932168 | tf_op jit(solution)/shard_map/ppermute | solution.py:294
  138.5 4.3 %collective-permute-start.29 = (bf16[5120,128]{1,0:T(8,128)(2,1)S(1)}, bf16[5120,128]{1,0:T(8,128)(2,1)}, u32[]{:S(2)}, u32[]{:S(2)}) collective-permute-start(bf16[5120,128]{1,0:T(8,128)(2,1)S(1)} %collective-permute-done.27.refs_26_.refs_24_), channel_id=1, source_target_pairs={{0,8},{8,0},{16,24},{24,16},{32,40},{40,32},{48,56},{56,48},{64,72... | collective-permute-start | bytes 3932168 | tf_op jit(solution)/shard_map/ppermute | solution.py:294
  142.8 1.5 collective-permute-start.24
  144.3 4.3 %collective-permute-start.20 = (bf16[5120,128]{1,0:T(8,128)(2,1)}, bf16[5120,128]{1,0:T(8,128)(2,1)}, u32[]{:S(2)}, u32[]{:S(2)}) collective-permute-start(bf16[5120,128]{1,0:T(8,128)(2,1)} %collective-permute-done.18.refs_18_.refs_16_), channel_id=1, source_target_pairs={{0,8},{8,0},{16,24},{24,16},{32,40},{40,32},{48,56},{56,48},{64,72... | collective-permute-start | bytes 3932168 | tf_op jit(solution)/shard_map/ppermute | solution.py:294
  148.6 1.9 slice.61
  151.8 11.1 %panel.1 = f32[1024,128]{1,0:T(8,128)} custom-call(s32[5]{0:T(128)} %stack.47.refs_0_, f32[1024,128]{1,0:T(8,128)} %bitcast.82, f32[128,128]{1,0:T(8,128)} %broadcast_select_fusion.1.refs_2_, bf16[128,5120]{1,0:T(8,128)(2,1)} %bitcast.71, bf16[128,5120]{1,0:T(8,128)(2,1)} %collective-permute-done.refs_4_.refs_2_, ...), custom_call_target="tpu_custom_call" | custom-call | tf_op jit(solution)/shard_map/panel/pallas_call | solution.py:232
  163.0 1.0 slice_bitcast_fusion
  163.9 4.1 %collective-permute-start.30 = (f32[4,128,128]{2,1,0:T(8,128)S(1)}, f32[4,128,128]{2,1,0:T(8,128)S(1)}, u32[]{:S(2)}, u32[]{:S(2)}) collective-permute-start(f32[4,128,128]{2,1,0:T(8,128)S(1)} %slice_bitcast_fusion), channel_id=1, source_target_pairs={{0,1},{8,9},{16,17},{24,25},{32,33},{40,41},{48,49},{56,57},{64,65... | collective-permute-start | bytes 786440 | tf_op jit(solution)/shard_map/ppermute | solution.py:342
  168.0 5.4 %collective-permute-done.30 = f32[4,128,128]{2,1,0:T(8,128)S(1)} collective-permute-done((f32[4,128,128]{2,1,0:T(8,128)S(1)}, f32[4,128,128]{2,1,0:T(8,128)S(1)}, u32[]{:S(2)}, u32[]{:S(2)}) %collective-permute-start.30) | collective-permute-done | bytes 262176 | tf_op jit(solution)/shard_map/ppermute | solution.py:342
  173.5 1.0 fusion.2
  174.5 1.3 collective-permute-start.32
  175.8 1.3 collective-permute-start.33
  177.1 1.3 collective-permute-start.31
  178.5 1.2 collective-permute-done.31
  179.7 3.8 %collective-permute-start.39 = (f32[128,128]{1,0:T(8,128)S(1)}, f32[128,128]{1,0:T(8,128)S(1)}, u32[]{:S(2)}, u32[]{:S(2)}) collective-permute-start(f32[128,128]{1,0:T(8,128)S(1)} %get-tuple-element.52), channel_id=1, source_target_pairs={{0,1},{1,0},{2,3},{3,2},{4,5},{5,4},{6,7},{7,6},{8,9},{9,8},{10,11... | collective-permute-start | bytes 196616 | tf_op jit(solution)/shard_map/ppermute | solution.py:348
  183.5 1.6 collective-permute-done.39
  185.2 1.8 collective-permute-done.34
  187.0 1.2 collective-permute-start.36
  188.5 0.9 collective-permute-start.37
  190.0 11.5 %product.5.refs_3_ = f32[1024,512]{1,0:T(8,128)} custom-call(s32[4]{0:T(128)} %copy-done.13, bf16[128,5120]{1,0:T(8,128)(2,1)} %bitcast.72, bf16[128,5120]{1,0:T(8,128)(2,1)} %collective-permute-done.refs_4_.refs_2_, bf16[128,5120]{1,0:T(8,128)(2,1)} %collective-permute-done.1.refs_5_.refs_3_, bf16[128,5120]{1,0:T(8,128)(2,1)} %copy-done.3, ...), custom_call_target="tpu_custom_call" | custom-call | tf_op jit(solution)/shard_map/product/pallas_call | solution.py:184
  201.5 11.5 %product.4.refs_2_ = f32[1024,512]{1,0:T(8,128)} custom-call(s32[4]{0:T(128)} %copy-done.13, bf16[128,5120]{1,0:T(8,128)(2,1)} %bitcast.73, bf16[128,5120]{1,0:T(8,128)(2,1)} %collective-permute-done.refs_4_.refs_2_, bf16[128,5120]{1,0:T(8,128)(2,1)} %collective-permute-done.1.refs_5_.refs_3_, bf16[128,5120]{1,0:T(8,128)(2,1)} %copy-done.3, ...), custom_call_target="tpu_custom_call" | custom-call | tf_op jit(solution)/shard_map/product/pallas_call | solution.py:184
  213.7 3.5 %collective-permute-start.41 = (f32[2,128,128]{2,1,0:T(8,128)S(1)}, f32[2,128,128]{2,1,0:T(8,128)S(1)}, u32[]{:S(2)}, u32[]{:S(2)}) collective-permute-start(f32[2,128,128]{2,1,0:T(8,128)S(1)} %get-tuple-element.62), channel_id=1, source_target_pairs={{0,6},{1,7},{2,0},{3,1},{4,2},{5,3},{6,4},{7,5},{8,14},{9,15},{10,... | collective-permute-start | bytes 393224 | tf_op jit(solution)/shard_map/ppermute | solution.py:46
  217.3 4.5 %collective-permute-start.38 = (f32[4,2,128,128]{3,2,1,0:T(8,128)S(1)}, f32[4,2,128,128]{3,2,1,0:T(8,128)S(1)}, u32[]{:S(2)}, u32[]{:S(2)}) collective-permute-start(f32[4,2,128,128]{3,2,1,0:T(8,128)S(1)} %get-tuple-element.56), channel_id=1, source_target_pairs={{0,8},{8,0},{16,24},{24,16},{32,40},{40,32},{48,56},{56,48},{64,72... | collective-permute-start | bytes 1572872 | tf_op jit(solution)/shard_map/ppermute | solution.py:352
  221.7 1.8 collective-permute-done.40
  225.6 1.3 pad_maximum_fusion.refs_4_.refs_5_
  226.9 14.5 %epilogue.2 = s16[8448,128]{1,0:T(8,128)(2,1)} custom-call(s32[57]{0:T(128)} %convert_element_type.35.refs_0_, f32[1024,16,128]{2,1,0:T(8,128)} %bitcast.76, f32[1024,512]{1,0:T(8,128)} %product.4.refs_2_, f32[1024,512]{1,0:T(8,128)} %product.5.refs_3_, bf16[384,2048]{1,0:T(8,128)(2,1)} %pad_maximum_fusion.refs_4_.refs_5_, ...), custom_call_target="tpu_custom_call" | custom-call | tf_op jit(solution)/shard_map/epilogue/pallas_call | solution.py:100
  241.3 8.4 %all-to-all-start.1 = ((s16[16,528,128]{2,1,0:T(8,128)(2,1)}), s16[16,528,128]{2,1,0:T(8,128)(2,1)S(1)}, u32[]{:S(2)}, u32[]{:S(2)}) async-start(s16[16,528,128]{2,1,0:T(8,128)(2,1)} %bitcast.78), calls=%async_computation.1 | async-start | bytes 4325376 | tf_op jit(solution)/shard_map/all_to_all | solution.py:378
  249.8 11.4 %product.7.refs_3_ = f32[1024,512]{1,0:T(8,128)} custom-call(s32[4]{0:T(128)} %copy-done.13, bf16[128,5120]{1,0:T(8,128)(2,1)} %bitcast.74, bf16[128,5120]{1,0:T(8,128)(2,1)} %collective-permute-done.refs_4_.refs_2_, bf16[128,5120]{1,0:T(8,128)(2,1)} %collective-permute-done.1.refs_5_.refs_3_, bf16[128,5120]{1,0:T(8,128)(2,1)} %copy-done.3, ...), custom_call_target="tpu_custom_call" | custom-call | tf_op jit(solution)/shard_map/product/pallas_call | solution.py:184
  261.2 11.8 %product.6.refs_2_ = f32[1024,512]{1,0:T(8,128)} custom-call(s32[4]{0:T(128)} %copy-done.13, bf16[128,5120]{1,0:T(8,128)(2,1)} %bitcast.75, bf16[128,5120]{1,0:T(8,128)(2,1)} %collective-permute-done.refs_4_.refs_2_, bf16[128,5120]{1,0:T(8,128)(2,1)} %collective-permute-done.1.refs_5_.refs_3_, bf16[128,5120]{1,0:T(8,128)(2,1)} %copy-done.3, ...), custom_call_target="tpu_custom_call" | custom-call | tf_op jit(solution)/shard_map/product/pallas_call | solution.py:184
  273.1 14.4 %epilogue.3 = s16[8448,128]{1,0:T(8,128)(2,1)} custom-call(s32[57]{0:T(128)} %convert_element_type.35.refs_0_, f32[1024,16,128]{2,1,0:T(8,128)} %bitcast.77, f32[1024,512]{1,0:T(8,128)} %product.6.refs_2_, f32[1024,512]{1,0:T(8,128)} %product.7.refs_3_, bf16[384,2048]{1,0:T(8,128)(2,1)} %pad_maximum_fusion.refs_4_.refs_5_, ...), custom_call_target="tpu_custom_call" | custom-call | tf_op jit(solution)/shard_map/epilogue/pallas_call | solution.py:100
  287.4 1.4 copy-done.11
  288.8 5.3 %all-to-all-start = ((s16[16,528,128]{2,1,0:T(8,128)(2,1)}), s16[16,528,128]{2,1,0:T(8,128)(2,1)}, u32[]{:S(2)}, u32[]{:S(2)}) async-start(s16[16,528,128]{2,1,0:T(8,128)(2,1)} %bitcast.79), calls=%async_computation | async-start | bytes 4325376 | tf_op jit(solution)/shard_map/all_to_all | solution.py:378
  294.2 6.1 %unpack.2.refs_0_ = f32[1024,16,128]{2,1,0:T(8,128)} custom-call(s16[16,528,128]{2,1,0:T(8,128)(2,1)} %copy-done.11), custom_call_target="tpu_custom_call" | custom-call | tf_op jit(solution)/shard_map/unpack/pallas_call | solution.py:268
  300.2 21.7 %all-to-all-done.coded = s16[16,528,128]{2,1,0:T(8,128)(2,1)} async-done(((s16[16,528,128]{2,1,0:T(8,128)(2,1)}), s16[16,528,128]{2,1,0:T(8,128)(2,1)}, u32[]{:S(2)}, u32[]{:S(2)}) %all-to-all-start) | async-done | bytes 2162720 | tf_op jit(solution)/shard_map/all_to_all | solution.py:378
  321.9 6.1 %unpack.3 = f32[1024,16,128]{2,1,0:T(8,128)} custom-call(s16[16,528,128]{2,1,0:T(8,128)(2,1)} %all-to-all-done.coded, f32[1024,16,128]{2,1,0:T(8,128)} %unpack.2.refs_0_), custom_call_target="tpu_custom_call", output_to_operand_aliasing={{}: (1, {})} | custom-call | tf_op jit(solution)/shard_map/unpack/pallas_call | solution.py:268
  (113 shorter events, 15.1 us)
Async XLA Ops:
  0.0 9.0 %copy-start = (bf16[5120,128]{1,0:T(8,128)(2,1)S(1)}, bf16[5120,128]{1,0:T(8,128)(2,1)}, u32[]{:S(2)}) copy-start(bf16[5120,128]{1,0:T(8,128)(2,1)} %refs_11_.7) | copy-start | bytes 3932164
  1.7 7.9 %copy-start.1 = (bf16[5120,128]{0,1:T(8,128)(2,1)}, bf16[5120,128]{0,1:T(8,128)(2,1)S(1)}, u32[]{:S(2)}) copy-start(bf16[5120,128]{0,1:T(8,128)(2,1)S(1)} %copy.14) | copy-start | bytes 3932164
  1.7 31.8 %collective-permute-start = (bf16[128,5120]{1,0:T(8,128)(2,1)S(1)}, bf16[128,5120]{1,0:T(8,128)(2,1)}, u32[]{:S(2)}, u32[]{:S(2)}) collective-permute-start(bf16[128,5120]{1,0:T(8,128)(2,1)S(1)} %bitcast.68), channel_id=1, source_target_pairs={{0,1},{1,0},{2,3},{3,2},{4,5},{5,4},{6,7},{7,6},{8,9},{9,8},{10,11... | collective-permute-start | bytes 3932168 | tf_op jit(solution)/shard_map/ppermute | solution.py:298
  5.4 52.4 %collective-permute-start.3 = (bf16[128,5120]{1,0:T(8,128)(2,1)S(1)}, bf16[128,5120]{1,0:T(8,128)(2,1)}, u32[]{:S(2)}, u32[]{:S(2)}) collective-permute-start(bf16[128,5120]{1,0:T(8,128)(2,1)S(1)} %bitcast.69), channel_id=1, source_target_pairs={{0,6},{1,7},{2,0},{3,1},{4,2},{5,3},{6,4},{7,5},{8,14},{9,15},{10,... | collective-permute-start | bytes 3932168 | tf_op jit(solution)/shard_map/ppermute | solution.py:35
  8.1 52.3 %collective-permute-start.1 = (bf16[128,5120]{1,0:T(8,128)(2,1)S(1)}, bf16[128,5120]{1,0:T(8,128)(2,1)}, u32[]{:S(2)}, u32[]{:S(2)}) collective-permute-start(bf16[128,5120]{1,0:T(8,128)(2,1)S(1)} %bitcast.70), channel_id=1, source_target_pairs={{0,2},{1,3},{2,4},{3,5},{4,6},{5,7},{6,0},{7,1},{8,10},{9,11},{10,... | collective-permute-start | bytes 3932168 | tf_op jit(solution)/shard_map/ppermute | solution.py:35
  43.6 2.0 collective-permute-start.11
  44.3 5.5 %collective-permute-start.10 = (f32[128,128]{1,0:T(8,128)S(1)}, f32[128,128]{1,0:T(8,128)S(1)}, u32[]{:S(2)}, u32[]{:S(2)}) collective-permute-start(f32[128,128]{1,0:T(8,128)S(1)} %fusion.4), channel_id=1, source_target_pairs={{0,64},{1,65},{2,66},{3,67},{4,68},{5,69},{6,70},{7,71}} | collective-permute-start | bytes 196616 | tf_op jit(solution)/shard_map/ppermute | solution.py:315
  45.0 4.8 %collective-permute-start.9 = (f32[128,128]{1,0:T(8,128)S(1)}, f32[128,128]{1,0:T(8,128)S(1)}, u32[]{:S(2)}, u32[]{:S(2)}) collective-permute-start(f32[128,128]{1,0:T(8,128)S(1)} %fusion.4), channel_id=1, source_target_pairs={{0,32},{1,33},{2,34},{3,35},{4,36},{5,37},{6,38},{7,39}} | collective-permute-start | bytes 196616 | tf_op jit(solution)/shard_map/ppermute | solution.py:315
  45.7 26.2 %collective-permute-start.21 = (bf16[5120,128]{1,0:T(8,128)(2,1)S(1)}, bf16[5120,128]{1,0:T(8,128)(2,1)}, u32[]{:S(2)}, u32[]{:S(2)}) collective-permute-start(bf16[5120,128]{1,0:T(8,128)(2,1)S(1)} %copy-done), channel_id=1, source_target_pairs={{0,96},{8,104},{16,112},{24,120},{32,0},{40,8},{48,16},{56,24},{64... | collective-permute-start | bytes 3932168 | tf_op jit(solution)/shard_map/ppermute | solution.py:35
  49.8 24.5 %collective-permute-start.17 = (bf16[5120,128]{1,0:T(8,128)(2,1)S(1)}, bf16[5120,128]{1,0:T(8,128)(2,1)}, u32[]{:S(2)}, u32[]{:S(2)}) collective-permute-start(bf16[5120,128]{1,0:T(8,128)(2,1)S(1)} %copy-done), channel_id=1, source_target_pairs={{0,32},{8,40},{16,48},{24,56},{32,64},{40,72},{48,80},{56,88},{64,... | collective-permute-start | bytes 3932168 | tf_op jit(solution)/shard_map/ppermute | solution.py:35
  49.8 29.2 %collective-permute-start.15 = (bf16[5120,128]{1,0:T(8,128)(2,1)S(1)}, bf16[5120,128]{1,0:T(8,128)(2,1)}, u32[]{:S(2)}, u32[]{:S(2)}) collective-permute-start(bf16[5120,128]{1,0:T(8,128)(2,1)S(1)} %copy-done), channel_id=1, source_target_pairs={{0,8},{8,0},{16,24},{24,16},{32,40},{40,32},{48,56},{56,48},{64,72... | collective-permute-start | bytes 3932168 | tf_op jit(solution)/shard_map/ppermute | solution.py:294
  57.7 7.4 %collective-permute-start.12 = (f32[128,128]{1,0:T(8,128)S(1)}, f32[128,128]{1,0:T(8,128)S(1)}, u32[]{:S(2)}, u32[]{:S(2)}) collective-permute-start(f32[128,128]{1,0:T(8,128)S(1)} %add_select_fusion), channel_id=1, source_target_pairs={{0,16},{32,48},{64,80},{96,112},{1,17},{33,49},{65,81},{97,113},{2... | collective-permute-start | bytes 196616 | tf_op jit(solution)/shard_map/ppermute | solution.py:318
  60.4 24.6 %collective-permute-start.6 = (bf16[64,5120]{1,0:T(8,128)(2,1)}, bf16[64,5120]{1,0:T(8,128)(2,1)S(1)}, u32[]{:S(2)}, u32[]{:S(2)}) collective-permute-start(bf16[64,5120]{1,0:T(8,128)(2,1)} %slice.71), channel_id=1, source_target_pairs={{0,6},{1,7},{2,0},{3,1},{4,2},{5,3},{6,4},{7,5},{8,14},{9,15},{10,... | collective-permute-start | bytes 1966088 | tf_op jit(solution)/shard_map/ppermute | solution.py:41
  65.1 22.6 %collective-permute-start.5 = (bf16[64,5120]{1,0:T(8,128)(2,1)}, bf16[64,5120]{1,0:T(8,128)(2,1)}, u32[]{:S(2)}, u32[]{:S(2)}) collective-permute-start(bf16[64,5120]{1,0:T(8,128)(2,1)} %slice.70), channel_id=1, source_target_pairs={{0,2},{1,3},{2,4},{3,5},{4,6},{5,7},{6,0},{7,1},{8,10},{9,11},{10,... | collective-permute-start | bytes 1966088 | tf_op jit(solution)/shard_map/ppermute | solution.py:40
  71.9 10.4 %collective-permute-start.13 = (f32[128,128]{1,0:T(8,128)S(1)}, f32[128,128]{1,0:T(8,128)S(1)}, u32[]{:S(2)}, u32[]{:S(2)}) collective-permute-start(f32[128,128]{1,0:T(8,128)S(1)} %broadcast_select_fusion), channel_id=1, source_target_pairs={{0,8},{16,24},{32,40},{48,56},{64,72},{80,88},{96,104},{112,120},{... | collective-permute-start | bytes 196616 | tf_op jit(solution)/shard_map/ppermute | solution.py:322
  74.3 14.0 %collective-permute-start.26 = (bf16[2560,128]{1,0:T(8,128)(2,1)S(1)}, bf16[2560,128]{1,0:T(8,128)(2,1)S(1)}, u32[]{:S(2)}, u32[]{:S(2)}) collective-permute-start(bf16[2560,128]{1,0:T(8,128)(2,1)S(1)} %slice.75), channel_id=1, source_target_pairs={{0,96},{8,104},{16,112},{24,120},{32,0},{40,8},{48,16},{56,24},{64... | collective-permute-start | bytes 1966088 | tf_op jit(solution)/shard_map/ppermute | solution.py:41
  79.0 15.6 %collective-permute-start.25 = (bf16[2560,128]{1,0:T(8,128)(2,1)S(1)}, bf16[2560,128]{1,0:T(8,128)(2,1)S(1)}, u32[]{:S(2)}, u32[]{:S(2)}) collective-permute-start(bf16[2560,128]{1,0:T(8,128)(2,1)S(1)} %slice.74), channel_id=1, source_target_pairs={{0,32},{8,40},{16,48},{24,56},{32,64},{40,72},{48,80},{56,88},{64,... | collective-permute-start | bytes 1966088 | tf_op jit(solution)/shard_map/ppermute | solution.py:40
  82.3 28.2 %collective-permute-start.14 = (bf16[5120,128]{1,0:T(8,128)(2,1)S(1)}, bf16[5120,128]{1,0:T(8,128)(2,1)S(1)}, u32[]{:S(2)}, u32[]{:S(2)}) collective-permute-start(bf16[5120,128]{1,0:T(8,128)(2,1)S(1)} %copy-done), channel_id=1, source_target_pairs={{0,16},{8,24},{16,0},{24,8},{32,48},{40,56},{48,32},{56,40},{64,80... | collective-permute-start | bytes 3932168 | tf_op jit(solution)/shard_map/ppermute | solution.py:306
  85.0 31.1 %copy-start.8 = (bf16[64,5120]{1,0:T(8,128)(2,1)}, bf16[64,5120]{1,0:T(8,128)(2,1)S(1)}, u32[]{:S(2)}) copy-start(bf16[64,5120]{1,0:T(8,128)(2,1)S(1)} %collective-permute-done.6.refs_10_.refs_8_) | copy-start | bytes 1966084
  85.0 28.0 %collective-permute-start.4 = (bf16[128,5120]{1,0:T(8,128)(2,1)}, bf16[128,5120]{1,0:T(8,128)(2,1)S(1)}, u32[]{:S(2)}, u32[]{:S(2)}) collective-permute-start(bf16[128,5120]{1,0:T(8,128)(2,1)} %collective-permute-done.refs_4_.refs_2_), channel_id=1, source_target_pairs={{0,6},{1,7},{2,0},{3,1},{4,2},{5,3},{6,4},{7,5},{8,14},{9,15},{10,... | collective-permute-start | bytes 3932168 | tf_op jit(solution)/shard_map/ppermute | solution.py:35
  87.7 28.3 %collective-permute-start.2 = (bf16[128,5120]{1,0:T(8,128)(2,1)}, bf16[128,5120]{1,0:T(8,128)(2,1)S(1)}, u32[]{:S(2)}, u32[]{:S(2)}) collective-permute-start(bf16[128,5120]{1,0:T(8,128)(2,1)} %collective-permute-done.refs_4_.refs_2_), channel_id=1, source_target_pairs={{0,2},{1,3},{2,4},{3,5},{4,6},{5,7},{6,0},{7,1},{8,10},{9,11},{10,... | collective-permute-start | bytes 3932168 | tf_op jit(solution)/shard_map/ppermute | solution.py:35
  88.3 28.8 %collective-permute-start.23 = (bf16[5120,128]{1,0:T(8,128)(2,1)}, bf16[5120,128]{1,0:T(8,128)(2,1)S(1)}, u32[]{:S(2)}, u32[]{:S(2)}) collective-permute-start(bf16[5120,128]{1,0:T(8,128)(2,1)} %collective-permute-done.21.refs_21_.refs_19_), channel_id=1, source_target_pairs={{0,8},{8,0},{16,24},{24,16},{32,40},{40,32},{48,56},{56,48},{64,72... | collective-permute-start | bytes 3932168 | tf_op jit(solution)/shard_map/ppermute | solution.py:294
  94.7 25.1 %collective-permute-start.19 = (bf16[5120,128]{1,0:T(8,128)(2,1)}, bf16[5120,128]{1,0:T(8,128)(2,1)S(1)}, u32[]{:S(2)}, u32[]{:S(2)}) collective-permute-start(bf16[5120,128]{1,0:T(8,128)(2,1)} %collective-permute-done.17.refs_17_.refs_15_), channel_id=1, source_target_pairs={{0,8},{8,0},{16,24},{24,16},{32,40},{40,32},{48,56},{56,48},{64,72... | collective-permute-start | bytes 3932168 | tf_op jit(solution)/shard_map/ppermute | solution.py:294
  110.4 41.4 %copy-start.4 = (bf16[5120,128]{1,0:T(8,128)(2,1)}, bf16[5120,128]{1,0:T(8,128)(2,1)S(1)}, u32[]{:S(2)}) copy-start(bf16[5120,128]{1,0:T(8,128)(2,1)S(1)} %collective-permute-done.14.refs_14_.refs_12_) | copy-start | bytes 3932164
  110.4 28.1 %collective-permute-start.27 = (bf16[5120,128]{1,0:T(8,128)(2,1)}, bf16[5120,128]{1,0:T(8,128)(2,1)S(1)}, u32[]{:S(2)}, u32[]{:S(2)}) collective-permute-start(bf16[5120,128]{1,0:T(8,128)(2,1)} %constant_dynamic-update-slice_fusion.refs_25_.refs_23_), channel_id=1, source_target_pairs={{0,16},{8,24},{16,0},{24,8},{32,48},{40,56},{48,32},{56,40},{64,80... | collective-permute-start | bytes 3932168 | tf_op jit(solution)/shard_map/ppermute | solution.py:320
  113.0 3.1 copy-start.2
  113.0 29.8 %collective-permute-start.22 = (bf16[5120,128]{1,0:T(8,128)(2,1)S(1)}, bf16[5120,128]{1,0:T(8,128)(2,1)}, u32[]{:S(2)}, u32[]{:S(2)}) collective-permute-start(bf16[5120,128]{1,0:T(8,128)(2,1)S(1)} %collective-permute-done.14.refs_14_.refs_12_), channel_id=1, source_target_pairs={{0,96},{8,104},{16,112},{24,120},{32,0},{40,8},{48,16},{56,24},{64... | collective-permute-start | bytes 3932168 | tf_op jit(solution)/shard_map/ppermute | solution.py:35
  116.0 1.1 copy-start.3
  116.0 28.3 %collective-permute-start.18 = (bf16[5120,128]{1,0:T(8,128)(2,1)S(1)}, bf16[5120,128]{1,0:T(8,128)(2,1)}, u32[]{:S(2)}, u32[]{:S(2)}) collective-permute-start(bf16[5120,128]{1,0:T(8,128)(2,1)S(1)} %collective-permute-done.14.refs_14_.refs_12_), channel_id=1, source_target_pairs={{0,32},{8,40},{16,48},{24,56},{32,64},{40,72},{48,80},{56,88},{64,... | collective-permute-start | bytes 3932168 | tf_op jit(solution)/shard_map/ppermute | solution.py:35
  117.2 27.2 %copy-start.5 = (bf16[5120,128]{1,0:T(8,128)(2,1)}, bf16[5120,128]{1,0:T(8,128)(2,1)S(1)}, u32[]{:S(2)}) copy-start(bf16[5120,128]{1,0:T(8,128)(2,1)S(1)} %collective-permute-done.23.refs_23_.refs_21_) | copy-start | bytes 3932164
  117.2 12.1 %collective-permute-start.8 = (bf16[64,5120]{1,0:T(8,128)(2,1)S(1)}, bf16[64,5120]{1,0:T(8,128)(2,1)S(1)}, u32[]{:S(2)}, u32[]{:S(2)}) collective-permute-start(bf16[64,5120]{1,0:T(8,128)(2,1)S(1)} %slice.73), channel_id=1, source_target_pairs={{0,6},{1,7},{2,0},{3,1},{4,2},{5,3},{6,4},{7,5},{8,14},{9,15},{10,... | collective-permute-start | bytes 1966088 | tf_op jit(solution)/shard_map/ppermute | solution.py:41
  119.8 24.6 %copy-start.6 = (bf16[5120,128]{1,0:T(8,128)(2,1)}, bf16[5120,128]{1,0:T(8,128)(2,1)S(1)}, u32[]{:S(2)}) copy-start(bf16[5120,128]{1,0:T(8,128)(2,1)S(1)} %collective-permute-done.19.refs_19_.refs_17_) | copy-start | bytes 3932164
  119.8 14.9 %collective-permute-start.7 = (bf16[64,5120]{1,0:T(8,128)(2,1)S(1)}, bf16[64,5120]{1,0:T(8,128)(2,1)S(1)}, u32[]{:S(2)}, u32[]{:S(2)}) collective-permute-start(bf16[64,5120]{1,0:T(8,128)(2,1)S(1)} %slice.72), channel_id=1, source_target_pairs={{0,2},{1,3},{2,4},{3,5},{4,6},{5,7},{6,0},{7,1},{8,10},{9,11},{10,... | collective-permute-start | bytes 1966088 | tf_op jit(solution)/shard_map/ppermute | solution.py:40
  129.3 22.5 %copy-start.9 = (bf16[64,5120]{1,0:T(8,128)(2,1)}, bf16[64,5120]{1,0:T(8,128)(2,1)S(1)}, u32[]{:S(2)}) copy-start(bf16[64,5120]{1,0:T(8,128)(2,1)S(1)} %collective-permute-done.8.refs_12_.refs_10_) | copy-start | bytes 1966084
  129.3 22.5 %collective-permute-start.28 = (bf16[5120,128]{1,0:T(8,128)(2,1)}, bf16[5120,128]{1,0:T(8,128)(2,1)}, u32[]{:S(2)}, u32[]{:S(2)}) collective-permute-start(bf16[5120,128]{1,0:T(8,128)(2,1)} %constant_dynamic-update-slice_fusion.refs_25_.refs_23_), channel_id=1, source_target_pairs={{0,8},{8,0},{16,24},{24,16},{32,40},{40,32},{48,56},{56,48},{64,72... | collective-permute-start | bytes 3932168 | tf_op jit(solution)/shard_map/ppermute | solution.py:294
  134.7 9.6 %copy-start.10 = (bf16[64,5120]{1,0:T(8,128)(2,1)}, bf16[64,5120]{1,0:T(8,128)(2,1)S(1)}, u32[]{:S(2)}) copy-start(bf16[64,5120]{1,0:T(8,128)(2,1)S(1)} %collective-permute-done.7.refs_11_.refs_9_) | copy-start | bytes 1966084
  134.7 17.1 %collective-permute-start.16 = (bf16[5120,128]{1,0:T(8,128)(2,1)S(1)}, bf16[5120,128]{1,0:T(8,128)(2,1)}, u32[]{:S(2)}, u32[]{:S(2)}) collective-permute-start(bf16[5120,128]{1,0:T(8,128)(2,1)S(1)} %collective-permute-done.14.refs_14_.refs_12_), channel_id=1, source_target_pairs={{0,8},{8,0},{16,24},{24,16},{32,40},{40,32},{48,56},{56,48},{64,72... | collective-permute-start | bytes 3932168 | tf_op jit(solution)/shard_map/ppermute | solution.py:294
  138.5 13.3 %copy-start.7 = (bf16[5120,128]{1,0:T(8,128)(2,1)}, bf16[5120,128]{1,0:T(8,128)(2,1)S(1)}, u32[]{:S(2)}) copy-start(bf16[5120,128]{1,0:T(8,128)(2,1)S(1)} %collective-permute-done.27.refs_26_.refs_24_) | copy-start | bytes 3932164
  138.5 13.3 %collective-permute-start.29 = (bf16[5120,128]{1,0:T(8,128)(2,1)S(1)}, bf16[5120,128]{1,0:T(8,128)(2,1)}, u32[]{:S(2)}, u32[]{:S(2)}) collective-permute-start(bf16[5120,128]{1,0:T(8,128)(2,1)S(1)} %collective-permute-done.27.refs_26_.refs_24_), channel_id=1, source_target_pairs={{0,8},{8,0},{16,24},{24,16},{32,40},{40,32},{48,56},{56,48},{64,72... | collective-permute-start | bytes 3932168 | tf_op jit(solution)/shard_map/ppermute | solution.py:294
  142.8 9.0 %collective-permute-start.24 = (bf16[5120,128]{1,0:T(8,128)(2,1)}, bf16[5120,128]{1,0:T(8,128)(2,1)}, u32[]{:S(2)}, u32[]{:S(2)}) collective-permute-start(bf16[5120,128]{1,0:T(8,128)(2,1)} %collective-permute-done.22.refs_22_.refs_20_), channel_id=1, source_target_pairs={{0,8},{8,0},{16,24},{24,16},{32,40},{40,32},{48,56},{56,48},{64,72... | collective-permute-start | bytes 3932168 | tf_op jit(solution)/shard_map/ppermute | solution.py:294
  144.3 7.5 %collective-permute-start.20 = (bf16[5120,128]{1,0:T(8,128)(2,1)}, bf16[5120,128]{1,0:T(8,128)(2,1)}, u32[]{:S(2)}, u32[]{:S(2)}) collective-permute-start(bf16[5120,128]{1,0:T(8,128)(2,1)} %collective-permute-done.18.refs_18_.refs_16_), channel_id=1, source_target_pairs={{0,8},{8,0},{16,24},{24,16},{32,40},{40,32},{48,56},{56,48},{64,72... | collective-permute-start | bytes 3932168 | tf_op jit(solution)/shard_map/ppermute | solution.py:294
  150.5 12.4 %copy-start.13 = (s32[4]{0:T(128)}, s32[4]{0:T(128)S(1)}, u32[]{:S(2)}) copy-start(s32[4]{0:T(128)S(1)} %compare_select_fusion.2.refs_0_) | copy-start | bytes 52
  163.0 15.4 %copy-start.14 = (s32[16]{0:T(128)S(1)}, s32[16]{0:T(128)}, u32[]{:S(2)}) copy-start(s32[16]{0:T(128)} %param.5) | copy-start | bytes 196
  163.9 9.5 %collective-permute-start.30 = (f32[4,128,128]{2,1,0:T(8,128)S(1)}, f32[4,128,128]{2,1,0:T(8,128)S(1)}, u32[]{:S(2)}, u32[]{:S(2)}) collective-permute-start(f32[4,128,128]{2,1,0:T(8,128)S(1)} %slice_bitcast_fusion), channel_id=1, source_target_pairs={{0,1},{8,9},{16,17},{24,25},{32,33},{40,41},{48,49},{56,57},{64,65... | collective-permute-start | bytes 786440 | tf_op jit(solution)/shard_map/ppermute | solution.py:342
  174.5 4.0 %collective-permute-start.32 = (f32[128,128]{1,0:T(8,128)S(1)}, f32[128,128]{1,0:T(8,128)S(1)}, u32[]{:S(2)}, u32[]{:S(2)}) collective-permute-start(f32[128,128]{1,0:T(8,128)S(1)} %get-tuple-element.57), channel_id=1, source_target_pairs={{0,4},{1,5},{8,12},{9,13},{16,20},{17,21},{24,28},{25,29},{32,36},... | collective-permute-start | bytes 196616 | tf_op jit(solution)/shard_map/ppermute | solution.py:345
  175.8 2.7 collective-permute-start.33
  177.1 2.6 collective-permute-start.31
  179.7 5.4 %collective-permute-start.39 = (f32[128,128]{1,0:T(8,128)S(1)}, f32[128,128]{1,0:T(8,128)S(1)}, u32[]{:S(2)}, u32[]{:S(2)}) collective-permute-start(f32[128,128]{1,0:T(8,128)S(1)} %get-tuple-element.52), channel_id=1, source_target_pairs={{0,1},{1,0},{2,3},{3,2},{4,5},{5,4},{6,7},{7,6},{8,9},{9,8},{10,11... | collective-permute-start | bytes 196616 | tf_op jit(solution)/shard_map/ppermute | solution.py:348
  183.5 3.4 %collective-permute-start.34 = (f32[128,128]{1,0:T(8,128)S(1)}, f32[128,128]{1,0:T(8,128)S(1)}, u32[]{:S(2)}, u32[]{:S(2)}) collective-permute-start(f32[128,128]{1,0:T(8,128)S(1)} %get-tuple-element.52), channel_id=1, source_target_pairs={{0,16},{8,24},{16,0},{24,8},{32,48},{40,56},{48,32},{56,40},{64,80... | collective-permute-start | bytes 196616 | tf_op jit(solution)/shard_map/ppermute | solution.py:350
  187.0 30.2 %collective-permute-start.36 = (f32[2,128,128]{2,1,0:T(8,128)S(1)}, f32[2,128,128]{2,1,0:T(8,128)S(1)}, u32[]{:S(2)}, u32[]{:S(2)}) collective-permute-start(f32[2,128,128]{2,1,0:T(8,128)S(1)} %get-tuple-element.61), channel_id=1, source_target_pairs={{0,96},{8,104},{16,112},{24,120},{32,0},{40,8},{48,16},{56,24},{64... | collective-permute-start | bytes 393224 | tf_op jit(solution)/shard_map/ppermute | solution.py:46
  188.1 29.1 %collective-permute-start.35 = (f32[2,128,128]{2,1,0:T(8,128)S(1)}, f32[2,128,128]{2,1,0:T(8,128)S(1)}, u32[]{:S(2)}, u32[]{:S(2)}) collective-permute-start(f32[2,128,128]{2,1,0:T(8,128)S(1)} %get-tuple-element.61), channel_id=1, source_target_pairs={{0,32},{8,40},{16,48},{24,56},{32,64},{40,72},{48,80},{56,88},{64,... | collective-permute-start | bytes 393224 | tf_op jit(solution)/shard_map/ppermute | solution.py:46
  188.5 28.7 %collective-permute-start.37 = (f32[2,128,128]{2,1,0:T(8,128)S(1)}, f32[2,128,128]{2,1,0:T(8,128)S(1)}, u32[]{:S(2)}, u32[]{:S(2)}) collective-permute-start(f32[2,128,128]{2,1,0:T(8,128)S(1)} %get-tuple-element.61), channel_id=1, source_target_pairs={{0,64},{8,72},{16,80},{24,88},{32,96},{40,104},{48,112},{56,120},{... | collective-permute-start | bytes 393224 | tf_op jit(solution)/shard_map/ppermute | solution.py:46
  212.9 10.6 %collective-permute-start.42 = (f32[2,128,128]{2,1,0:T(8,128)S(1)}, f32[2,128,128]{2,1,0:T(8,128)S(1)}, u32[]{:S(2)}, u32[]{:S(2)}) collective-permute-start(f32[2,128,128]{2,1,0:T(8,128)S(1)} %get-tuple-element.62), channel_id=1, source_target_pairs={{0,4},{1,5},{2,6},{3,7},{4,0},{5,1},{6,2},{7,3},{8,12},{9,13},{10,... | collective-permute-start | bytes 393224 | tf_op jit(solution)/shard_map/ppermute | solution.py:46
  213.7 9.9 %collective-permute-start.41 = (f32[2,128,128]{2,1,0:T(8,128)S(1)}, f32[2,128,128]{2,1,0:T(8,128)S(1)}, u32[]{:S(2)}, u32[]{:S(2)}) collective-permute-start(f32[2,128,128]{2,1,0:T(8,128)S(1)} %get-tuple-element.62), channel_id=1, source_target_pairs={{0,6},{1,7},{2,0},{3,1},{4,2},{5,3},{6,4},{7,5},{8,14},{9,15},{10,... | collective-permute-start | bytes 393224 | tf_op jit(solution)/shard_map/ppermute | solution.py:46
  217.2 6.3 %collective-permute-start.40 = (f32[2,128,128]{2,1,0:T(8,128)S(1)}, f32[2,128,128]{2,1,0:T(8,128)S(1)}, u32[]{:S(2)}, u32[]{:S(2)}) collective-permute-start(f32[2,128,128]{2,1,0:T(8,128)S(1)} %get-tuple-element.62), channel_id=1, source_target_pairs={{0,2},{1,3},{2,4},{3,5},{4,6},{5,7},{6,0},{7,1},{8,10},{9,11},{10,... | collective-permute-start | bytes 393224 | tf_op jit(solution)/shard_map/ppermute | solution.py:46
  217.3 6.3 %collective-permute-start.38 = (f32[4,2,128,128]{3,2,1,0:T(8,128)S(1)}, f32[4,2,128,128]{3,2,1,0:T(8,128)S(1)}, u32[]{:S(2)}, u32[]{:S(2)}) collective-permute-start(f32[4,2,128,128]{3,2,1,0:T(8,128)S(1)} %get-tuple-element.56), channel_id=1, source_target_pairs={{0,8},{8,0},{16,24},{24,16},{32,40},{40,32},{48,56},{56,48},{64,72... | collective-permute-start | bytes 1572872 | tf_op jit(solution)/shard_map/ppermute | solution.py:352
  223.6 0.9 copy-start.12
  241.3 46.1 %all-to-all-start.1 = ((s16[16,528,128]{2,1,0:T(8,128)(2,1)}), s16[16,528,128]{2,1,0:T(8,128)(2,1)S(1)}, u32[]{:S(2)}, u32[]{:S(2)}) async-start(s16[16,528,128]{2,1,0:T(8,128)(2,1)} %bitcast.78), calls=%async_computation.1 | async-start | bytes 4325376 | tf_op jit(solution)/shard_map/all_to_all | solution.py:378
  287.4 1.4 copy-start.11
  288.8 33.1 %all-to-all-start = ((s16[16,528,128]{2,1,0:T(8,128)(2,1)}), s16[16,528,128]{2,1,0:T(8,128)(2,1)}, u32[]{:S(2)}, u32[]{:S(2)}) async-start(s16[16,528,128]{2,1,0:T(8,128)(2,1)} %bitcast.79), calls=%async_computation | async-start | bytes 4325376 | tf_op jit(solution)/shard_map/all_to_all | solution.py:378

commit v2 on v1

--- a/solution.py
+++ b/solution.py
@@ -13,6 +13,7 @@
 TILE_ROWS = 64
 HALF = 8
 PAIRS = TILE_ROWS * HALF // 16
+TILES_STEP = 2
 CODED_ROWS = TILE_ROWS * HALF + 16
 LEVELS = 32767.0
 LOG_STEP = 0.6931471805599453 / 64.0
@@ -51,71 +52,85 @@
     return high.astype(jnp.bfloat16), (value - high).astype(jnp.bfloat16)
 
 
-def epilogue_kernel(table, running, *refs, part, inv_snp):
-    prods, col_factors, (row_factor, out, values) = refs[:2], refs[2:4], refs[4:]
-    step = pl.program_id(0)
-    row_start = table[32 + step]
-    old_rows = running.reshape(TILE_ROWS * HALF, 128)
-    mine = row_factor[...]
-    high = mine.astype(jnp.bfloat16)
-    low = (mine - high.astype(jnp.float32)).astype(jnp.bfloat16)
-    left = jnp.concatenate([high, high, low], axis=1)
-    for plane in range(2):
-        outer = jnp.dot(left, col_factors[plane][...], preferred_element_type=jnp.float32)
-        for side in range(4):
-            place = table[48 + side] + plane * 4
-            lanes = slice(side * 128, (side + 1) * 128)
-            old = old_rows[pl.ds(place, TILE_ROWS, stride=HALF), :]
-            values[pl.ds(place, TILE_ROWS, stride=HALF), :] = (
-                old + prods[plane][:, lanes] * inv_snp - outer[:, lanes]
-            )
-
-    @pl.when(row_start < NB)
-    def _():
-        values[...] = jnp.zeros_like(values)
-
-    if part == 0:
-
-        @pl.when(table[56] == 1)
+def epilogue_kernel(table, *refs, part, inv_snp):
+    tiles, (col_factor0, col_factor1, out, values) = refs[: 4 * TILES_STEP], refs[4 * TILES_STEP :]
+    for n in range(TILES_STEP):
+        running, prod0, prod1, row_factor = tiles[n * 4 : (n + 1) * 4]
+        row_start = table[32 + pl.program_id(0) * TILES_STEP + n]
+        old_rows = running.reshape(TILE_ROWS * HALF, 128)
+        mine = row_factor[...]
+        high = mine.astype(jnp.bfloat16)
+        low = (mine - high.astype(jnp.float32)).astype(jnp.bfloat16)
+        left = jnp.concatenate([high, high, low], axis=1)
+        for plane, (prod, col_factor) in enumerate(((prod0, col_factor0), (prod1, col_factor1))):
+            outer = jnp.dot(left, col_factor[...], preferred_element_type=jnp.float32)
+            for side in range(4):
+                place = table[48 + side] + plane * 4
+                lanes = slice(side * 128, (side + 1) * 128)
+                old = old_rows[pl.ds(place, TILE_ROWS, stride=HALF), :]
+                values[n, pl.ds(place, TILE_ROWS, stride=HALF), :] = (
+                    old + prod[:, lanes] * inv_snp - outer[:, lanes]
+                )
+
+        @pl.when(row_start < NB)
         def _():
-            row_pos = row_start + lax.broadcasted_iota(jnp.int32, (TILE_ROWS, NB), 0)
-            lane = lax.broadcasted_iota(jnp.int32, (TILE_ROWS, NB), 1)
-            values[pl.ds(0, TILE_ROWS, stride=HALF), :] = jnp.where(row_pos >= lane, mine, 0.0)
-
-    peak = jnp.full((16, 128), 1e-30, jnp.float32)
-    for a in range(PAIRS):
-        peak = jnp.maximum(peak, jnp.abs(values[a * 16 : (a + 1) * 16, :]))
-    peak = jnp.maximum(peak[:8], peak[8:])
-    code = jnp.minimum(jnp.ceil(jnp.log(peak) * (1.0 / LOG_STEP)) + 1.0, 8190.0)
-    code = jnp.concatenate([code, code], axis=0)
-    gain = LEVELS / jnp.exp(code * LOG_STEP)
-    for a in range(PAIRS):
-        scaled = jnp.round(values[a * 16 : (a + 1) * 16, :] * gain)
-        out[a * 16 : (a + 1) * 16, :] = scaled.astype(jnp.int32).astype(jnp.int16)
-    out[TILE_ROWS * HALF :, :] = code.astype(jnp.int32).astype(jnp.int16)
+            values[n] = jnp.zeros((TILE_ROWS * HALF, 128), jnp.float32)
+
+        if part == 0:
+
+            @pl.when(table[56] == 1)
+            def _():
+                row_pos = row_start + lax.broadcasted_iota(jnp.int32, (TILE_ROWS, NB), 0)
+                lane = lax.broadcasted_iota(jnp.int32, (TILE_ROWS, NB), 1)
+                values[n, pl.ds(0, TILE_ROWS, stride=HALF), :] = jnp.where(
+                    row_pos >= lane, mine, 0.0
+                )
+
+    for n in range(TILES_STEP):
+        peak = jnp.full((16, 128), 1e-30, jnp.float32)
+        for a in range(PAIRS):
+            peak = jnp.maximum(peak, jnp.abs(values[n, a * 16 : (a + 1) * 16, :]))
+        peak = jnp.maximum(peak[:8], peak[8:])
+        code = jnp.minimum(jnp.ceil(jnp.log(peak) * (1.0 / LOG_STEP)) + 1.0, 8190.0)
+        code = jnp.concatenate([code, code], axis=0)
+        gain = LEVELS / jnp.exp(code * LOG_STEP)
+        base = n * CODED_ROWS
+        for a in range(PAIRS):
+            scaled = jnp.round(values[n, a * 16 : (a + 1) * 16, :] * gain)
+            out[base + a * 16 : base + (a + 1) * 16, :] = scaled.astype(jnp.int32).astype(jnp.int16)
+        last = base + TILE_ROWS * HALF
+        out[last : last + 16, :] = code.astype(jnp.int32).astype(jnp.int16)
 
 
 def epilogue(part, table, running, prods, row_factor, col_factor, snp_count):
-    block = pl.BlockSpec((TILE_ROWS, 512), lambda i, t: (t[16 + i], 0))
+    specs, arrays = [], []
+    for n in range(TILES_STEP):
+        block = pl.BlockSpec((TILE_ROWS, 512), lambda i, t, n=n: (t[16 + i * TILES_STEP + n], 0))
+        specs += [
+            pl.BlockSpec(
+                (TILE_ROWS, HALF, 128), lambda i, t, n=n: (t[i * TILES_STEP + n], part, 0)
+            ),
+            block,
+            block,
+            pl.BlockSpec((TILE_ROWS, NB), lambda i, t, n=n: (t[16 + i * TILES_STEP + n], 0)),
+        ]
+        arrays += [running, *prods, row_factor]
     return pl.pallas_call(
         lambda *refs: epilogue_kernel(*refs, part=part, inv_snp=1.0 / snp_count),
         grid_spec=pltpu.PrefetchScalarGridSpec(
             num_scalar_prefetch=1,
-            grid=(16,),
+            grid=(16 // TILES_STEP,),
             in_specs=[
-                pl.BlockSpec((TILE_ROWS, HALF, 128), lambda i, t: (t[i], part, 0)),
-                block,
-                block,
+                *specs,
                 pl.BlockSpec((3 * NB, 512), lambda i, t: (0, t[52 + part * 2])),
                 pl.BlockSpec((3 * NB, 512), lambda i, t: (0, t[53 + part * 2])),
-                pl.BlockSpec((TILE_ROWS, NB), lambda i, t: (t[16 + i], 0)),
             ],
-            out_specs=pl.BlockSpec((CODED_ROWS, 128), lambda i, t: (i, 0)),
-            scratch_shapes=[pltpu.VMEM((TILE_ROWS * HALF, 128), jnp.float32)],
+            out_specs=pl.BlockSpec((TILES_STEP * CODED_ROWS, 128), lambda i, t: (i, 0)),
+            scratch_shapes=[pltpu.VMEM((TILES_STEP, TILE_ROWS * HALF, 128), jnp.float32)],
         ),
         out_shape=jax.ShapeDtypeStruct((16 * CODED_ROWS, 128), jnp.int16),
         name="epilogue",
-    )(table, running, *prods, col_factor, col_factor, row_factor)
+    )(table, *arrays, col_factor, col_factor)
 
 
 ROW_STEP = 256
@@ -254,7 +269,7 @@
 
 def unpack_kernel(coded, *refs):
     out = refs[-1]
-    for source in range(2):
+    for source in range(4):
         code = coded[source, TILE_ROWS * HALF :, :].astype(jnp.float32)
         scale = jnp.exp(code * LOG_STEP) * (1.0 / LEVELS)
         for a in range(PAIRS):
@@ -267,12 +282,12 @@
     begun = [] if before is None else [before]
     return pl.pallas_call(
         unpack_kernel,
-        grid=(8,),
+        grid=(4,),
         in_specs=[
-            pl.BlockSpec((2, CODED_ROWS, 128), lambda i: (i, 0, 0)),
+            pl.BlockSpec((4, CODED_ROWS, 128), lambda i: (i, 0, 0)),
             *[pl.BlockSpec(memory_space=pl.ANY)] * len(begun),
         ],
-        out_specs=pl.BlockSpec((2 * TILE_ROWS, HALF, 128), lambda i: (i, part, 0)),
+        out_specs=pl.BlockSpec((4 * TILE_ROWS, HALF, 128), lambda i: (i, part, 0)),
         out_shape=jax.ShapeDtypeStruct((16 * TILE_ROWS, 2 * HALF, 128), jnp.float32),
         input_output_aliases={1: 0} if begun else {},
         name="unpack",
@@ -367,14 +382,19 @@
         [inverse_map, tile, row_start, place, slots.astype(jnp.uint32), is_col0[None]]
     ).astype(jnp.int32)
 
-    result, packed = None, factor
+    prods = []
     running = running.reshape(1024, 16, 128)
+    late_rows, factor = lax.optimization_barrier((row_parts, factor))
+    for plane in range(3):
+        prods.append(product(plane, slots, late_rows, flat_shards))
+    result = None
     for part in range(2):
-        late_rows, packed = lax.optimization_barrier((row_parts, packed))
-        prods = []
-        for plane in (2 * part, 2 * part + 1):
-            prods.append(product(plane, slots, late_rows, flat_shards))
-        packed = epilogue(part, table, running, prods, row_factor, col_factor, snp_count)
+        if part == 1:
+            late_rows, packed = lax.optimization_barrier((row_parts, packed))
+            prods.append(product(3, slots, late_rows, flat_shards))
+        packed = epilogue(
+            part, table, running, prods[2 * part : 2 * part + 2], row_factor, col_factor, snp_count
+        )
         coded = lax.all_to_all(
             packed.reshape(16, CODED_ROWS, 128), "row", split_axis=0, concat_axis=0, tiled=True
         )

time: 330 us -> 319 us (0.967)
  Pallas kernels: 98.2 us -> 87.9 us
    pallas_call x2, Pallas kernels: 28.8 us -> 22.1 us  [epilogue(): pl.pallas_call(lambda *refs: epilogue_kernel(*refs, part=part, inv_snp=1....]
    pallas_call x2, Pallas kernels: 12.1 us -> 8.59 us  [unpack(): pl.pallas_call(unpack_kernel, grid=(4,), in_specs=[pl.BlockSpec((4, CODED...]
    unnamed x36 -> x34, local copies, waits for them, and re-layouts: 5.14 us -> 7.45 us
  transfers between devices with their start and end apart: 45 -> 45, of which waited for: 15 -> 12; matrix products, arithmetic and copies ran while one was open for 11% -> 12% of each run, Pallas kernels for 20% -> 19%
where the time goes in v2:
time: 319 us; the launch traced here: 317 us
  starting transfers between devices  108 us (34%)
  Pallas kernels  87.9 us (28%)
  waiting for transfers between devices  73.6 us (23%)
  other arithmetic  26.9 us (8%)
  local copies, waits for them, and re-layouts  19.5 us (6%)
    pallas_call x4, Pallas kernels, product(): pl.pallas_call(lambda *refs: product_kernel(*refs, plane=plane), grid_spe...  46.2 us
    ppermute x8, starting transfers between devices, twin(): return lax.ppermute(value, 'row', row_perm(0, 0, 1))  37.5 us
    all_to_all x2, waiting for transfers between devices, compute(): lax.all_to_all(packed.reshape(16, CODED_ROWS, 128), 'row', split_axis=0,...  23.5 us
    pallas_call x2, Pallas kernels, epilogue(): pl.pallas_call(lambda *refs: epilogue_kernel(*refs, part=part, inv_snp=1....  22.1 us
    all_to_all x2, starting transfers between devices, compute(): lax.all_to_all(packed.reshape(16, CODED_ROWS, 128), 'row', split_axis=0,...  13.8 us
    another operation x3, other arithmetic, compute(): lower = jnp.linalg.cholesky(leading)  12.4 us
    ppermute x4, starting transfers between devices, ring_sides(): lax.ppermute(shard, axis, perm(-1))  11.9 us
    pallas_call x1, Pallas kernels, panel(): pl.pallas_call(lambda *refs: panel_kernel(*refs, inv_snp=1.0 / count), gr...  11.1 us
  transfers between devices with their start and end apart: 45, of which 12 were waited for; matrix products, arithmetic and copies ran while one was open for 12% of the time, Pallas kernels for 19%

profile of v2, /device:TPU:1, one launch (start us, length us, event | category | flops | bytes accessed | tf_op | source)
XLA Modules:
  0.0 317.4 jit_solution(1364424999415812196)
XLA Ops:
  0.0 1.7 copy.19
  1.7 3.6 %collective-permute-start = (bf16[128,5120]{1,0:T(8,128)(2,1)S(1)}, bf16[128,5120]{1,0:T(8,128)(2,1)}, u32[]{:S(2)}, u32[]{:S(2)}) collective-permute-start(bf16[128,5120]{1,0:T(8,128)(2,1)S(1)} %bitcast.75), channel_id=1, source_target_pairs={{0,1},{1,0},{2,3},{3,2},{4,5},{5,4},{6,7},{7,6},{8,9},{9,8},{10,11... | collective-permute-start | bytes 3932168 | tf_op jit(solution)/shard_map/ppermute | solution.py:313
  5.4 2.7 collective-permute-start.3
  9.7 11.7 %cholesky.20 = f32[128,128]{1,0:T(8,128)S(1)} custom-call(f32[128,128]{1,0:T(8,128)S(1)} %fusion.5), custom_call_target="Cholesky" | custom-call | tf_op jit(solution)/shard_map/jit(cholesky)/cholesky | solution.py:318
  22.8 10.8 %collective-permute-done.refs_4_.refs_2_ = bf16[128,5120]{1,0:T(8,128)(2,1)} collective-permute-done((bf16[128,5120]{1,0:T(8,128)(2,1)S(1)}, bf16[128,5120]{1,0:T(8,128)(2,1)}, u32[]{:S(2)}, u32[]{:S(2)}) %collective-permute-start) | collective-permute-done | bytes 1310752 | tf_op jit(solution)/shard_map/ppermute | solution.py:313
  33.6 9.8 %custom-call.6 = f32[1,128,128]{1,2,0:T(8,128)S(1)} custom-call(f32[1,128,128]{2,1,0:T(8,128)S(1)} %select_bitcast_fusion), custom_call_target="InvertDiagBlocksLowerTriangular" | custom-call | tf_op jit(solution)/shard_map/triangular_solve | solution.py:326
  45.7 4.2 %collective-permute-start.21 = (bf16[5120,128]{1,0:T(8,128)(2,1)S(1)}, bf16[5120,128]{1,0:T(8,128)(2,1)}, u32[]{:S(2)}, u32[]{:S(2)}) collective-permute-start(bf16[5120,128]{1,0:T(8,128)(2,1)S(1)} %copy-done), channel_id=1, source_target_pairs={{0,96},{8,104},{16,112},{24,120},{32,0},{40,8},{48,16},{56,24},{64... | collective-permute-start | bytes 3932168 | tf_op jit(solution)/shard_map/ppermute | solution.py:36
  49.8 7.9 %collective-permute-start.15 = (bf16[5120,128]{1,0:T(8,128)(2,1)S(1)}, bf16[5120,128]{1,0:T(8,128)(2,1)}, u32[]{:S(2)}, u32[]{:S(2)}) collective-permute-start(bf16[5120,128]{1,0:T(8,128)(2,1)S(1)} %copy-done), channel_id=1, source_target_pairs={{0,8},{8,0},{16,24},{24,16},{32,40},{40,32},{48,56},{56,48},{64,72... | collective-permute-start | bytes 3932168 | tf_op jit(solution)/shard_map/ppermute | solution.py:309
  58.4 1.1 slice.71
  59.5 2.8 collective-permute-start.6
  62.3 1.1 slice.70
  63.6 8.3 %collective-permute-done.21.refs_21_.refs_19_ = bf16[5120,128]{1,0:T(8,128)(2,1)} collective-permute-done((bf16[5120,128]{1,0:T(8,128)(2,1)S(1)}, bf16[5120,128]{1,0:T(8,128)(2,1)}, u32[]{:S(2)}, u32[]{:S(2)}) %collective-permute-start.21) | collective-permute-done | bytes 1310752 | tf_op jit(solution)/shard_map/ppermute | solution.py:36
  71.9 1.3 collective-permute-start.13
  73.1 1.1 slice.75
  74.3 3.6 %collective-permute-start.26 = (bf16[2560,128]{1,0:T(8,128)(2,1)S(1)}, bf16[2560,128]{1,0:T(8,128)(2,1)S(1)}, u32[]{:S(2)}, u32[]{:S(2)}) collective-permute-start(bf16[2560,128]{1,0:T(8,128)(2,1)S(1)} %slice.75), channel_id=1, source_target_pairs={{0,96},{8,104},{16,112},{24,120},{32,0},{40,8},{48,16},{56,24},{64... | collective-permute-start | bytes 1966088 | tf_op jit(solution)/shard_map/ppermute | solution.py:42
  77.9 1.1 slice.74
  79.0 1.1 collective-permute-start.25
  80.1 2.2 collective-permute-done.13
  82.3 2.7 collective-permute-start.14
  85.0 2.7 collective-permute-start.4
  88.3 6.3 %collective-permute-start.23 = (bf16[5120,128]{1,0:T(8,128)(2,1)}, bf16[5120,128]{1,0:T(8,128)(2,1)S(1)}, u32[]{:S(2)}, u32[]{:S(2)}) collective-permute-start(bf16[5120,128]{1,0:T(8,128)(2,1)} %collective-permute-done.21.refs_21_.refs_19_), channel_id=1, source_target_pairs={{0,8},{8,0},{16,24},{24,16},{32,40},{40,32},{48,56},{56,48},{64,72... | collective-permute-start | bytes 3932168 | tf_op jit(solution)/shard_map/ppermute | solution.py:309
  94.7 4.9 %collective-permute-start.19 = (bf16[5120,128]{1,0:T(8,128)(2,1)}, bf16[5120,128]{1,0:T(8,128)(2,1)}, u32[]{:S(2)}, u32[]{:S(2)}) collective-permute-start(bf16[5120,128]{1,0:T(8,128)(2,1)} %collective-permute-done.17.refs_17_.refs_15_), channel_id=1, source_target_pairs={{0,8},{8,0},{16,24},{24,16},{32,40},{40,32},{48,56},{56,48},{64,72... | collective-permute-start | bytes 3932168 | tf_op jit(solution)/shard_map/ppermute | solution.py:309
  99.6 0.9 constant_dynamic-update-slice_fusion.1
  101.4 9.1 %collective-permute-done.14.refs_14_.refs_12_ = bf16[5120,128]{1,0:T(8,128)(2,1)} collective-permute-done((bf16[5120,128]{1,0:T(8,128)(2,1)S(1)}, bf16[5120,128]{1,0:T(8,128)(2,1)}, u32[]{:S(2)}, u32[]{:S(2)}) %collective-permute-start.14) | collective-permute-done | bytes 1310752 | tf_op jit(solution)/shard_map/ppermute | solution.py:321
  110.4 2.3 collective-permute-start.27
  113.0 2.3 collective-permute-start.22
  116.1 1.0 copy-done.3
  117.1 1.1 copy-done.4
  118.2 2.6 collective-permute-start.8
  120.8 9.5 %collective-permute-done.8.refs_12_.refs_10_ = bf16[64,5120]{1,0:T(8,128)(2,1)S(1)} collective-permute-done((bf16[64,5120]{1,0:T(8,128)(2,1)S(1)}, bf16[64,5120]{1,0:T(8,128)(2,1)S(1)}, u32[]{:S(2)}, u32[]{:S(2)}) %collective-permute-start.8) | collective-permute-done | bytes 655392 | tf_op jit(solution)/shard_map/ppermute | solution.py:42
  130.3 5.4 %collective-permute-start.28 = (bf16[5120,128]{1,0:T(8,128)(2,1)}, bf16[5120,128]{1,0:T(8,128)(2,1)S(1)}, u32[]{:S(2)}, u32[]{:S(2)}) collective-permute-start(bf16[5120,128]{1,0:T(8,128)(2,1)} %constant_dynamic-update-slice_fusion.refs_25_.refs_23_), channel_id=1, source_target_pairs={{0,8},{8,0},{16,24},{24,16},{32,40},{40,32},{48,56},{56,48},{64,72... | collective-permute-start | bytes 3932168 | tf_op jit(solution)/shard_map/ppermute | solution.py:309
  135.7 3.4 %collective-permute-start.16 = (bf16[5120,128]{1,0:T(8,128)(2,1)}, bf16[5120,128]{1,0:T(8,128)(2,1)}, u32[]{:S(2)}, u32[]{:S(2)}) collective-permute-start(bf16[5120,128]{1,0:T(8,128)(2,1)} %collective-permute-done.14.refs_14_.refs_12_), channel_id=1, source_target_pairs={{0,8},{8,0},{16,24},{24,16},{32,40},{40,32},{48,56},{56,48},{64,72... | collective-permute-start | bytes 3932168 | tf_op jit(solution)/shard_map/ppermute | solution.py:309
  139.1 3.7 %collective-permute-start.29 = (bf16[5120,128]{1,0:T(8,128)(2,1)S(1)}, bf16[5120,128]{1,0:T(8,128)(2,1)}, u32[]{:S(2)}, u32[]{:S(2)}) collective-permute-start(bf16[5120,128]{1,0:T(8,128)(2,1)S(1)} %collective-permute-done.27.refs_26_.refs_24_), channel_id=1, source_target_pairs={{0,8},{8,0},{16,24},{24,16},{32,40},{40,32},{48,56},{56,48},{64,72... | collective-permute-start | bytes 3932168 | tf_op jit(solution)/shard_map/ppermute | solution.py:309
  142.8 1.8 collective-permute-start.24
  144.6 4.1 %collective-permute-start.20 = (bf16[5120,128]{1,0:T(8,128)(2,1)}, bf16[5120,128]{1,0:T(8,128)(2,1)}, u32[]{:S(2)}, u32[]{:S(2)}) collective-permute-start(bf16[5120,128]{1,0:T(8,128)(2,1)} %collective-permute-done.18.refs_18_.refs_16_), channel_id=1, source_target_pairs={{0,8},{8,0},{16,24},{24,16},{32,40},{40,32},{48,56},{56,48},{64,72... | collective-permute-start | bytes 3932168 | tf_op jit(solution)/shard_map/ppermute | solution.py:309
  148.7 1.9 slice.61
  152.0 1.0 copy-done.6
  153.0 11.1 %panel.1 = f32[1024,128]{1,0:T(8,128)} custom-call(s32[5]{0:T(128)} %stack.47.refs_0_, f32[1024,128]{1,0:T(8,128)} %bitcast.89, f32[128,128]{1,0:T(8,128)} %broadcast_select_fusion.1.refs_2_, bf16[128,5120]{1,0:T(8,128)(2,1)} %bitcast.78, bf16[128,5120]{1,0:T(8,128)(2,1)} %collective-permute-done.refs_4_.refs_2_, ...), custom_call_target="tpu_custom_call" | custom-call | tf_op jit(solution)/shard_map/panel/pallas_call | solution.py:247
  164.1 1.1 fusion.12
  165.3 4.1 %collective-permute-start.30 = (f32[4,128,128]{1,2,0:T(8,128)S(1)}, f32[4,128,128]{1,2,0:T(8,128)S(1)}, u32[]{:S(2)}, u32[]{:S(2)}) collective-permute-start(f32[4,128,128]{1,2,0:T(8,128)S(1)} %bitcast.100), channel_id=1, source_target_pairs={{0,1},{8,9},{16,17},{24,25},{32,33},{40,41},{48,49},{56,57},{64,65... | collective-permute-start | bytes 786440 | tf_op jit(solution)/shard_map/ppermute | solution.py:357
  169.7 5.4 %collective-permute-done.30 = f32[4,128,128]{1,2,0:T(8,128)S(1)} collective-permute-done((f32[4,128,128]{1,2,0:T(8,128)S(1)}, f32[4,128,128]{1,2,0:T(8,128)S(1)}, u32[]{:S(2)}, u32[]{:S(2)}) %collective-permute-start.30) | collective-permute-done | bytes 262176 | tf_op jit(solution)/shard_map/ppermute | solution.py:357
  175.1 1.3 collective-permute-start.32
  176.4 1.3 collective-permute-start.33
  177.7 1.3 collective-permute-start.31
  179.1 1.3 collective-permute-done.31
  180.4 3.8 %collective-permute-start.34 = (f32[128,128]{0,1:T(8,128)S(1)}, f32[128,128]{0,1:T(8,128)S(1)}, u32[]{:S(2)}, u32[]{:S(2)}) collective-permute-start(f32[128,128]{0,1:T(8,128)S(1)} %get-tuple-element.52), channel_id=1, source_target_pairs={{0,1},{1,0},{2,3},{3,2},{4,5},{5,4},{6,7},{7,6},{8,9},{9,8},{10,11... | collective-permute-start | bytes 196616 | tf_op jit(solution)/shard_map/ppermute | solution.py:363
  184.4 1.2 collective-permute-start.40
  187.5 11.4 %product.6.refs_3_.refs_7_ = f32[1024,512]{1,0:T(8,128)} custom-call(s32[4]{0:T(128)} %copy-done.11, bf16[128,5120]{1,0:T(8,128)(2,1)} %bitcast.79, bf16[128,5120]{1,0:T(8,128)(2,1)} %collective-permute-done.refs_4_.refs_2_, bf16[128,5120]{1,0:T(8,128)(2,1)} %collective-permute-done.1.refs_5_.refs_3_, bf16[128,5120]{1,0:T(8,128)(2,1)} %copy-done.3, ...), custom_call_target="tpu_custom_call" | custom-call | tf_op jit(solution)/shard_map/product/pallas_call | solution.py:199
  198.9 11.5 %product.5.refs_2_.refs_6_ = f32[1024,512]{1,0:T(8,128)} custom-call(s32[4]{0:T(128)} %copy-done.11, bf16[128,5120]{1,0:T(8,128)(2,1)} %bitcast.80, bf16[128,5120]{1,0:T(8,128)(2,1)} %collective-permute-done.refs_4_.refs_2_, bf16[128,5120]{1,0:T(8,128)(2,1)} %collective-permute-done.1.refs_5_.refs_3_, bf16[128,5120]{1,0:T(8,128)(2,1)} %copy-done.3, ...), custom_call_target="tpu_custom_call" | custom-call | tf_op jit(solution)/shard_map/product/pallas_call | solution.py:199
  211.2 3.5 %collective-permute-start.36 = (f32[2,128,128]{1,2,0:T(8,128)S(1)}, f32[2,128,128]{1,2,0:T(8,128)S(1)}, u32[]{:S(2)}, u32[]{:S(2)}) collective-permute-start(f32[2,128,128]{1,2,0:T(8,128)S(1)} %pad_maximum_fusion.3), channel_id=1, source_target_pairs={{0,6},{1,7},{2,0},{3,1},{4,2},{5,3},{6,4},{7,5},{8,14},{9,15},{10,... | collective-permute-start | bytes 393224 | tf_op jit(solution)/shard_map/ppermute | solution.py:47
  215.0 3.6 %collective-permute-start.42 = (f32[4,2,128,128]{2,1,0,3:T(2,128)S(1)}, f32[4,2,128,128]{2,1,0,3:T(2,128)S(1)}, u32[]{:S(2)}, u32[]{:S(2)}) collective-permute-start(f32[4,2,128,128]{2,1,0,3:T(2,128)S(1)} %pad_maximum_fusion.2), channel_id=1, source_target_pairs={{0,8},{8,0},{16,24},{24,16},{32,40},{40,32},{48,56},{56,48},{64,72... | collective-permute-start | bytes 1572872 | tf_op jit(solution)/shard_map/ppermute | solution.py:367
  218.6 2.1 collective-permute-done.35
  220.7 1.0 copy.26
  223.5 1.3 pad_maximum_fusion.refs_9_.refs_10_
  224.8 11.1 %epilogue.2 = s16[8448,128]{1,0:T(8,128)(2,1)} custom-call(s32[57]{0:T(128)} %convert_element_type.35.refs_0_, f32[1024,16,128]{2,1,0:T(8,128)} %bitcast.71, f32[1024,512]{1,0:T(8,128)} %product.5.refs_2_.refs_6_, f32[1024,512]{1,0:T(8,128)} %product.6.refs_3_.refs_7_, f32[1024,128]{1,0:T(8,128)} %bitcast.83, f32[1024,16,128]{2,1,0:T(8,128)} %bitcast.72, ...), custom_call_target="tpu_custom_call" | custom-call | tf_op jit(solution)/shard_map/epilogue/pallas_call | solution.py:118
  235.9 8.4 %all-to-all-start.1 = ((s16[16,528,128]{2,1,0:T(8,128)(2,1)}), s16[16,528,128]{2,1,0:T(8,128)(2,1)S(1)}, u32[]{:S(2)}, u32[]{:S(2)}) async-start(s16[16,528,128]{2,1,0:T(8,128)(2,1)} %bitcast.87), calls=%async_computation.1 | async-start | bytes 4325376 | tf_op jit(solution)/shard_map/all_to_all | solution.py:398
  244.3 11.8 %product.4.refs_2_.refs_6_ = f32[1024,512]{1,0:T(8,128)} custom-call(s32[4]{0:T(128)} %copy-done.11, bf16[128,5120]{1,0:T(8,128)(2,1)} %bitcast.81, bf16[128,5120]{1,0:T(8,128)(2,1)} %collective-permute-done.refs_4_.refs_2_, bf16[128,5120]{1,0:T(8,128)(2,1)} %collective-permute-done.1.refs_5_.refs_3_, bf16[128,5120]{1,0:T(8,128)(2,1)} %copy-done.3, ...), custom_call_target="tpu_custom_call" | custom-call | tf_op jit(solution)/shard_map/product/pallas_call | solution.py:199
  256.1 11.5 %product.7.refs_3_.refs_7_ = f32[1024,512]{1,0:T(8,128)} custom-call(s32[4]{0:T(128)} %copy-done.11, bf16[128,5120]{1,0:T(8,128)(2,1)} %bitcast.82, bf16[128,5120]{1,0:T(8,128)(2,1)} %collective-permute-done.refs_4_.refs_2_, bf16[128,5120]{1,0:T(8,128)(2,1)} %collective-permute-done.1.refs_5_.refs_3_, bf16[128,5120]{1,0:T(8,128)(2,1)} %copy-done.3, ...), custom_call_target="tpu_custom_call" | custom-call | tf_op jit(solution)/shard_map/product/pallas_call | solution.py:199
  267.6 11.0 %epilogue.3 = s16[8448,128]{1,0:T(8,128)(2,1)} custom-call(s32[57]{0:T(128)} %convert_element_type.35.refs_0_, f32[1024,16,128]{2,1,0:T(8,128)} %bitcast.73, f32[1024,512]{1,0:T(8,128)} %product.4.refs_2_.refs_6_, f32[1024,512]{1,0:T(8,128)} %product.7.refs_3_.refs_7_, f32[1024,128]{1,0:T(8,128)} %bitcast.85, f32[1024,16,128]{2,1,0:T(8,128)} %bitcast.74, ...), custom_call_target="tpu_custom_call" | custom-call | tf_op jit(solution)/shard_map/epilogue/pallas_call | solution.py:118
  278.6 1.4 copy-done.10
  280.0 5.4 %all-to-all-start = ((s16[16,528,128]{2,1,0:T(8,128)(2,1)}), s16[16,528,128]{2,1,0:T(8,128)(2,1)}, u32[]{:S(2)}, u32[]{:S(2)}) async-start(s16[16,528,128]{2,1,0:T(8,128)(2,1)} %bitcast.88), calls=%async_computation | async-start | bytes 4325376 | tf_op jit(solution)/shard_map/all_to_all | solution.py:398
  285.3 4.3 %unpack.2.refs_0_ = f32[1024,16,128]{2,1,0:T(8,128)} custom-call(s16[16,528,128]{2,1,0:T(8,128)(2,1)} %copy-done.10), custom_call_target="tpu_custom_call" | custom-call | tf_op jit(solution)/shard_map/unpack/pallas_call | solution.py:283
  289.6 23.5 %all-to-all-done.coded = s16[16,528,128]{2,1,0:T(8,128)(2,1)} async-done(((s16[16,528,128]{2,1,0:T(8,128)(2,1)}), s16[16,528,128]{2,1,0:T(8,128)(2,1)}, u32[]{:S(2)}, u32[]{:S(2)}) %all-to-all-start) | async-done | bytes 2162720 | tf_op jit(solution)/shard_map/all_to_all | solution.py:398
  313.1 4.3 %unpack.3 = f32[1024,16,128]{2,1,0:T(8,128)} custom-call(s16[16,528,128]{2,1,0:T(8,128)(2,1)} %all-to-all-done.coded, f32[1024,16,128]{2,1,0:T(8,128)} %unpack.2.refs_0_), custom_call_target="tpu_custom_call", output_to_operand_aliasing={{}: (1, {})} | custom-call | tf_op jit(solution)/shard_map/unpack/pallas_call | solution.py:283
  (113 shorter events, 15.3 us)
Async XLA Ops:
  0.0 9.0 %copy-start = (bf16[5120,128]{1,0:T(8,128)(2,1)S(1)}, bf16[5120,128]{1,0:T(8,128)(2,1)}, u32[]{:S(2)}) copy-start(bf16[5120,128]{1,0:T(8,128)(2,1)} %refs_11_.7) | copy-start | bytes 3932164
  1.7 7.9 %copy-start.1 = (bf16[5120,128]{0,1:T(8,128)(2,1)}, bf16[5120,128]{0,1:T(8,128)(2,1)S(1)}, u32[]{:S(2)}) copy-start(bf16[5120,128]{0,1:T(8,128)(2,1)S(1)} %copy.19) | copy-start | bytes 3932164
  1.7 31.8 %collective-permute-start = (bf16[128,5120]{1,0:T(8,128)(2,1)S(1)}, bf16[128,5120]{1,0:T(8,128)(2,1)}, u32[]{:S(2)}, u32[]{:S(2)}) collective-permute-start(bf16[128,5120]{1,0:T(8,128)(2,1)S(1)} %bitcast.75), channel_id=1, source_target_pairs={{0,1},{1,0},{2,3},{3,2},{4,5},{5,4},{6,7},{7,6},{8,9},{9,8},{10,11... | collective-permute-start | bytes 3932168 | tf_op jit(solution)/shard_map/ppermute | solution.py:313
  5.4 52.4 %collective-permute-start.3 = (bf16[128,5120]{1,0:T(8,128)(2,1)S(1)}, bf16[128,5120]{1,0:T(8,128)(2,1)}, u32[]{:S(2)}, u32[]{:S(2)}) collective-permute-start(bf16[128,5120]{1,0:T(8,128)(2,1)S(1)} %bitcast.76), channel_id=1, source_target_pairs={{0,6},{1,7},{2,0},{3,1},{4,2},{5,3},{6,4},{7,5},{8,14},{9,15},{10,... | collective-permute-start | bytes 3932168 | tf_op jit(solution)/shard_map/ppermute | solution.py:36
  8.1 51.4 %collective-permute-start.1 = (bf16[128,5120]{1,0:T(8,128)(2,1)S(1)}, bf16[128,5120]{1,0:T(8,128)(2,1)}, u32[]{:S(2)}, u32[]{:S(2)}) collective-permute-start(bf16[128,5120]{1,0:T(8,128)(2,1)S(1)} %bitcast.77), channel_id=1, source_target_pairs={{0,2},{1,3},{2,4},{3,5},{4,6},{5,7},{6,0},{7,1},{8,10},{9,11},{10,... | collective-permute-start | bytes 3932168 | tf_op jit(solution)/shard_map/ppermute | solution.py:36
  43.6 2.0 collective-permute-start.11
  44.3 5.5 %collective-permute-start.10 = (f32[128,128]{1,0:T(8,128)S(1)}, f32[128,128]{1,0:T(8,128)S(1)}, u32[]{:S(2)}, u32[]{:S(2)}) collective-permute-start(f32[128,128]{1,0:T(8,128)S(1)} %fusion.3), channel_id=1, source_target_pairs={{0,64},{1,65},{2,66},{3,67},{4,68},{5,69},{6,70},{7,71}} | collective-permute-start | bytes 196616 | tf_op jit(solution)/shard_map/ppermute | solution.py:330
  45.0 4.8 %collective-permute-start.9 = (f32[128,128]{1,0:T(8,128)S(1)}, f32[128,128]{1,0:T(8,128)S(1)}, u32[]{:S(2)}, u32[]{:S(2)}) collective-permute-start(f32[128,128]{1,0:T(8,128)S(1)} %fusion.3), channel_id=1, source_target_pairs={{0,32},{1,33},{2,34},{3,35},{4,36},{5,37},{6,38},{7,39}} | collective-permute-start | bytes 196616 | tf_op jit(solution)/shard_map/ppermute | solution.py:330
  45.7 26.2 %collective-permute-start.21 = (bf16[5120,128]{1,0:T(8,128)(2,1)S(1)}, bf16[5120,128]{1,0:T(8,128)(2,1)}, u32[]{:S(2)}, u32[]{:S(2)}) collective-permute-start(bf16[5120,128]{1,0:T(8,128)(2,1)S(1)} %copy-done), channel_id=1, source_target_pairs={{0,96},{8,104},{16,112},{24,120},{32,0},{40,8},{48,16},{56,24},{64... | collective-permute-start | bytes 3932168 | tf_op jit(solution)/shard_map/ppermute | solution.py:36
  49.8 24.5 %collective-permute-start.17 = (bf16[5120,128]{1,0:T(8,128)(2,1)S(1)}, bf16[5120,128]{1,0:T(8,128)(2,1)}, u32[]{:S(2)}, u32[]{:S(2)}) collective-permute-start(bf16[5120,128]{1,0:T(8,128)(2,1)S(1)} %copy-done), channel_id=1, source_target_pairs={{0,32},{8,40},{16,48},{24,56},{32,64},{40,72},{48,80},{56,88},{64,... | collective-permute-start | bytes 3932168 | tf_op jit(solution)/shard_map/ppermute | solution.py:36
  49.8 29.2 %collective-permute-start.15 = (bf16[5120,128]{1,0:T(8,128)(2,1)S(1)}, bf16[5120,128]{1,0:T(8,128)(2,1)}, u32[]{:S(2)}, u32[]{:S(2)}) collective-permute-start(bf16[5120,128]{1,0:T(8,128)(2,1)S(1)} %copy-done), channel_id=1, source_target_pairs={{0,8},{8,0},{16,24},{24,16},{32,40},{40,32},{48,56},{56,48},{64,72... | collective-permute-start | bytes 3932168 | tf_op jit(solution)/shard_map/ppermute | solution.py:309
  57.7 5.8 %collective-permute-start.12 = (f32[128,128]{1,0:T(8,128)S(1)}, f32[128,128]{1,0:T(8,128)S(1)}, u32[]{:S(2)}, u32[]{:S(2)}) collective-permute-start(f32[128,128]{1,0:T(8,128)S(1)} %add_select_fusion), channel_id=1, source_target_pairs={{0,16},{32,48},{64,80},{96,112},{1,17},{33,49},{65,81},{97,113},{2... | collective-permute-start | bytes 196616 | tf_op jit(solution)/shard_map/ppermute | solution.py:333
  59.5 25.4 %collective-permute-start.6 = (bf16[64,5120]{1,0:T(8,128)(2,1)S(1)}, bf16[64,5120]{1,0:T(8,128)(2,1)S(1)}, u32[]{:S(2)}, u32[]{:S(2)}) collective-permute-start(bf16[64,5120]{1,0:T(8,128)(2,1)S(1)} %slice.71), channel_id=1, source_target_pairs={{0,6},{1,7},{2,0},{3,1},{4,2},{5,3},{6,4},{7,5},{8,14},{9,15},{10,... | collective-permute-start | bytes 1966088 | tf_op jit(solution)/shard_map/ppermute | solution.py:42
  63.5 24.2 %collective-permute-start.5 = (bf16[64,5120]{1,0:T(8,128)(2,1)S(1)}, bf16[64,5120]{1,0:T(8,128)(2,1)}, u32[]{:S(2)}, u32[]{:S(2)}) collective-permute-start(bf16[64,5120]{1,0:T(8,128)(2,1)S(1)} %slice.70), channel_id=1, source_target_pairs={{0,2},{1,3},{2,4},{3,5},{4,6},{5,7},{6,0},{7,1},{8,10},{9,11},{10,... | collective-permute-start | bytes 1966088 | tf_op jit(solution)/shard_map/ppermute | solution.py:41
  71.9 10.4 %collective-permute-start.13 = (f32[128,128]{1,0:T(8,128)S(1)}, f32[128,128]{1,0:T(8,128)S(1)}, u32[]{:S(2)}, u32[]{:S(2)}) collective-permute-start(f32[128,128]{1,0:T(8,128)S(1)} %broadcast_select_fusion), channel_id=1, source_target_pairs={{0,8},{16,24},{32,40},{48,56},{64,72},{80,88},{96,104},{112,120},{... | collective-permute-start | bytes 196616 | tf_op jit(solution)/shard_map/ppermute | solution.py:337
  74.3 14.0 %collective-permute-start.26 = (bf16[2560,128]{1,0:T(8,128)(2,1)S(1)}, bf16[2560,128]{1,0:T(8,128)(2,1)S(1)}, u32[]{:S(2)}, u32[]{:S(2)}) collective-permute-start(bf16[2560,128]{1,0:T(8,128)(2,1)S(1)} %slice.75), channel_id=1, source_target_pairs={{0,96},{8,104},{16,112},{24,120},{32,0},{40,8},{48,16},{56,24},{64... | collective-permute-start | bytes 1966088 | tf_op jit(solution)/shard_map/ppermute | solution.py:42
  79.0 15.6 %collective-permute-start.25 = (bf16[2560,128]{1,0:T(8,128)(2,1)S(1)}, bf16[2560,128]{1,0:T(8,128)(2,1)S(1)}, u32[]{:S(2)}, u32[]{:S(2)}) collective-permute-start(bf16[2560,128]{1,0:T(8,128)(2,1)S(1)} %slice.74), channel_id=1, source_target_pairs={{0,32},{8,40},{16,48},{24,56},{32,64},{40,72},{48,80},{56,88},{64,... | collective-permute-start | bytes 1966088 | tf_op jit(solution)/shard_map/ppermute | solution.py:41
  82.3 28.2 %collective-permute-start.14 = (bf16[5120,128]{1,0:T(8,128)(2,1)S(1)}, bf16[5120,128]{1,0:T(8,128)(2,1)}, u32[]{:S(2)}, u32[]{:S(2)}) collective-permute-start(bf16[5120,128]{1,0:T(8,128)(2,1)S(1)} %copy-done), channel_id=1, source_target_pairs={{0,16},{8,24},{16,0},{24,8},{32,48},{40,56},{48,32},{56,40},{64,80... | collective-permute-start | bytes 3932168 | tf_op jit(solution)/shard_map/ppermute | solution.py:321
  85.0 31.1 %copy-start.7 = (bf16[64,5120]{1,0:T(8,128)(2,1)}, bf16[64,5120]{1,0:T(8,128)(2,1)S(1)}, u32[]{:S(2)}) copy-start(bf16[64,5120]{1,0:T(8,128)(2,1)S(1)} %collective-permute-done.6.refs_10_.refs_8_) | copy-start | bytes 1966084
  85.0 28.0 %collective-permute-start.4 = (bf16[128,5120]{1,0:T(8,128)(2,1)}, bf16[128,5120]{1,0:T(8,128)(2,1)S(1)}, u32[]{:S(2)}, u32[]{:S(2)}) collective-permute-start(bf16[128,5120]{1,0:T(8,128)(2,1)} %collective-permute-done.refs_4_.refs_2_), channel_id=1, source_target_pairs={{0,6},{1,7},{2,0},{3,1},{4,2},{5,3},{6,4},{7,5},{8,14},{9,15},{10,... | collective-permute-start | bytes 3932168 | tf_op jit(solution)/shard_map/ppermute | solution.py:36
  87.7 28.3 %collective-permute-start.2 = (bf16[128,5120]{1,0:T(8,128)(2,1)}, bf16[128,5120]{1,0:T(8,128)(2,1)S(1)}, u32[]{:S(2)}, u32[]{:S(2)}) collective-permute-start(bf16[128,5120]{1,0:T(8,128)(2,1)} %collective-permute-done.refs_4_.refs_2_), channel_id=1, source_target_pairs={{0,2},{1,3},{2,4},{3,5},{4,6},{5,7},{6,0},{7,1},{8,10},{9,11},{10,... | collective-permute-start | bytes 3932168 | tf_op jit(solution)/shard_map/ppermute | solution.py:36
  88.3 28.8 %collective-permute-start.23 = (bf16[5120,128]{1,0:T(8,128)(2,1)}, bf16[5120,128]{1,0:T(8,128)(2,1)S(1)}, u32[]{:S(2)}, u32[]{:S(2)}) collective-permute-start(bf16[5120,128]{1,0:T(8,128)(2,1)} %collective-permute-done.21.refs_21_.refs_19_), channel_id=1, source_target_pairs={{0,8},{8,0},{16,24},{24,16},{32,40},{40,32},{48,56},{56,48},{64,72... | collective-permute-start | bytes 3932168 | tf_op jit(solution)/shard_map/ppermute | solution.py:309
  94.7 26.1 %collective-permute-start.19 = (bf16[5120,128]{1,0:T(8,128)(2,1)}, bf16[5120,128]{1,0:T(8,128)(2,1)}, u32[]{:S(2)}, u32[]{:S(2)}) collective-permute-start(bf16[5120,128]{1,0:T(8,128)(2,1)} %collective-permute-done.17.refs_17_.refs_15_), channel_id=1, source_target_pairs={{0,8},{8,0},{16,24},{24,16},{32,40},{40,32},{48,56},{56,48},{64,72... | collective-permute-start | bytes 3932168 | tf_op jit(solution)/shard_map/ppermute | solution.py:309
  110.4 28.7 %collective-permute-start.27 = (bf16[5120,128]{1,0:T(8,128)(2,1)}, bf16[5120,128]{1,0:T(8,128)(2,1)S(1)}, u32[]{:S(2)}, u32[]{:S(2)}) collective-permute-start(bf16[5120,128]{1,0:T(8,128)(2,1)} %constant_dynamic-update-slice_fusion.refs_25_.refs_23_), channel_id=1, source_target_pairs={{0,16},{8,24},{16,0},{24,8},{32,48},{40,56},{48,32},{56,40},{64,80... | collective-permute-start | bytes 3932168 | tf_op jit(solution)/shard_map/ppermute | solution.py:335
  113.0 3.1 copy-start.2
  113.0 29.8 %collective-permute-start.22 = (bf16[5120,128]{1,0:T(8,128)(2,1)}, bf16[5120,128]{1,0:T(8,128)(2,1)}, u32[]{:S(2)}, u32[]{:S(2)}) collective-permute-start(bf16[5120,128]{1,0:T(8,128)(2,1)} %collective-permute-done.14.refs_14_.refs_12_), channel_id=1, source_target_pairs={{0,96},{8,104},{16,112},{24,120},{32,0},{40,8},{48,16},{56,24},{64... | collective-permute-start | bytes 3932168 | tf_op jit(solution)/shard_map/ppermute | solution.py:36
  116.0 1.1 copy-start.3
  116.0 28.6 %collective-permute-start.18 = (bf16[5120,128]{1,0:T(8,128)(2,1)}, bf16[5120,128]{1,0:T(8,128)(2,1)}, u32[]{:S(2)}, u32[]{:S(2)}) collective-permute-start(bf16[5120,128]{1,0:T(8,128)(2,1)} %collective-permute-done.14.refs_14_.refs_12_), channel_id=1, source_target_pairs={{0,32},{8,40},{16,48},{24,56},{32,64},{40,72},{48,80},{56,88},{64,... | collective-permute-start | bytes 3932168 | tf_op jit(solution)/shard_map/ppermute | solution.py:36
  117.1 1.1 copy-start.4
  118.2 12.1 %collective-permute-start.8 = (bf16[64,5120]{1,0:T(8,128)(2,1)S(1)}, bf16[64,5120]{1,0:T(8,128)(2,1)S(1)}, u32[]{:S(2)}, u32[]{:S(2)}) collective-permute-start(bf16[64,5120]{1,0:T(8,128)(2,1)S(1)} %slice.73), channel_id=1, source_target_pairs={{0,6},{1,7},{2,0},{3,1},{4,2},{5,3},{6,4},{7,5},{8,14},{9,15},{10,... | collective-permute-start | bytes 1966088 | tf_op jit(solution)/shard_map/ppermute | solution.py:42
  120.8 14.9 %collective-permute-start.7 = (bf16[64,5120]{1,0:T(8,128)(2,1)S(1)}, bf16[64,5120]{1,0:T(8,128)(2,1)S(1)}, u32[]{:S(2)}, u32[]{:S(2)}) collective-permute-start(bf16[64,5120]{1,0:T(8,128)(2,1)S(1)} %slice.72), channel_id=1, source_target_pairs={{0,2},{1,3},{2,4},{3,5},{4,6},{5,7},{6,0},{7,1},{8,10},{9,11},{10,... | collective-permute-start | bytes 1966088 | tf_op jit(solution)/shard_map/ppermute | solution.py:41
  130.3 21.7 %copy-start.8 = (bf16[64,5120]{1,0:T(8,128)(2,1)}, bf16[64,5120]{1,0:T(8,128)(2,1)S(1)}, u32[]{:S(2)}) copy-start(bf16[64,5120]{1,0:T(8,128)(2,1)S(1)} %collective-permute-done.8.refs_12_.refs_10_) | copy-start | bytes 1966084
  130.3 21.7 %collective-permute-start.28 = (bf16[5120,128]{1,0:T(8,128)(2,1)}, bf16[5120,128]{1,0:T(8,128)(2,1)S(1)}, u32[]{:S(2)}, u32[]{:S(2)}) collective-permute-start(bf16[5120,128]{1,0:T(8,128)(2,1)} %constant_dynamic-update-slice_fusion.refs_25_.refs_23_), channel_id=1, source_target_pairs={{0,8},{8,0},{16,24},{24,16},{32,40},{40,32},{48,56},{56,48},{64,72... | collective-permute-start | bytes 3932168 | tf_op jit(solution)/shard_map/ppermute | solution.py:309
  135.7 3.4 %copy-start.9 = (bf16[64,5120]{1,0:T(8,128)(2,1)}, bf16[64,5120]{1,0:T(8,128)(2,1)S(1)}, u32[]{:S(2)}) copy-start(bf16[64,5120]{1,0:T(8,128)(2,1)S(1)} %collective-permute-done.7.refs_11_.refs_9_) | copy-start | bytes 1966084
  135.7 16.2 %collective-permute-start.16 = (bf16[5120,128]{1,0:T(8,128)(2,1)}, bf16[5120,128]{1,0:T(8,128)(2,1)}, u32[]{:S(2)}, u32[]{:S(2)}) collective-permute-start(bf16[5120,128]{1,0:T(8,128)(2,1)} %collective-permute-done.14.refs_14_.refs_12_), channel_id=1, source_target_pairs={{0,8},{8,0},{16,24},{24,16},{32,40},{40,32},{48,56},{56,48},{64,72... | collective-permute-start | bytes 3932168 | tf_op jit(solution)/shard_map/ppermute | solution.py:309
  139.1 12.9 %copy-start.5 = (bf16[5120,128]{1,0:T(8,128)(2,1)}, bf16[5120,128]{1,0:T(8,128)(2,1)S(1)}, u32[]{:S(2)}) copy-start(bf16[5120,128]{1,0:T(8,128)(2,1)S(1)} %collective-permute-done.27.refs_26_.refs_24_) | copy-start | bytes 3932164
  139.1 12.8 %collective-permute-start.29 = (bf16[5120,128]{1,0:T(8,128)(2,1)S(1)}, bf16[5120,128]{1,0:T(8,128)(2,1)}, u32[]{:S(2)}, u32[]{:S(2)}) collective-permute-start(bf16[5120,128]{1,0:T(8,128)(2,1)S(1)} %collective-permute-done.27.refs_26_.refs_24_), channel_id=1, source_target_pairs={{0,8},{8,0},{16,24},{24,16},{32,40},{40,32},{48,56},{56,48},{64,72... | collective-permute-start | bytes 3932168 | tf_op jit(solution)/shard_map/ppermute | solution.py:309
  142.8 9.2 %collective-permute-start.24 = (bf16[5120,128]{1,0:T(8,128)(2,1)}, bf16[5120,128]{1,0:T(8,128)(2,1)}, u32[]{:S(2)}, u32[]{:S(2)}) collective-permute-start(bf16[5120,128]{1,0:T(8,128)(2,1)} %collective-permute-done.22.refs_22_.refs_20_), channel_id=1, source_target_pairs={{0,8},{8,0},{16,24},{24,16},{32,40},{40,32},{48,56},{56,48},{64,72... | collective-permute-start | bytes 3932168 | tf_op jit(solution)/shard_map/ppermute | solution.py:309
  144.6 7.4 %collective-permute-start.20 = (bf16[5120,128]{1,0:T(8,128)(2,1)}, bf16[5120,128]{1,0:T(8,128)(2,1)}, u32[]{:S(2)}, u32[]{:S(2)}) collective-permute-start(bf16[5120,128]{1,0:T(8,128)(2,1)} %collective-permute-done.18.refs_18_.refs_16_), channel_id=1, source_target_pairs={{0,8},{8,0},{16,24},{24,16},{32,40},{40,32},{48,56},{56,48},{64,72... | collective-permute-start | bytes 3932168 | tf_op jit(solution)/shard_map/ppermute | solution.py:309
  150.6 13.5 %copy-start.11 = (s32[4]{0:T(128)}, s32[4]{0:T(128)S(1)}, u32[]{:S(2)}) copy-start(s32[4]{0:T(128)S(1)} %compare_select_fusion.2.refs_0_) | copy-start | bytes 52
  152.0 1.1 copy-start.6
  164.1 5.3 %copy-start.12 = (s32[16]{0:T(128)S(1)}, s32[16]{0:T(128)}, u32[]{:S(2)}) copy-start(s32[16]{0:T(128)} %param.5) | copy-start | bytes 196
  165.3 9.7 %collective-permute-start.30 = (f32[4,128,128]{1,2,0:T(8,128)S(1)}, f32[4,128,128]{1,2,0:T(8,128)S(1)}, u32[]{:S(2)}, u32[]{:S(2)}) collective-permute-start(f32[4,128,128]{1,2,0:T(8,128)S(1)} %bitcast.100), channel_id=1, source_target_pairs={{0,1},{8,9},{16,17},{24,25},{32,33},{40,41},{48,49},{56,57},{64,65... | collective-permute-start | bytes 786440 | tf_op jit(solution)/shard_map/ppermute | solution.py:357
  175.1 3.9 %collective-permute-start.32 = (f32[128,128]{0,1:T(8,128)S(1)}, f32[128,128]{0,1:T(8,128)S(1)}, u32[]{:S(2)}, u32[]{:S(2)}) collective-permute-start(f32[128,128]{0,1:T(8,128)S(1)} %get-tuple-element.57), channel_id=1, source_target_pairs={{0,4},{1,5},{8,12},{9,13},{16,20},{17,21},{24,28},{25,29},{32,36},... | collective-permute-start | bytes 196616 | tf_op jit(solution)/shard_map/ppermute | solution.py:360
  176.4 2.6 collective-permute-start.33
  177.7 2.6 collective-permute-start.31
  180.3 3.9 %collective-permute-start.38 = (f32[128,128]{0,1:T(8,128)S(1)}, f32[128,128]{0,1:T(8,128)S(1)}, u32[]{:S(2)}, u32[]{:S(2)}) collective-permute-start(f32[128,128]{0,1:T(8,128)S(1)} %get-tuple-element.52), channel_id=1, source_target_pairs={{0,16},{8,24},{16,0},{24,8},{32,48},{40,56},{48,32},{56,40},{64,80... | collective-permute-start | bytes 196616 | tf_op jit(solution)/shard_map/ppermute | solution.py:365
  180.4 30.0 %collective-permute-start.34 = (f32[128,128]{0,1:T(8,128)S(1)}, f32[128,128]{0,1:T(8,128)S(1)}, u32[]{:S(2)}, u32[]{:S(2)}) collective-permute-start(f32[128,128]{0,1:T(8,128)S(1)} %get-tuple-element.52), channel_id=1, source_target_pairs={{0,1},{1,0},{2,3},{3,2},{4,5},{5,4},{6,7},{7,6},{8,9},{9,8},{10,11... | collective-permute-start | bytes 196616 | tf_op jit(solution)/shard_map/ppermute | solution.py:363
  184.4 30.3 %collective-permute-start.40 = (f32[2,128,128]{1,0,2:T(2,128)S(1)}, f32[2,128,128]{1,0,2:T(2,128)S(1)}, u32[]{:S(2)}, u32[]{:S(2)}) collective-permute-start(f32[2,128,128]{1,0,2:T(2,128)S(1)} %get-tuple-element.61), channel_id=1, source_target_pairs={{0,96},{8,104},{16,112},{24,120},{32,0},{40,8},{48,16},{56,24},{64... | collective-permute-start | bytes 393224 | tf_op jit(solution)/shard_map/ppermute | solution.py:47
  185.5 29.2 %collective-permute-start.39 = (f32[2,128,128]{1,0,2:T(2,128)S(1)}, f32[2,128,128]{1,0,2:T(2,128)S(1)}, u32[]{:S(2)}, u32[]{:S(2)}) collective-permute-start(f32[2,128,128]{1,0,2:T(2,128)S(1)} %get-tuple-element.61), channel_id=1, source_target_pairs={{0,32},{8,40},{16,48},{24,56},{32,64},{40,72},{48,80},{56,88},{64,... | collective-permute-start | bytes 393224 | tf_op jit(solution)/shard_map/ppermute | solution.py:47
  185.9 28.8 %collective-permute-start.41 = (f32[2,128,128]{1,0,2:T(2,128)S(1)}, f32[2,128,128]{1,0,2:T(2,128)S(1)}, u32[]{:S(2)}, u32[]{:S(2)}) collective-permute-start(f32[2,128,128]{1,0,2:T(2,128)S(1)} %get-tuple-element.61), channel_id=1, source_target_pairs={{0,64},{8,72},{16,80},{24,88},{32,96},{40,104},{48,112},{56,120},{... | collective-permute-start | bytes 393224 | tf_op jit(solution)/shard_map/ppermute | solution.py:47
  210.4 10.2 %collective-permute-start.37 = (f32[2,128,128]{1,2,0:T(8,128)S(1)}, f32[2,128,128]{1,2,0:T(8,128)S(1)}, u32[]{:S(2)}, u32[]{:S(2)}) collective-permute-start(f32[2,128,128]{1,2,0:T(8,128)S(1)} %pad_maximum_fusion.3), channel_id=1, source_target_pairs={{0,4},{1,5},{2,6},{3,7},{4,0},{5,1},{6,2},{7,3},{8,12},{9,13},{10,... | collective-permute-start | bytes 393224 | tf_op jit(solution)/shard_map/ppermute | solution.py:47
  211.2 9.4 %collective-permute-start.36 = (f32[2,128,128]{1,2,0:T(8,128)S(1)}, f32[2,128,128]{1,2,0:T(8,128)S(1)}, u32[]{:S(2)}, u32[]{:S(2)}) collective-permute-start(f32[2,128,128]{1,2,0:T(8,128)S(1)} %pad_maximum_fusion.3), channel_id=1, source_target_pairs={{0,6},{1,7},{2,0},{3,1},{4,2},{5,3},{6,4},{7,5},{8,14},{9,15},{10,... | collective-permute-start | bytes 393224 | tf_op jit(solution)/shard_map/ppermute | solution.py:47
  214.7 5.9 %collective-permute-start.35 = (f32[2,128,128]{1,2,0:T(8,128)S(1)}, f32[2,128,128]{1,2,0:T(8,128)S(1)}, u32[]{:S(2)}, u32[]{:S(2)}) collective-permute-start(f32[2,128,128]{1,2,0:T(8,128)S(1)} %pad_maximum_fusion.3), channel_id=1, source_target_pairs={{0,2},{1,3},{2,4},{3,5},{4,6},{5,7},{6,0},{7,1},{8,10},{9,11},{10,... | collective-permute-start | bytes 393224 | tf_op jit(solution)/shard_map/ppermute | solution.py:47
  215.0 7.0 %collective-permute-start.42 = (f32[4,2,128,128]{2,1,0,3:T(2,128)S(1)}, f32[4,2,128,128]{2,1,0,3:T(2,128)S(1)}, u32[]{:S(2)}, u32[]{:S(2)}) collective-permute-start(f32[4,2,128,128]{2,1,0,3:T(2,128)S(1)} %pad_maximum_fusion.2), channel_id=1, source_target_pairs={{0,8},{8,0},{16,24},{24,16},{32,40},{40,32},{48,56},{56,48},{64,72... | collective-permute-start | bytes 1572872 | tf_op jit(solution)/shard_map/ppermute | solution.py:367
  235.9 42.7 %all-to-all-start.1 = ((s16[16,528,128]{2,1,0:T(8,128)(2,1)}), s16[16,528,128]{2,1,0:T(8,128)(2,1)S(1)}, u32[]{:S(2)}, u32[]{:S(2)}) async-start(s16[16,528,128]{2,1,0:T(8,128)(2,1)} %bitcast.87), calls=%async_computation.1 | async-start | bytes 4325376 | tf_op jit(solution)/shard_map/all_to_all | solution.py:398
  278.6 1.4 copy-start.10
  280.0 33.1 %all-to-all-start = ((s16[16,528,128]{2,1,0:T(8,128)(2,1)}), s16[16,528,128]{2,1,0:T(8,128)(2,1)}, u32[]{:S(2)}, u32[]{:S(2)}) async-start(s16[16,528,128]{2,1,0:T(8,128)(2,1)} %bitcast.88), calls=%async_computation | async-start | bytes 4325376 | tf_op jit(solution)/shard_map/all_to_all | solution.py:398

commit v3 on v2

--- a/solution.py
+++ b/solution.py
@@ -224,11 +224,14 @@
 
             @pl.when(pick[0] == n)
             def _():
-                copy = pltpu.make_async_copy(shards[n], first, sem)
-                copy.start()
-                copy.wait()
+                pltpu.make_async_copy(shards[n], first, sem).start()
 
     fetch_rows(parts, rows, row_sems)
+
+    @pl.when(pl.program_id(0) == 0)
+    def _():
+        pltpu.make_async_copy(shards[0], first, sem).wait()
+
     product_rows = jnp.dot(
         rows[pl.program_id(0) % 2], first[...], preferred_element_type=jnp.float32
     )
@@ -316,16 +319,24 @@
 
     leading = running[:NB, 0, 0, :] + dot0(genotypes, genotypes) * inv_snp
     lower = jnp.linalg.cholesky(leading)
-
-    late, across, lower = lax.optimization_barrier((genotypes, across, lower))
+    inverse = lax.linalg.triangular_solve(
+        lower, jnp.eye(NB, dtype=jnp.float32), left_side=True, lower=True
+    )
+
+    away = (jnp.arange(4, dtype=jnp.uint32) - z) & 3
+    slots = jnp.where(away == 0, 0, jnp.where(away == 1, 2, jnp.where(away == 2, 3, 1)))
+    slots = slots.astype(jnp.int32)
+    pick = slots[0] * 4 + (core * 2 + x_lo).astype(jnp.int32)
+    pick = jnp.stack([pick, *[jnp.int32(step) for step in STEP_OF_SLOT]])
+
+    late, across, inverse, old_panel, pick, slots = lax.optimization_barrier(
+        (genotypes, across, inverse, running[:, 0, 0, :], pick, slots)
+    )
     beside = lax.ppermute(late, "row", row_perm(0, 1, 0))
     y_up_across, y_down_across = ring_sides(across, "col", col_perm)
     z_opposite = jnp.concatenate(ring_relay(z_up, z_down, "row", row_perm), axis=0)
     y_opposite = ring_relay(y_up, y_down, "col", col_perm)
     z_up_twin, z_down_twin = twin(z_up), twin(z_down)
-    inverse = lax.linalg.triangular_solve(
-        lower, jnp.eye(NB, dtype=jnp.float32), left_side=True, lower=True
-    )
 
     heard = sum(lax.ppermute(inverse, "row", [(0, d * NX * NC)]) for d in range(1, NZ))
     inverse = jnp.where(z == 0, inverse, heard)
@@ -346,13 +357,8 @@
         (z_opposite, z_opposite_side, twin(z_opposite), twin(z_opposite_side)),
     ]
 
-    away = (jnp.arange(4, dtype=jnp.uint32) - z) & 3
-    slots = jnp.where(away == 0, 0, jnp.where(away == 1, 2, jnp.where(away == 2, 3, 1)))
-    slots = slots.astype(jnp.int32)
-    pick = slots[0] * 4 + (core * 2 + x_lo).astype(jnp.int32)
-    pick = jnp.stack([pick, *[jnp.int32(step) for step in STEP_OF_SLOT]])
     flat_shards = [shard for group in col_shards for shard in group]
-    factor = panel(pick, running[:, 0, 0, :], inverse, row_parts, flat_shards)
+    factor = panel(pick, old_panel, inverse, row_parts, flat_shards)
     pieces = factor.reshape(NY, NH, 128, NB)
     heard = lax.ppermute(pieces[:, 1], "col", [(0, 1)])
     pieces = jnp.where(x_hi == 0, pieces[:, 0], heard)

time: 319 us -> 309 us (0.969)
  waiting for transfers between devices: 73.6 us -> 63.1 us
    ppermute x1, waiting for transfers between devices: 10.8 us -> 1.03 us  [compute(): across = lax.ppermute(turned, 'col', col_perm(0, 1))]
  transfers between devices with their start and end apart: 45 -> 45, of which waited for: 12 -> 12; matrix products, arithmetic and copies ran while one was open for 12% -> 12% of each run, Pallas kernels for 19% -> 20%
where the time goes in v3:
time: 309 us; the launch traced here: 307 us
  starting transfers between devices  110 us (36%)
  Pallas kernels  87 us (28%)
  waiting for transfers between devices  63.1 us (20%)
  other arithmetic  26.7 us (9%)
  local copies, waits for them, and re-layouts  18.5 us (6%)
    pallas_call x4, Pallas kernels, product(): pl.pallas_call(lambda *refs: product_kernel(*refs, plane=plane), grid_spe...  46.2 us
    ppermute x8, starting transfers between devices, twin(): return lax.ppermute(value, 'row', row_perm(0, 0, 1))  39.8 us
    all_to_all x2, waiting for transfers between devices, compute(): lax.all_to_all(packed.reshape(16, CODED_ROWS, 128), 'row', split_axis=0,...  23.5 us
    pallas_call x2, Pallas kernels, epilogue(): pl.pallas_call(lambda *refs: epilogue_kernel(*refs, part=part, inv_snp=1....  22.1 us
    all_to_all x2, starting transfers between devices, compute(): lax.all_to_all(packed.reshape(16, CODED_ROWS, 128), 'row', split_axis=0,...  13 us
    another operation x3, other arithmetic, compute(): lower = jnp.linalg.cholesky(leading)  12.4 us
    ppermute x4, starting transfers between devices, ring_sides(): lax.ppermute(shard, axis, perm(-1))  11.9 us
    another operation x2, other arithmetic, compute(): lax.linalg.triangular_solve(lower, jnp.eye(NB, dtype=jnp.float32), left_s...  10.4 us
  transfers between devices with their start and end apart: 45, of which 12 were waited for; matrix products, arithmetic and copies ran while one was open for 12% of the time, Pallas kernels for 20%

profile of v3, /device:TPU:1, one launch (start us, length us, event | category | flops | bytes accessed | tf_op | source)
XLA Modules:
  0.0 307.1 jit_solution(5457407479908013884)
XLA Ops:
  0.0 1.7 copy.19
  1.7 3.6 %collective-permute-start.3 = (bf16[128,5120]{1,0:T(8,128)(2,1)S(1)}, bf16[128,5120]{1,0:T(8,128)(2,1)}, u32[]{:S(2)}, u32[]{:S(2)}) collective-permute-start(bf16[128,5120]{1,0:T(8,128)(2,1)S(1)} %bitcast.75), channel_id=1, source_target_pairs={{0,6},{1,7},{2,0},{3,1},{4,2},{5,3},{6,4},{7,5},{8,14},{9,15},{10,... | collective-permute-start | bytes 3932168 | tf_op jit(solution)/shard_map/ppermute | solution.py:36
  5.3 2.7 collective-permute-start
  9.7 11.7 %cholesky.17 = f32[128,128]{1,0:T(8,128)S(1)} custom-call(f32[128,128]{1,0:T(8,128)S(1)} %fusion.6), custom_call_target="Cholesky" | custom-call | tf_op jit(solution)/shard_map/jit(cholesky)/cholesky | solution.py:321
  22.1 1.9 slice.56
  24.5 9.8 %custom-call.6 = f32[1,128,128]{1,2,0:T(8,128)S(1)} custom-call(f32[1,128,128]{2,1,0:T(8,128)S(1)} %fusion.2), custom_call_target="InvertDiagBlocksLowerTriangular" | custom-call | tf_op jit(solution)/shard_map/triangular_solve | solution.py:322
  35.3 1.0 collective-permute-done.refs_4_.refs_2_
  38.4 3.8 %collective-permute-start.21 = (bf16[5120,128]{1,0:T(8,128)(2,1)S(1)}, bf16[5120,128]{1,0:T(8,128)(2,1)}, u32[]{:S(2)}, u32[]{:S(2)}) collective-permute-start(bf16[5120,128]{1,0:T(8,128)(2,1)S(1)} %copy-done), channel_id=1, source_target_pairs={{0,96},{8,104},{16,112},{24,120},{32,0},{40,8},{48,16},{56,24},{64... | collective-permute-start | bytes 3932168 | tf_op jit(solution)/shard_map/ppermute | solution.py:36
  42.2 8.1 %collective-permute-start.15 = (bf16[5120,128]{1,0:T(8,128)(2,1)S(1)}, bf16[5120,128]{1,0:T(8,128)(2,1)}, u32[]{:S(2)}, u32[]{:S(2)}) collective-permute-start(bf16[5120,128]{1,0:T(8,128)(2,1)S(1)} %copy-done), channel_id=1, source_target_pairs={{0,8},{8,0},{16,24},{24,16},{32,40},{40,32},{48,56},{56,48},{64,72... | collective-permute-start | bytes 3932168 | tf_op jit(solution)/shard_map/ppermute | solution.py:312
  51.0 1.1 slice.71
  52.2 2.7 collective-permute-start.6
  54.9 1.1 slice.70
  56.2 7.8 %collective-permute-done.21.refs_21_.refs_19_ = bf16[5120,128]{1,0:T(8,128)(2,1)} collective-permute-done((bf16[5120,128]{1,0:T(8,128)(2,1)S(1)}, bf16[5120,128]{1,0:T(8,128)(2,1)}, u32[]{:S(2)}, u32[]{:S(2)}) %collective-permute-start.21) | collective-permute-done | bytes 1310752 | tf_op jit(solution)/shard_map/ppermute | solution.py:36
  63.9 1.3 collective-permute-start.13
  65.2 1.1 slice.75
  66.4 3.6 %collective-permute-start.26 = (bf16[2560,128]{1,0:T(8,128)(2,1)S(1)}, bf16[2560,128]{1,0:T(8,128)(2,1)S(1)}, u32[]{:S(2)}, u32[]{:S(2)}) collective-permute-start(bf16[2560,128]{1,0:T(8,128)(2,1)S(1)} %slice.75), channel_id=1, source_target_pairs={{0,96},{8,104},{16,112},{24,120},{32,0},{40,8},{48,16},{56,24},{64... | collective-permute-start | bytes 1966088 | tf_op jit(solution)/shard_map/ppermute | solution.py:42
  70.0 1.1 slice.74
  71.1 1.1 collective-permute-start.25
  72.1 2.7 collective-permute-done.13
  74.9 2.2 collective-permute-start.14
  77.1 2.1 collective-permute-start.4
  79.8 7.5 %collective-permute-start.23 = (bf16[5120,128]{1,0:T(8,128)(2,1)}, bf16[5120,128]{1,0:T(8,128)(2,1)S(1)}, u32[]{:S(2)}, u32[]{:S(2)}) collective-permute-start(bf16[5120,128]{1,0:T(8,128)(2,1)} %collective-permute-done.21.refs_21_.refs_19_), channel_id=1, source_target_pairs={{0,8},{8,0},{16,24},{24,16},{32,40},{40,32},{48,56},{56,48},{64,72... | collective-permute-start | bytes 3932168 | tf_op jit(solution)/shard_map/ppermute | solution.py:312
  87.3 4.9 %collective-permute-start.19 = (bf16[5120,128]{1,0:T(8,128)(2,1)}, bf16[5120,128]{1,0:T(8,128)(2,1)}, u32[]{:S(2)}, u32[]{:S(2)}) collective-permute-start(bf16[5120,128]{1,0:T(8,128)(2,1)} %collective-permute-done.17.refs_17_.refs_15_), channel_id=1, source_target_pairs={{0,8},{8,0},{16,24},{24,16},{32,40},{40,32},{48,56},{56,48},{64,72... | collective-permute-start | bytes 3932168 | tf_op jit(solution)/shard_map/ppermute | solution.py:312
  94.0 8.0 %collective-permute-done.14.refs_14_.refs_12_ = bf16[5120,128]{1,0:T(8,128)(2,1)} collective-permute-done((bf16[5120,128]{1,0:T(8,128)(2,1)S(1)}, bf16[5120,128]{1,0:T(8,128)(2,1)}, u32[]{:S(2)}, u32[]{:S(2)}) %collective-permute-start.14) | collective-permute-done | bytes 1310752 | tf_op jit(solution)/shard_map/ppermute | solution.py:335
  102.0 2.3 collective-permute-start.27
  104.3 2.3 collective-permute-start.22
  106.8 1.0 copy-done.3
  107.7 1.1 copy-done.4
  108.8 2.3 collective-permute-start.8
  111.1 8.3 %collective-permute-done.8.refs_12_.refs_10_ = bf16[64,5120]{1,0:T(8,128)(2,1)S(1)} collective-permute-done((bf16[64,5120]{1,0:T(8,128)(2,1)S(1)}, bf16[64,5120]{1,0:T(8,128)(2,1)S(1)}, u32[]{:S(2)}, u32[]{:S(2)}) %collective-permute-start.8) | collective-permute-done | bytes 655392 | tf_op jit(solution)/shard_map/ppermute | solution.py:42
  119.4 6.6 %collective-permute-start.28 = (bf16[5120,128]{1,0:T(8,128)(2,1)}, bf16[5120,128]{1,0:T(8,128)(2,1)S(1)}, u32[]{:S(2)}, u32[]{:S(2)}) collective-permute-start(bf16[5120,128]{1,0:T(8,128)(2,1)} %constant_dynamic-update-slice_fusion.refs_25_.refs_23_), channel_id=1, source_target_pairs={{0,8},{8,0},{16,24},{24,16},{32,40},{40,32},{48,56},{56,48},{64,72... | collective-permute-start | bytes 3932168 | tf_op jit(solution)/shard_map/ppermute | solution.py:312
  126.1 3.4 %collective-permute-start.16 = (bf16[5120,128]{1,0:T(8,128)(2,1)}, bf16[5120,128]{1,0:T(8,128)(2,1)}, u32[]{:S(2)}, u32[]{:S(2)}) collective-permute-start(bf16[5120,128]{1,0:T(8,128)(2,1)} %collective-permute-done.14.refs_14_.refs_12_), channel_id=1, source_target_pairs={{0,8},{8,0},{16,24},{24,16},{32,40},{40,32},{48,56},{56,48},{64,72... | collective-permute-start | bytes 3932168 | tf_op jit(solution)/shard_map/ppermute | solution.py:312
  130.1 4.8 %collective-permute-start.29 = (bf16[5120,128]{1,0:T(8,128)(2,1)S(1)}, bf16[5120,128]{1,0:T(8,128)(2,1)}, u32[]{:S(2)}, u32[]{:S(2)}) collective-permute-start(bf16[5120,128]{1,0:T(8,128)(2,1)S(1)} %collective-permute-done.27.refs_26_.refs_24_), channel_id=1, source_target_pairs={{0,8},{8,0},{16,24},{24,16},{32,40},{40,32},{48,56},{56,48},{64,72... | collective-permute-start | bytes 3932168 | tf_op jit(solution)/shard_map/ppermute | solution.py:312
  134.9 1.0 collective-permute-start.24
  135.9 3.4 %collective-permute-start.20 = (bf16[5120,128]{1,0:T(8,128)(2,1)}, bf16[5120,128]{1,0:T(8,128)(2,1)}, u32[]{:S(2)}, u32[]{:S(2)}) collective-permute-start(bf16[5120,128]{1,0:T(8,128)(2,1)} %collective-permute-done.18.refs_18_.refs_16_), channel_id=1, source_target_pairs={{0,8},{8,0},{16,24},{24,16},{32,40},{40,32},{48,56},{56,48},{64,72... | collective-permute-start | bytes 3932168 | tf_op jit(solution)/shard_map/ppermute | solution.py:312
  140.0 2.3 collective-permute-done.20.refs_20_.refs_18_
  142.4 10.1 %panel.1 = f32[1024,128]{1,0:T(8,128)} custom-call(s32[5]{0:T(128)} %stack.47.refs_0_, f32[1024,128]{1,0:T(8,128)} %bitcast.89, f32[128,128]{1,0:T(8,128)} %broadcast_select_fusion.1.refs_2_, bf16[128,5120]{1,0:T(8,128)(2,1)} %bitcast.78, bf16[128,5120]{1,0:T(8,128)(2,1)} %collective-permute-done.refs_4_.refs_2_, ...), custom_call_target="tpu_custom_call" | custom-call | tf_op jit(solution)/shard_map/panel/pallas_call | solution.py:250
  152.4 1.1 fusion.12
  153.7 4.1 %collective-permute-start.30 = (f32[4,128,128]{1,2,0:T(8,128)S(1)}, f32[4,128,128]{1,2,0:T(8,128)S(1)}, u32[]{:S(2)}, u32[]{:S(2)}) collective-permute-start(f32[4,128,128]{1,2,0:T(8,128)S(1)} %bitcast.100), channel_id=1, source_target_pairs={{0,1},{8,9},{16,17},{24,25},{32,33},{40,41},{48,49},{56,57},{64,65... | collective-permute-start | bytes 786440 | tf_op jit(solution)/shard_map/ppermute | solution.py:363
  157.9 5.1 %collective-permute-done.30 = f32[4,128,128]{1,2,0:T(8,128)S(1)} collective-permute-done((f32[4,128,128]{1,2,0:T(8,128)S(1)}, f32[4,128,128]{1,2,0:T(8,128)S(1)}, u32[]{:S(2)}, u32[]{:S(2)}) %collective-permute-start.30) | collective-permute-done | bytes 262176 | tf_op jit(solution)/shard_map/ppermute | solution.py:363
  163.0 1.3 collective-permute-start.32
  164.3 1.3 collective-permute-start.33
  165.6 1.3 collective-permute-start.31
  167.1 1.2 collective-permute-done.31
  168.6 4.4 %collective-permute-start.34 = (f32[128,128]{0,1:T(8,128)S(1)}, f32[128,128]{0,1:T(8,128)S(1)}, u32[]{:S(2)}, u32[]{:S(2)}) collective-permute-start(f32[128,128]{0,1:T(8,128)S(1)} %get-tuple-element.58), channel_id=1, source_target_pairs={{0,1},{1,0},{2,3},{3,2},{4,5},{5,4},{6,7},{7,6},{8,9},{9,8},{10,11... | collective-permute-start | bytes 196616 | tf_op jit(solution)/shard_map/ppermute | solution.py:369
  173.1 2.6 collective-permute-start.40
  175.7 1.3 collective-permute-start.41
  177.7 11.4 %product.6.refs_3_.refs_7_ = f32[1024,512]{1,0:T(8,128)} custom-call(s32[4]{0:T(128)} %copy-done.11, bf16[128,5120]{1,0:T(8,128)(2,1)} %bitcast.79, bf16[128,5120]{1,0:T(8,128)(2,1)} %collective-permute-done.refs_4_.refs_2_, bf16[128,5120]{1,0:T(8,128)(2,1)} %collective-permute-done.1.refs_5_.refs_3_, bf16[128,5120]{1,0:T(8,128)(2,1)} %copy-done.3, ...), custom_call_target="tpu_custom_call" | custom-call | tf_op jit(solution)/shard_map/product/pallas_call | solution.py:199
  189.1 11.5 %product.5.refs_2_.refs_6_ = f32[1024,512]{1,0:T(8,128)} custom-call(s32[4]{0:T(128)} %copy-done.11, bf16[128,5120]{1,0:T(8,128)(2,1)} %bitcast.80, bf16[128,5120]{1,0:T(8,128)(2,1)} %collective-permute-done.refs_4_.refs_2_, bf16[128,5120]{1,0:T(8,128)(2,1)} %collective-permute-done.1.refs_5_.refs_3_, bf16[128,5120]{1,0:T(8,128)(2,1)} %copy-done.3, ...), custom_call_target="tpu_custom_call" | custom-call | tf_op jit(solution)/shard_map/product/pallas_call | solution.py:199
  201.4 3.5 %collective-permute-start.36 = (f32[2,128,128]{1,2,0:T(8,128)S(1)}, f32[2,128,128]{1,2,0:T(8,128)S(1)}, u32[]{:S(2)}, u32[]{:S(2)}) collective-permute-start(f32[2,128,128]{1,2,0:T(8,128)S(1)} %pad_maximum_fusion.3), channel_id=1, source_target_pairs={{0,6},{1,7},{2,0},{3,1},{4,2},{5,3},{6,4},{7,5},{8,14},{9,15},{10,... | collective-permute-start | bytes 393224 | tf_op jit(solution)/shard_map/ppermute | solution.py:47
  205.2 4.1 %collective-permute-start.42 = (f32[4,2,128,128]{2,1,0,3:T(2,128)S(1)}, f32[4,2,128,128]{2,1,0,3:T(2,128)S(1)}, u32[]{:S(2)}, u32[]{:S(2)}) collective-permute-start(f32[4,2,128,128]{2,1,0,3:T(2,128)S(1)} %pad_maximum_fusion.2), channel_id=1, source_target_pairs={{0,8},{8,0},{16,24},{24,16},{32,40},{40,32},{48,56},{56,48},{64,72... | collective-permute-start | bytes 1572872 | tf_op jit(solution)/shard_map/ppermute | solution.py:373
  209.3 1.8 collective-permute-done.35
  211.2 1.0 copy.26
  213.9 1.3 pad_maximum_fusion.refs_9_.refs_10_
  215.3 11.1 %epilogue.2 = s16[8448,128]{1,0:T(8,128)(2,1)} custom-call(s32[57]{0:T(128)} %convert_element_type.36.refs_0_, f32[1024,16,128]{2,1,0:T(8,128)} %bitcast.71, f32[1024,512]{1,0:T(8,128)} %product.5.refs_2_.refs_6_, f32[1024,512]{1,0:T(8,128)} %product.6.refs_3_.refs_7_, f32[1024,128]{1,0:T(8,128)} %bitcast.83, f32[1024,16,128]{2,1,0:T(8,128)} %bitcast.72, ...), custom_call_target="tpu_custom_call" | custom-call | tf_op jit(solution)/shard_map/epilogue/pallas_call | solution.py:118
  226.3 7.6 %all-to-all-start.1 = ((s16[16,528,128]{2,1,0:T(8,128)(2,1)}), s16[16,528,128]{2,1,0:T(8,128)(2,1)S(1)}, u32[]{:S(2)}, u32[]{:S(2)}) async-start(s16[16,528,128]{2,1,0:T(8,128)(2,1)} %bitcast.87), calls=%async_computation.1 | async-start | bytes 4325376 | tf_op jit(solution)/shard_map/all_to_all | solution.py:404
  234.0 11.8 %product.4.refs_2_.refs_6_ = f32[1024,512]{1,0:T(8,128)} custom-call(s32[4]{0:T(128)} %copy-done.11, bf16[128,5120]{1,0:T(8,128)(2,1)} %bitcast.81, bf16[128,5120]{1,0:T(8,128)(2,1)} %collective-permute-done.refs_4_.refs_2_, bf16[128,5120]{1,0:T(8,128)(2,1)} %collective-permute-done.1.refs_5_.refs_3_, bf16[128,5120]{1,0:T(8,128)(2,1)} %copy-done.3, ...), custom_call_target="tpu_custom_call" | custom-call | tf_op jit(solution)/shard_map/product/pallas_call | solution.py:199
  245.8 11.5 %product.7.refs_3_.refs_7_ = f32[1024,512]{1,0:T(8,128)} custom-call(s32[4]{0:T(128)} %copy-done.11, bf16[128,5120]{1,0:T(8,128)(2,1)} %bitcast.82, bf16[128,5120]{1,0:T(8,128)(2,1)} %collective-permute-done.refs_4_.refs_2_, bf16[128,5120]{1,0:T(8,128)(2,1)} %collective-permute-done.1.refs_5_.refs_3_, bf16[128,5120]{1,0:T(8,128)(2,1)} %copy-done.3, ...), custom_call_target="tpu_custom_call" | custom-call | tf_op jit(solution)/shard_map/product/pallas_call | solution.py:199
  257.3 11.0 %epilogue.3 = s16[8448,128]{1,0:T(8,128)(2,1)} custom-call(s32[57]{0:T(128)} %convert_element_type.36.refs_0_, f32[1024,16,128]{2,1,0:T(8,128)} %bitcast.73, f32[1024,512]{1,0:T(8,128)} %product.4.refs_2_.refs_6_, f32[1024,512]{1,0:T(8,128)} %product.7.refs_3_.refs_7_, f32[1024,128]{1,0:T(8,128)} %bitcast.85, f32[1024,16,128]{2,1,0:T(8,128)} %bitcast.74, ...), custom_call_target="tpu_custom_call" | custom-call | tf_op jit(solution)/shard_map/epilogue/pallas_call | solution.py:118
  268.3 1.4 copy-done.10
  269.7 5.4 %all-to-all-start = ((s16[16,528,128]{2,1,0:T(8,128)(2,1)}), s16[16,528,128]{2,1,0:T(8,128)(2,1)}, u32[]{:S(2)}, u32[]{:S(2)}) async-start(s16[16,528,128]{2,1,0:T(8,128)(2,1)} %bitcast.88), calls=%async_computation | async-start | bytes 4325376 | tf_op jit(solution)/shard_map/all_to_all | solution.py:404
  275.0 4.3 %unpack.2.refs_0_ = f32[1024,16,128]{2,1,0:T(8,128)} custom-call(s16[16,528,128]{2,1,0:T(8,128)(2,1)} %copy-done.10), custom_call_target="tpu_custom_call" | custom-call | tf_op jit(solution)/shard_map/unpack/pallas_call | solution.py:286
  279.3 23.5 %all-to-all-done.coded = s16[16,528,128]{2,1,0:T(8,128)(2,1)} async-done(((s16[16,528,128]{2,1,0:T(8,128)(2,1)}), s16[16,528,128]{2,1,0:T(8,128)(2,1)}, u32[]{:S(2)}, u32[]{:S(2)}) %all-to-all-start) | async-done | bytes 2162720 | tf_op jit(solution)/shard_map/all_to_all | solution.py:404
  302.8 4.3 %unpack.3 = f32[1024,16,128]{2,1,0:T(8,128)} custom-call(s16[16,528,128]{2,1,0:T(8,128)(2,1)} %all-to-all-done.coded, f32[1024,16,128]{2,1,0:T(8,128)} %unpack.2.refs_0_), custom_call_target="tpu_custom_call", output_to_operand_aliasing={{}: (1, {})} | custom-call | tf_op jit(solution)/shard_map/unpack/pallas_call | solution.py:286
  (112 shorter events, 14.7 us)
Async XLA Ops:
  0.0 9.0 %copy-start = (bf16[5120,128]{1,0:T(8,128)(2,1)S(1)}, bf16[5120,128]{1,0:T(8,128)(2,1)}, u32[]{:S(2)}) copy-start(bf16[5120,128]{1,0:T(8,128)(2,1)} %refs_11_.7) | copy-start | bytes 3932164
  1.7 7.9 %copy-start.1 = (bf16[5120,128]{0,1:T(8,128)(2,1)}, bf16[5120,128]{0,1:T(8,128)(2,1)S(1)}, u32[]{:S(2)}) copy-start(bf16[5120,128]{0,1:T(8,128)(2,1)S(1)} %copy.19) | copy-start | bytes 3932164
  1.7 48.6 %collective-permute-start.3 = (bf16[128,5120]{1,0:T(8,128)(2,1)S(1)}, bf16[128,5120]{1,0:T(8,128)(2,1)}, u32[]{:S(2)}, u32[]{:S(2)}) collective-permute-start(bf16[128,5120]{1,0:T(8,128)(2,1)S(1)} %bitcast.75), channel_id=1, source_target_pairs={{0,6},{1,7},{2,0},{3,1},{4,2},{5,3},{6,4},{7,5},{8,14},{9,15},{10,... | collective-permute-start | bytes 3932168 | tf_op jit(solution)/shard_map/ppermute | solution.py:36
  5.3 46.8 %collective-permute-start.1 = (bf16[128,5120]{1,0:T(8,128)(2,1)S(1)}, bf16[128,5120]{1,0:T(8,128)(2,1)}, u32[]{:S(2)}, u32[]{:S(2)}) collective-permute-start(bf16[128,5120]{1,0:T(8,128)(2,1)S(1)} %bitcast.76), channel_id=1, source_target_pairs={{0,2},{1,3},{2,4},{3,5},{4,6},{5,7},{6,0},{7,1},{8,10},{9,11},{10,... | collective-permute-start | bytes 3932168 | tf_op jit(solution)/shard_map/ppermute | solution.py:36
  5.3 31.0 %collective-permute-start = (bf16[128,5120]{1,0:T(8,128)(2,1)S(1)}, bf16[128,5120]{1,0:T(8,128)(2,1)}, u32[]{:S(2)}, u32[]{:S(2)}) collective-permute-start(bf16[128,5120]{1,0:T(8,128)(2,1)S(1)} %bitcast.77), channel_id=1, source_target_pairs={{0,1},{1,0},{2,3},{3,2},{4,5},{5,4},{6,7},{7,6},{8,9},{9,8},{10,11... | collective-permute-start | bytes 3932168 | tf_op jit(solution)/shard_map/ppermute | solution.py:316
  34.3 142.7 %copy-start.11 = (s32[4]{0:T(128)}, s32[4]{0:T(128)S(1)}, u32[]{:S(2)}) copy-start(s32[4]{0:T(128)S(1)} %compare_select_fusion.2.refs_0_) | copy-start | bytes 52
  36.3 2.0 collective-permute-start.11
  37.0 5.2 %collective-permute-start.10 = (f32[128,128]{1,0:T(8,128)S(1)}, f32[128,128]{1,0:T(8,128)S(1)}, u32[]{:S(2)}, u32[]{:S(2)}) collective-permute-start(f32[128,128]{1,0:T(8,128)S(1)} %fusion.4), channel_id=1, source_target_pairs={{0,64},{1,65},{2,66},{3,67},{4,68},{5,69},{6,70},{7,71}} | collective-permute-start | bytes 196616 | tf_op jit(solution)/shard_map/ppermute | solution.py:341
  37.7 4.5 %collective-permute-start.9 = (f32[128,128]{1,0:T(8,128)S(1)}, f32[128,128]{1,0:T(8,128)S(1)}, u32[]{:S(2)}, u32[]{:S(2)}) collective-permute-start(f32[128,128]{1,0:T(8,128)S(1)} %fusion.4), channel_id=1, source_target_pairs={{0,32},{1,33},{2,34},{3,35},{4,36},{5,37},{6,38},{7,39}} | collective-permute-start | bytes 196616 | tf_op jit(solution)/shard_map/ppermute | solution.py:341
  38.4 25.6 %collective-permute-start.21 = (bf16[5120,128]{1,0:T(8,128)(2,1)S(1)}, bf16[5120,128]{1,0:T(8,128)(2,1)}, u32[]{:S(2)}, u32[]{:S(2)}) collective-permute-start(bf16[5120,128]{1,0:T(8,128)(2,1)S(1)} %copy-done), channel_id=1, source_target_pairs={{0,96},{8,104},{16,112},{24,120},{32,0},{40,8},{48,16},{56,24},{64... | collective-permute-start | bytes 3932168 | tf_op jit(solution)/shard_map/ppermute | solution.py:36
  42.2 24.2 %collective-permute-start.17 = (bf16[5120,128]{1,0:T(8,128)(2,1)S(1)}, bf16[5120,128]{1,0:T(8,128)(2,1)}, u32[]{:S(2)}, u32[]{:S(2)}) collective-permute-start(bf16[5120,128]{1,0:T(8,128)(2,1)S(1)} %copy-done), channel_id=1, source_target_pairs={{0,32},{8,40},{16,48},{24,56},{32,64},{40,72},{48,80},{56,88},{64,... | collective-permute-start | bytes 3932168 | tf_op jit(solution)/shard_map/ppermute | solution.py:36
  42.2 28.9 %collective-permute-start.15 = (bf16[5120,128]{1,0:T(8,128)(2,1)S(1)}, bf16[5120,128]{1,0:T(8,128)(2,1)}, u32[]{:S(2)}, u32[]{:S(2)}) collective-permute-start(bf16[5120,128]{1,0:T(8,128)(2,1)S(1)} %copy-done), channel_id=1, source_target_pairs={{0,8},{8,0},{16,24},{24,16},{32,40},{40,32},{48,56},{56,48},{64,72... | collective-permute-start | bytes 3932168 | tf_op jit(solution)/shard_map/ppermute | solution.py:312
  50.4 5.7 %collective-permute-start.12 = (f32[128,128]{1,0:T(8,128)S(1)}, f32[128,128]{1,0:T(8,128)S(1)}, u32[]{:S(2)}, u32[]{:S(2)}) collective-permute-start(f32[128,128]{1,0:T(8,128)S(1)} %add_select_fusion), channel_id=1, source_target_pairs={{0,16},{32,48},{64,80},{96,112},{1,17},{33,49},{65,81},{97,113},{2... | collective-permute-start | bytes 196616 | tf_op jit(solution)/shard_map/ppermute | solution.py:344
  52.2 24.9 %collective-permute-start.6 = (bf16[64,5120]{1,0:T(8,128)(2,1)S(1)}, bf16[64,5120]{1,0:T(8,128)(2,1)S(1)}, u32[]{:S(2)}, u32[]{:S(2)}) collective-permute-start(bf16[64,5120]{1,0:T(8,128)(2,1)S(1)} %slice.71), channel_id=1, source_target_pairs={{0,6},{1,7},{2,0},{3,1},{4,2},{5,3},{6,4},{7,5},{8,14},{9,15},{10,... | collective-permute-start | bytes 1966088 | tf_op jit(solution)/shard_map/ppermute | solution.py:42
  56.1 23.1 %collective-permute-start.5 = (bf16[64,5120]{1,0:T(8,128)(2,1)S(1)}, bf16[64,5120]{1,0:T(8,128)(2,1)}, u32[]{:S(2)}, u32[]{:S(2)}) collective-permute-start(bf16[64,5120]{1,0:T(8,128)(2,1)S(1)} %slice.70), channel_id=1, source_target_pairs={{0,2},{1,3},{2,4},{3,5},{4,6},{5,7},{6,0},{7,1},{8,10},{9,11},{10,... | collective-permute-start | bytes 1966088 | tf_op jit(solution)/shard_map/ppermute | solution.py:41
  63.9 11.0 %collective-permute-start.13 = (f32[128,128]{1,0:T(8,128)S(1)}, f32[128,128]{1,0:T(8,128)S(1)}, u32[]{:S(2)}, u32[]{:S(2)}) collective-permute-start(f32[128,128]{1,0:T(8,128)S(1)} %broadcast_select_fusion), channel_id=1, source_target_pairs={{0,8},{16,24},{32,40},{48,56},{64,72},{80,88},{96,104},{112,120},{... | collective-permute-start | bytes 196616 | tf_op jit(solution)/shard_map/ppermute | solution.py:348
  66.4 13.5 %collective-permute-start.26 = (bf16[2560,128]{1,0:T(8,128)(2,1)S(1)}, bf16[2560,128]{1,0:T(8,128)(2,1)S(1)}, u32[]{:S(2)}, u32[]{:S(2)}) collective-permute-start(bf16[2560,128]{1,0:T(8,128)(2,1)S(1)} %slice.75), channel_id=1, source_target_pairs={{0,96},{8,104},{16,112},{24,120},{32,0},{40,8},{48,16},{56,24},{64... | collective-permute-start | bytes 1966088 | tf_op jit(solution)/shard_map/ppermute | solution.py:42
  71.1 16.2 %collective-permute-start.25 = (bf16[2560,128]{1,0:T(8,128)(2,1)S(1)}, bf16[2560,128]{1,0:T(8,128)(2,1)S(1)}, u32[]{:S(2)}, u32[]{:S(2)}) collective-permute-start(bf16[2560,128]{1,0:T(8,128)(2,1)S(1)} %slice.74), channel_id=1, source_target_pairs={{0,32},{8,40},{16,48},{24,56},{32,64},{40,72},{48,80},{56,88},{64,... | collective-permute-start | bytes 1966088 | tf_op jit(solution)/shard_map/ppermute | solution.py:41
  74.9 27.1 %collective-permute-start.14 = (bf16[5120,128]{1,0:T(8,128)(2,1)S(1)}, bf16[5120,128]{1,0:T(8,128)(2,1)}, u32[]{:S(2)}, u32[]{:S(2)}) collective-permute-start(bf16[5120,128]{1,0:T(8,128)(2,1)S(1)} %copy-done), channel_id=1, source_target_pairs={{0,16},{8,24},{16,0},{24,8},{32,48},{40,56},{48,32},{56,40},{64,80... | collective-permute-start | bytes 3932168 | tf_op jit(solution)/shard_map/ppermute | solution.py:335
  77.1 29.6 %copy-start.7 = (bf16[64,5120]{1,0:T(8,128)(2,1)}, bf16[64,5120]{1,0:T(8,128)(2,1)S(1)}, u32[]{:S(2)}) copy-start(bf16[64,5120]{1,0:T(8,128)(2,1)S(1)} %collective-permute-done.6.refs_10_.refs_8_) | copy-start | bytes 1966084
  77.1 27.3 %collective-permute-start.4 = (bf16[128,5120]{1,0:T(8,128)(2,1)}, bf16[128,5120]{1,0:T(8,128)(2,1)S(1)}, u32[]{:S(2)}, u32[]{:S(2)}) collective-permute-start(bf16[128,5120]{1,0:T(8,128)(2,1)} %collective-permute-done.refs_4_.refs_2_), channel_id=1, source_target_pairs={{0,6},{1,7},{2,0},{3,1},{4,2},{5,3},{6,4},{7,5},{8,14},{9,15},{10,... | collective-permute-start | bytes 3932168 | tf_op jit(solution)/shard_map/ppermute | solution.py:36
  79.2 27.5 %collective-permute-start.2 = (bf16[128,5120]{1,0:T(8,128)(2,1)}, bf16[128,5120]{1,0:T(8,128)(2,1)S(1)}, u32[]{:S(2)}, u32[]{:S(2)}) collective-permute-start(bf16[128,5120]{1,0:T(8,128)(2,1)} %collective-permute-done.refs_4_.refs_2_), channel_id=1, source_target_pairs={{0,2},{1,3},{2,4},{3,5},{4,6},{5,7},{6,0},{7,1},{8,10},{9,11},{10,... | collective-permute-start | bytes 3932168 | tf_op jit(solution)/shard_map/ppermute | solution.py:36
  79.8 27.9 %collective-permute-start.23 = (bf16[5120,128]{1,0:T(8,128)(2,1)}, bf16[5120,128]{1,0:T(8,128)(2,1)S(1)}, u32[]{:S(2)}, u32[]{:S(2)}) collective-permute-start(bf16[5120,128]{1,0:T(8,128)(2,1)} %collective-permute-done.21.refs_21_.refs_19_), channel_id=1, source_target_pairs={{0,8},{8,0},{16,24},{24,16},{32,40},{40,32},{48,56},{56,48},{64,72... | collective-permute-start | bytes 3932168 | tf_op jit(solution)/shard_map/ppermute | solution.py:312
  87.3 23.8 %collective-permute-start.19 = (bf16[5120,128]{1,0:T(8,128)(2,1)}, bf16[5120,128]{1,0:T(8,128)(2,1)}, u32[]{:S(2)}, u32[]{:S(2)}) collective-permute-start(bf16[5120,128]{1,0:T(8,128)(2,1)} %collective-permute-done.17.refs_17_.refs_15_), channel_id=1, source_target_pairs={{0,8},{8,0},{16,24},{24,16},{32,40},{40,32},{48,56},{56,48},{64,72... | collective-permute-start | bytes 3932168 | tf_op jit(solution)/shard_map/ppermute | solution.py:312
  102.0 28.1 %collective-permute-start.27 = (bf16[5120,128]{1,0:T(8,128)(2,1)}, bf16[5120,128]{1,0:T(8,128)(2,1)S(1)}, u32[]{:S(2)}, u32[]{:S(2)}) collective-permute-start(bf16[5120,128]{1,0:T(8,128)(2,1)} %constant_dynamic-update-slice_fusion.refs_25_.refs_23_), channel_id=1, source_target_pairs={{0,16},{8,24},{16,0},{24,8},{32,48},{40,56},{48,32},{56,40},{64,80... | collective-permute-start | bytes 3932168 | tf_op jit(solution)/shard_map/ppermute | solution.py:346
  104.3 2.4 copy-start.2
  104.3 30.6 %collective-permute-start.22 = (bf16[5120,128]{1,0:T(8,128)(2,1)}, bf16[5120,128]{1,0:T(8,128)(2,1)}, u32[]{:S(2)}, u32[]{:S(2)}) collective-permute-start(bf16[5120,128]{1,0:T(8,128)(2,1)} %collective-permute-done.14.refs_14_.refs_12_), channel_id=1, source_target_pairs={{0,96},{8,104},{16,112},{24,120},{32,0},{40,8},{48,16},{56,24},{64... | collective-permute-start | bytes 3932168 | tf_op jit(solution)/shard_map/ppermute | solution.py:36
  106.6 1.1 copy-start.3
  106.6 29.3 %collective-permute-start.18 = (bf16[5120,128]{1,0:T(8,128)(2,1)}, bf16[5120,128]{1,0:T(8,128)(2,1)}, u32[]{:S(2)}, u32[]{:S(2)}) collective-permute-start(bf16[5120,128]{1,0:T(8,128)(2,1)} %collective-permute-done.14.refs_14_.refs_12_), channel_id=1, source_target_pairs={{0,32},{8,40},{16,48},{24,56},{32,64},{40,72},{48,80},{56,88},{64,... | collective-permute-start | bytes 3932168 | tf_op jit(solution)/shard_map/ppermute | solution.py:36
  107.7 1.1 copy-start.4
  108.8 10.6 %collective-permute-start.8 = (bf16[64,5120]{1,0:T(8,128)(2,1)S(1)}, bf16[64,5120]{1,0:T(8,128)(2,1)S(1)}, u32[]{:S(2)}, u32[]{:S(2)}) collective-permute-start(bf16[64,5120]{1,0:T(8,128)(2,1)S(1)} %slice.73), channel_id=1, source_target_pairs={{0,6},{1,7},{2,0},{3,1},{4,2},{5,3},{6,4},{7,5},{8,14},{9,15},{10,... | collective-permute-start | bytes 1966088 | tf_op jit(solution)/shard_map/ppermute | solution.py:42
  111.1 14.9 %collective-permute-start.7 = (bf16[64,5120]{1,0:T(8,128)(2,1)S(1)}, bf16[64,5120]{1,0:T(8,128)(2,1)S(1)}, u32[]{:S(2)}, u32[]{:S(2)}) collective-permute-start(bf16[64,5120]{1,0:T(8,128)(2,1)S(1)} %slice.72), channel_id=1, source_target_pairs={{0,2},{1,3},{2,4},{3,5},{4,6},{5,7},{6,0},{7,1},{8,10},{9,11},{10,... | collective-permute-start | bytes 1966088 | tf_op jit(solution)/shard_map/ppermute | solution.py:41
  119.4 22.9 %copy-start.8 = (bf16[64,5120]{1,0:T(8,128)(2,1)}, bf16[64,5120]{1,0:T(8,128)(2,1)S(1)}, u32[]{:S(2)}) copy-start(bf16[64,5120]{1,0:T(8,128)(2,1)S(1)} %collective-permute-done.8.refs_12_.refs_10_) | copy-start | bytes 1966084
  119.4 20.5 %collective-permute-start.28 = (bf16[5120,128]{1,0:T(8,128)(2,1)}, bf16[5120,128]{1,0:T(8,128)(2,1)S(1)}, u32[]{:S(2)}, u32[]{:S(2)}) collective-permute-start(bf16[5120,128]{1,0:T(8,128)(2,1)} %constant_dynamic-update-slice_fusion.refs_25_.refs_23_), channel_id=1, source_target_pairs={{0,8},{8,0},{16,24},{24,16},{32,40},{40,32},{48,56},{56,48},{64,72... | collective-permute-start | bytes 3932168 | tf_op jit(solution)/shard_map/ppermute | solution.py:312
  126.1 4.0 %copy-start.9 = (bf16[64,5120]{1,0:T(8,128)(2,1)}, bf16[64,5120]{1,0:T(8,128)(2,1)S(1)}, u32[]{:S(2)}) copy-start(bf16[64,5120]{1,0:T(8,128)(2,1)S(1)} %collective-permute-done.7.refs_11_.refs_9_) | copy-start | bytes 1966084
  126.1 13.9 %collective-permute-start.16 = (bf16[5120,128]{1,0:T(8,128)(2,1)}, bf16[5120,128]{1,0:T(8,128)(2,1)}, u32[]{:S(2)}, u32[]{:S(2)}) collective-permute-start(bf16[5120,128]{1,0:T(8,128)(2,1)} %collective-permute-done.14.refs_14_.refs_12_), channel_id=1, source_target_pairs={{0,8},{8,0},{16,24},{24,16},{32,40},{40,32},{48,56},{56,48},{64,72... | collective-permute-start | bytes 3932168 | tf_op jit(solution)/shard_map/ppermute | solution.py:312
  130.1 12.3 %copy-start.5 = (bf16[5120,128]{1,0:T(8,128)(2,1)}, bf16[5120,128]{1,0:T(8,128)(2,1)S(1)}, u32[]{:S(2)}) copy-start(bf16[5120,128]{1,0:T(8,128)(2,1)S(1)} %collective-permute-done.27.refs_26_.refs_24_) | copy-start | bytes 3932164
  130.1 9.9 %collective-permute-start.29 = (bf16[5120,128]{1,0:T(8,128)(2,1)S(1)}, bf16[5120,128]{1,0:T(8,128)(2,1)}, u32[]{:S(2)}, u32[]{:S(2)}) collective-permute-start(bf16[5120,128]{1,0:T(8,128)(2,1)S(1)} %collective-permute-done.27.refs_26_.refs_24_), channel_id=1, source_target_pairs={{0,8},{8,0},{16,24},{24,16},{32,40},{40,32},{48,56},{56,48},{64,72... | collective-permute-start | bytes 3932168 | tf_op jit(solution)/shard_map/ppermute | solution.py:312
  134.9 5.1 %collective-permute-start.24 = (bf16[5120,128]{1,0:T(8,128)(2,1)}, bf16[5120,128]{1,0:T(8,128)(2,1)}, u32[]{:S(2)}, u32[]{:S(2)}) collective-permute-start(bf16[5120,128]{1,0:T(8,128)(2,1)} %collective-permute-done.22.refs_22_.refs_20_), channel_id=1, source_target_pairs={{0,8},{8,0},{16,24},{24,16},{32,40},{40,32},{48,56},{56,48},{64,72... | collective-permute-start | bytes 3932168 | tf_op jit(solution)/shard_map/ppermute | solution.py:312
  135.9 6.4 %collective-permute-start.20 = (bf16[5120,128]{1,0:T(8,128)(2,1)}, bf16[5120,128]{1,0:T(8,128)(2,1)}, u32[]{:S(2)}, u32[]{:S(2)}) collective-permute-start(bf16[5120,128]{1,0:T(8,128)(2,1)} %collective-permute-done.18.refs_18_.refs_16_), channel_id=1, source_target_pairs={{0,8},{8,0},{16,24},{24,16},{32,40},{40,32},{48,56},{56,48},{64,72... | collective-permute-start | bytes 3932168 | tf_op jit(solution)/shard_map/ppermute | solution.py:312
  140.0 2.4 copy-start.6
  153.5 13.4 %copy-start.12 = (s32[16]{0:T(128)S(1)}, s32[16]{0:T(128)}, u32[]{:S(2)}) copy-start(s32[16]{0:T(128)} %param.5) | copy-start | bytes 196
  153.7 9.3 %collective-permute-start.30 = (f32[4,128,128]{1,2,0:T(8,128)S(1)}, f32[4,128,128]{1,2,0:T(8,128)S(1)}, u32[]{:S(2)}, u32[]{:S(2)}) collective-permute-start(f32[4,128,128]{1,2,0:T(8,128)S(1)} %bitcast.100), channel_id=1, source_target_pairs={{0,1},{8,9},{16,17},{24,25},{32,33},{40,41},{48,49},{56,57},{64,65... | collective-permute-start | bytes 786440 | tf_op jit(solution)/shard_map/ppermute | solution.py:363
  163.0 4.0 %collective-permute-start.32 = (f32[128,128]{0,1:T(8,128)S(1)}, f32[128,128]{0,1:T(8,128)S(1)}, u32[]{:S(2)}, u32[]{:S(2)}) collective-permute-start(f32[128,128]{0,1:T(8,128)S(1)} %get-tuple-element.63), channel_id=1, source_target_pairs={{0,4},{1,5},{8,12},{9,13},{16,20},{17,21},{24,28},{25,29},{32,36},... | collective-permute-start | bytes 196616 | tf_op jit(solution)/shard_map/ppermute | solution.py:366
  164.3 2.7 collective-permute-start.33
  165.6 2.6 collective-permute-start.31
  168.3 4.7 %collective-permute-start.38 = (f32[128,128]{0,1:T(8,128)S(1)}, f32[128,128]{0,1:T(8,128)S(1)}, u32[]{:S(2)}, u32[]{:S(2)}) collective-permute-start(f32[128,128]{0,1:T(8,128)S(1)} %get-tuple-element.58), channel_id=1, source_target_pairs={{0,16},{8,24},{16,0},{24,8},{32,48},{40,56},{48,32},{56,40},{64,80... | collective-permute-start | bytes 196616 | tf_op jit(solution)/shard_map/ppermute | solution.py:371
  168.6 32.1 %collective-permute-start.34 = (f32[128,128]{0,1:T(8,128)S(1)}, f32[128,128]{0,1:T(8,128)S(1)}, u32[]{:S(2)}, u32[]{:S(2)}) collective-permute-start(f32[128,128]{0,1:T(8,128)S(1)} %get-tuple-element.58), channel_id=1, source_target_pairs={{0,1},{1,0},{2,3},{3,2},{4,5},{5,4},{6,7},{7,6},{8,9},{9,8},{10,11... | collective-permute-start | bytes 196616 | tf_op jit(solution)/shard_map/ppermute | solution.py:369
  173.1 31.8 %collective-permute-start.40 = (f32[2,128,128]{1,0,2:T(2,128)S(1)}, f32[2,128,128]{1,0,2:T(2,128)S(1)}, u32[]{:S(2)}, u32[]{:S(2)}) collective-permute-start(f32[2,128,128]{1,0,2:T(2,128)S(1)} %get-tuple-element.67), channel_id=1, source_target_pairs={{0,96},{8,104},{16,112},{24,120},{32,0},{40,8},{48,16},{56,24},{64... | collective-permute-start | bytes 393224 | tf_op jit(solution)/shard_map/ppermute | solution.py:47
  175.7 29.2 %collective-permute-start.39 = (f32[2,128,128]{1,0,2:T(2,128)S(1)}, f32[2,128,128]{1,0,2:T(2,128)S(1)}, u32[]{:S(2)}, u32[]{:S(2)}) collective-permute-start(f32[2,128,128]{1,0,2:T(2,128)S(1)} %get-tuple-element.67), channel_id=1, source_target_pairs={{0,32},{8,40},{16,48},{24,56},{32,64},{40,72},{48,80},{56,88},{64,... | collective-permute-start | bytes 393224 | tf_op jit(solution)/shard_map/ppermute | solution.py:47
  175.7 29.2 %collective-permute-start.41 = (f32[2,128,128]{1,0,2:T(2,128)S(1)}, f32[2,128,128]{1,0,2:T(2,128)S(1)}, u32[]{:S(2)}, u32[]{:S(2)}) collective-permute-start(f32[2,128,128]{1,0,2:T(2,128)S(1)} %get-tuple-element.67), channel_id=1, source_target_pairs={{0,64},{8,72},{16,80},{24,88},{32,96},{40,104},{48,112},{56,120},{... | collective-permute-start | bytes 393224 | tf_op jit(solution)/shard_map/ppermute | solution.py:47
  200.6 10.5 %collective-permute-start.37 = (f32[2,128,128]{1,2,0:T(8,128)S(1)}, f32[2,128,128]{1,2,0:T(8,128)S(1)}, u32[]{:S(2)}, u32[]{:S(2)}) collective-permute-start(f32[2,128,128]{1,2,0:T(8,128)S(1)} %pad_maximum_fusion.3), channel_id=1, source_target_pairs={{0,4},{1,5},{2,6},{3,7},{4,0},{5,1},{6,2},{7,3},{8,12},{9,13},{10,... | collective-permute-start | bytes 393224 | tf_op jit(solution)/shard_map/ppermute | solution.py:47
  201.4 9.7 %collective-permute-start.36 = (f32[2,128,128]{1,2,0:T(8,128)S(1)}, f32[2,128,128]{1,2,0:T(8,128)S(1)}, u32[]{:S(2)}, u32[]{:S(2)}) collective-permute-start(f32[2,128,128]{1,2,0:T(8,128)S(1)} %pad_maximum_fusion.3), channel_id=1, source_target_pairs={{0,6},{1,7},{2,0},{3,1},{4,2},{5,3},{6,4},{7,5},{8,14},{9,15},{10,... | collective-permute-start | bytes 393224 | tf_op jit(solution)/shard_map/ppermute | solution.py:47
  204.9 6.2 %collective-permute-start.35 = (f32[2,128,128]{1,2,0:T(8,128)S(1)}, f32[2,128,128]{1,2,0:T(8,128)S(1)}, u32[]{:S(2)}, u32[]{:S(2)}) collective-permute-start(f32[2,128,128]{1,2,0:T(8,128)S(1)} %pad_maximum_fusion.3), channel_id=1, source_target_pairs={{0,2},{1,3},{2,4},{3,5},{4,6},{5,7},{6,0},{7,1},{8,10},{9,11},{10,... | collective-permute-start | bytes 393224 | tf_op jit(solution)/shard_map/ppermute | solution.py:47
  205.2 7.3 %collective-permute-start.42 = (f32[4,2,128,128]{2,1,0,3:T(2,128)S(1)}, f32[4,2,128,128]{2,1,0,3:T(2,128)S(1)}, u32[]{:S(2)}, u32[]{:S(2)}) collective-permute-start(f32[4,2,128,128]{2,1,0,3:T(2,128)S(1)} %pad_maximum_fusion.2), channel_id=1, source_target_pairs={{0,8},{8,0},{16,24},{24,16},{32,40},{40,32},{48,56},{56,48},{64,72... | collective-permute-start | bytes 1572872 | tf_op jit(solution)/shard_map/ppermute | solution.py:373
  226.3 42.0 %all-to-all-start.1 = ((s16[16,528,128]{2,1,0:T(8,128)(2,1)}), s16[16,528,128]{2,1,0:T(8,128)(2,1)S(1)}, u32[]{:S(2)}, u32[]{:S(2)}) async-start(s16[16,528,128]{2,1,0:T(8,128)(2,1)} %bitcast.87), calls=%async_computation.1 | async-start | bytes 4325376 | tf_op jit(solution)/shard_map/all_to_all | solution.py:404
  268.3 1.4 copy-start.10
  269.7 33.1 %all-to-all-start = ((s16[16,528,128]{2,1,0:T(8,128)(2,1)}), s16[16,528,128]{2,1,0:T(8,128)(2,1)}, u32[]{:S(2)}, u32[]{:S(2)}) async-start(s16[16,528,128]{2,1,0:T(8,128)(2,1)} %bitcast.88), calls=%async_computation | async-start | bytes 4325376 | tf_op jit(solution)/shard_map/all_to_all | solution.py:404

commit v4 on v3

--- a/solution.py
+++ b/solution.py
@@ -311,17 +311,14 @@
     def twin(value):
         return lax.ppermute(value, "row", row_perm(0, 0, 1))
 
-    z_up, z_down = ring_sides(genotypes, "row", row_perm)
     turned = genotypes.T
     across = lax.ppermute(turned, "col", col_perm(0, 1))
+    z_up, z_down = ring_sides(genotypes, "row", row_perm)
     y_up, y_down = ring_sides(turned, "col", col_perm)
     own_twin = twin(genotypes)
 
     leading = running[:NB, 0, 0, :] + dot0(genotypes, genotypes) * inv_snp
     lower = jnp.linalg.cholesky(leading)
-    inverse = lax.linalg.triangular_solve(
-        lower, jnp.eye(NB, dtype=jnp.float32), left_side=True, lower=True
-    )
 
     away = (jnp.arange(4, dtype=jnp.uint32) - z) & 3
     slots = jnp.where(away == 0, 0, jnp.where(away == 1, 2, jnp.where(away == 2, 3, 1)))
@@ -329,8 +326,8 @@
     pick = slots[0] * 4 + (core * 2 + x_lo).astype(jnp.int32)
     pick = jnp.stack([pick, *[jnp.int32(step) for step in STEP_OF_SLOT]])
 
-    late, across, inverse, old_panel, pick, slots = lax.optimization_barrier(
-        (genotypes, across, inverse, running[:, 0, 0, :], pick, slots)
+    late, across, lower, pick, slots = lax.optimization_barrier(
+        (genotypes, across, lower, pick, slots)
     )
     beside = lax.ppermute(late, "row", row_perm(0, 1, 0))
     y_up_across, y_down_across = ring_sides(across, "col", col_perm)
@@ -338,10 +335,14 @@
     y_opposite = ring_relay(y_up, y_down, "col", col_perm)
     z_up_twin, z_down_twin = twin(z_up), twin(z_down)
 
+    inverse = lax.linalg.triangular_solve(
+        lower, jnp.eye(NB, dtype=jnp.float32), left_side=True, lower=True
+    )
     heard = sum(lax.ppermute(inverse, "row", [(0, d * NX * NC)]) for d in range(1, NZ))
     inverse = jnp.where(z == 0, inverse, heard)
     z_up_side, z_down_side = ring_sides(beside, "row", row_perm)
     heard = lax.ppermute(inverse, "row", [(d * NX * NC, d * NX * NC + NC) for d in range(NZ)])
+    heard, old_panel = lax.optimization_barrier((heard, running[:, 0, 0, :]))
     inverse = jnp.where(x_lo == 0, inverse, heard)
     z_opposite_side = lax.ppermute(z_opposite, "row", row_perm(0, 1, 0))
     y_opposite_across = ring_relay(y_up_across, y_down_across, "col", col_perm)

time: 309 us -> 317 us (1.026)
  waiting for transfers between devices: 63.1 us -> 72.7 us
    ppermute x1, waiting for transfers between devices: 1.03 us -> 10 us  [compute(): across = lax.ppermute(turned, 'col', col_perm(0, 1))]
  transfers between devices with their start and end apart: 45 -> 45, of which waited for: 12 -> 13; matrix products, arithmetic and copies ran while one was open for 12% -> 12% of each run, Pallas kernels for 20% -> 20%
where the time goes in v4:
time: 317 us; the launch traced here: 315 us
  starting transfers between devices  109 us (34%)
  Pallas kernels  87 us (27%)
  waiting for transfers between devices  72.7 us (23%)
  other arithmetic  26.9 us (8%)
  local copies, waits for them, and re-layouts  18.5 us (6%)
    pallas_call x4, Pallas kernels, product(): pl.pallas_call(lambda *refs: product_kernel(*refs, plane=plane), grid_spe...  46.2 us
    ppermute x8, starting transfers between devices, twin(): return lax.ppermute(value, 'row', row_perm(0, 0, 1))  37.5 us
    all_to_all x2, waiting for transfers between devices, compute(): lax.all_to_all(packed.reshape(16, CODED_ROWS, 128), 'row', split_axis=0,...  23.5 us
    pallas_call x2, Pallas kernels, epilogue(): pl.pallas_call(lambda *refs: epilogue_kernel(*refs, part=part, inv_snp=1....  22.1 us
    all_to_all x2, starting transfers between devices, compute(): lax.all_to_all(packed.reshape(16, CODED_ROWS, 128), 'row', split_axis=0,...  13.2 us
    another operation x3, other arithmetic, compute(): lower = jnp.linalg.cholesky(leading)  12.4 us
    ppermute x4, starting transfers between devices, ring_sides(): lax.ppermute(shard, axis, perm(-1))  11.9 us
    ppermute x3, waiting for transfers between devices, ring_relay(): bottom = lax.ppermute(down[half:], axis, perm(-1))  10.1 us
  transfers between devices with their start and end apart: 45, of which 13 were waited for; matrix products, arithmetic and copies ran while one was open for 12% of the time, Pallas kernels for 20%

profile of v4, /device:TPU:1, one launch (start us, length us, event | category | flops | bytes accessed | tf_op | source)
XLA Modules:
  0.0 315.2 jit_solution(15288868761539553979)
XLA Ops:
  0.0 1.7 copy.19
  1.7 3.6 %collective-permute-start = (bf16[128,5120]{1,0:T(8,128)(2,1)S(1)}, bf16[128,5120]{1,0:T(8,128)(2,1)}, u32[]{:S(2)}, u32[]{:S(2)}) collective-permute-start(bf16[128,5120]{1,0:T(8,128)(2,1)S(1)} %bitcast.75), channel_id=1, source_target_pairs={{0,1},{1,0},{2,3},{3,2},{4,5},{5,4},{6,7},{7,6},{8,9},{9,8},{10,11... | collective-permute-start | bytes 3932168 | tf_op jit(solution)/shard_map/ppermute | solution.py:315
  5.4 2.7 collective-permute-start.3
  9.7 11.7 %cholesky.20 = f32[128,128]{1,0:T(8,128)S(1)} custom-call(f32[128,128]{1,0:T(8,128)S(1)} %fusion.5), custom_call_target="Cholesky" | custom-call | tf_op jit(solution)/shard_map/jit(cholesky)/cholesky | solution.py:321
  23.5 10.0 %collective-permute-done.refs_4_.refs_2_ = bf16[128,5120]{1,0:T(8,128)(2,1)} collective-permute-done((bf16[128,5120]{1,0:T(8,128)(2,1)S(1)}, bf16[128,5120]{1,0:T(8,128)(2,1)}, u32[]{:S(2)}, u32[]{:S(2)}) %collective-permute-start) | collective-permute-done | bytes 1310752 | tf_op jit(solution)/shard_map/ppermute | solution.py:315
  33.6 9.8 %custom-call.6 = f32[1,128,128]{1,2,0:T(8,128)S(1)} custom-call(f32[1,128,128]{2,1,0:T(8,128)S(1)} %select_bitcast_fusion), custom_call_target="InvertDiagBlocksLowerTriangular" | custom-call | tf_op jit(solution)/shard_map/triangular_solve | solution.py:338
  45.7 4.2 %collective-permute-start.21 = (bf16[5120,128]{1,0:T(8,128)(2,1)S(1)}, bf16[5120,128]{1,0:T(8,128)(2,1)}, u32[]{:S(2)}, u32[]{:S(2)}) collective-permute-start(bf16[5120,128]{1,0:T(8,128)(2,1)S(1)} %copy-done), channel_id=1, source_target_pairs={{0,96},{8,104},{16,112},{24,120},{32,0},{40,8},{48,16},{56,24},{64... | collective-permute-start | bytes 3932168 | tf_op jit(solution)/shard_map/ppermute | solution.py:36
  49.8 7.9 %collective-permute-start.15 = (bf16[5120,128]{1,0:T(8,128)(2,1)S(1)}, bf16[5120,128]{1,0:T(8,128)(2,1)}, u32[]{:S(2)}, u32[]{:S(2)}) collective-permute-start(bf16[5120,128]{1,0:T(8,128)(2,1)S(1)} %copy-done), channel_id=1, source_target_pairs={{0,8},{8,0},{16,24},{24,16},{32,40},{40,32},{48,56},{56,48},{64,72... | collective-permute-start | bytes 3932168 | tf_op jit(solution)/shard_map/ppermute | solution.py:312
  58.4 1.1 slice.71
  59.5 2.8 collective-permute-start.6
  62.3 1.1 slice.70
  63.6 1.9 slice.61
  65.5 6.4 %collective-permute-done.21.refs_21_.refs_19_ = bf16[5120,128]{1,0:T(8,128)(2,1)} collective-permute-done((bf16[5120,128]{1,0:T(8,128)(2,1)S(1)}, bf16[5120,128]{1,0:T(8,128)(2,1)}, u32[]{:S(2)}, u32[]{:S(2)}) %collective-permute-start.21) | collective-permute-done | bytes 1310752 | tf_op jit(solution)/shard_map/ppermute | solution.py:36
  71.9 1.3 collective-permute-start.13
  73.1 1.1 slice.75
  74.3 3.6 %collective-permute-start.26 = (bf16[2560,128]{1,0:T(8,128)(2,1)S(1)}, bf16[2560,128]{1,0:T(8,128)(2,1)S(1)}, u32[]{:S(2)}, u32[]{:S(2)}) collective-permute-start(bf16[2560,128]{1,0:T(8,128)(2,1)S(1)} %slice.75), channel_id=1, source_target_pairs={{0,96},{8,104},{16,112},{24,120},{32,0},{40,8},{48,16},{56,24},{64... | collective-permute-start | bytes 1966088 | tf_op jit(solution)/shard_map/ppermute | solution.py:42
  77.9 1.1 slice.74
  79.0 1.1 collective-permute-start.25
  80.1 2.2 collective-permute-done.13
  82.3 2.7 collective-permute-start.14
  85.0 2.7 collective-permute-start.4
  88.3 6.3 %collective-permute-start.23 = (bf16[5120,128]{1,0:T(8,128)(2,1)}, bf16[5120,128]{1,0:T(8,128)(2,1)S(1)}, u32[]{:S(2)}, u32[]{:S(2)}) collective-permute-start(bf16[5120,128]{1,0:T(8,128)(2,1)} %collective-permute-done.21.refs_21_.refs_19_), channel_id=1, source_target_pairs={{0,8},{8,0},{16,24},{24,16},{32,40},{40,32},{48,56},{56,48},{64,72... | collective-permute-start | bytes 3932168 | tf_op jit(solution)/shard_map/ppermute | solution.py:312
  94.7 4.9 %collective-permute-start.19 = (bf16[5120,128]{1,0:T(8,128)(2,1)}, bf16[5120,128]{1,0:T(8,128)(2,1)}, u32[]{:S(2)}, u32[]{:S(2)}) collective-permute-start(bf16[5120,128]{1,0:T(8,128)(2,1)} %collective-permute-done.17.refs_17_.refs_15_), channel_id=1, source_target_pairs={{0,8},{8,0},{16,24},{24,16},{32,40},{40,32},{48,56},{56,48},{64,72... | collective-permute-start | bytes 3932168 | tf_op jit(solution)/shard_map/ppermute | solution.py:312
  101.4 9.1 %collective-permute-done.14.refs_14_.refs_12_ = bf16[5120,128]{1,0:T(8,128)(2,1)} collective-permute-done((bf16[5120,128]{1,0:T(8,128)(2,1)S(1)}, bf16[5120,128]{1,0:T(8,128)(2,1)}, u32[]{:S(2)}, u32[]{:S(2)}) %collective-permute-start.14) | collective-permute-done | bytes 1310752 | tf_op jit(solution)/shard_map/ppermute | solution.py:332
  110.4 2.3 collective-permute-start.27
  113.0 2.3 collective-permute-start.22
  116.1 1.0 copy-done.3
  117.1 1.1 copy-done.4
  118.2 2.6 collective-permute-start.8
  120.8 9.5 %collective-permute-done.8.refs_12_.refs_10_ = bf16[64,5120]{1,0:T(8,128)(2,1)S(1)} collective-permute-done((bf16[64,5120]{1,0:T(8,128)(2,1)S(1)}, bf16[64,5120]{1,0:T(8,128)(2,1)S(1)}, u32[]{:S(2)}, u32[]{:S(2)}) %collective-permute-start.8) | collective-permute-done | bytes 655392 | tf_op jit(solution)/shard_map/ppermute | solution.py:42
  130.3 5.4 %collective-permute-start.28 = (bf16[5120,128]{1,0:T(8,128)(2,1)}, bf16[5120,128]{1,0:T(8,128)(2,1)S(1)}, u32[]{:S(2)}, u32[]{:S(2)}) collective-permute-start(bf16[5120,128]{1,0:T(8,128)(2,1)} %constant_dynamic-update-slice_fusion.refs_25_.refs_23_), channel_id=1, source_target_pairs={{0,8},{8,0},{16,24},{24,16},{32,40},{40,32},{48,56},{56,48},{64,72... | collective-permute-start | bytes 3932168 | tf_op jit(solution)/shard_map/ppermute | solution.py:312
  135.7 3.4 %collective-permute-start.16 = (bf16[5120,128]{1,0:T(8,128)(2,1)}, bf16[5120,128]{1,0:T(8,128)(2,1)}, u32[]{:S(2)}, u32[]{:S(2)}) collective-permute-start(bf16[5120,128]{1,0:T(8,128)(2,1)} %collective-permute-done.14.refs_14_.refs_12_), channel_id=1, source_target_pairs={{0,8},{8,0},{16,24},{24,16},{32,40},{40,32},{48,56},{56,48},{64,72... | collective-permute-start | bytes 3932168 | tf_op jit(solution)/shard_map/ppermute | solution.py:312
  139.2 3.6 %collective-permute-start.29 = (bf16[5120,128]{1,0:T(8,128)(2,1)S(1)}, bf16[5120,128]{1,0:T(8,128)(2,1)}, u32[]{:S(2)}, u32[]{:S(2)}) collective-permute-start(bf16[5120,128]{1,0:T(8,128)(2,1)S(1)} %collective-permute-done.27.refs_26_.refs_24_), channel_id=1, source_target_pairs={{0,8},{8,0},{16,24},{24,16},{32,40},{40,32},{48,56},{56,48},{64,72... | collective-permute-start | bytes 3932168 | tf_op jit(solution)/shard_map/ppermute | solution.py:312
  142.8 1.8 collective-permute-start.24
  144.6 4.1 %collective-permute-start.20 = (bf16[5120,128]{1,0:T(8,128)(2,1)}, bf16[5120,128]{1,0:T(8,128)(2,1)}, u32[]{:S(2)}, u32[]{:S(2)}) collective-permute-start(bf16[5120,128]{1,0:T(8,128)(2,1)} %collective-permute-done.18.refs_18_.refs_16_), channel_id=1, source_target_pairs={{0,8},{8,0},{16,24},{24,16},{32,40},{40,32},{48,56},{56,48},{64,72... | collective-permute-start | bytes 3932168 | tf_op jit(solution)/shard_map/ppermute | solution.py:312
  149.4 2.3 collective-permute-done.20.refs_20_.refs_18_
  151.8 10.1 %panel.1 = f32[1024,128]{1,0:T(8,128)} custom-call(s32[5]{0:T(128)} %stack.47.refs_0_, f32[1024,128]{1,0:T(8,128)} %bitcast.89, f32[128,128]{1,0:T(8,128)} %broadcast_select_fusion.1.refs_2_, bf16[128,5120]{1,0:T(8,128)(2,1)} %bitcast.78, bf16[128,5120]{1,0:T(8,128)(2,1)} %collective-permute-done.refs_4_.refs_2_, ...), custom_call_target="tpu_custom_call" | custom-call | tf_op jit(solution)/shard_map/panel/pallas_call | solution.py:250
  161.8 1.1 fusion.11
  163.1 4.1 %collective-permute-start.30 = (f32[4,128,128]{1,2,0:T(8,128)S(1)}, f32[4,128,128]{1,2,0:T(8,128)S(1)}, u32[]{:S(2)}, u32[]{:S(2)}) collective-permute-start(f32[4,128,128]{1,2,0:T(8,128)S(1)} %bitcast.100), channel_id=1, source_target_pairs={{0,1},{8,9},{16,17},{24,25},{32,33},{40,41},{48,49},{56,57},{64,65... | collective-permute-start | bytes 786440 | tf_op jit(solution)/shard_map/ppermute | solution.py:364
  167.3 5.1 %collective-permute-done.30 = f32[4,128,128]{1,2,0:T(8,128)S(1)} collective-permute-done((f32[4,128,128]{1,2,0:T(8,128)S(1)}, f32[4,128,128]{1,2,0:T(8,128)S(1)}, u32[]{:S(2)}, u32[]{:S(2)}) %collective-permute-start.30) | collective-permute-done | bytes 262176 | tf_op jit(solution)/shard_map/ppermute | solution.py:364
  172.4 1.3 collective-permute-start.32
  173.7 1.3 collective-permute-start.33
  175.0 1.3 collective-permute-start.31
  176.5 1.2 collective-permute-done.31
  177.8 3.8 %collective-permute-start.34 = (f32[128,128]{0,1:T(8,128)S(1)}, f32[128,128]{0,1:T(8,128)S(1)}, u32[]{:S(2)}, u32[]{:S(2)}) collective-permute-start(f32[128,128]{0,1:T(8,128)S(1)} %get-tuple-element.60), channel_id=1, source_target_pairs={{0,1},{1,0},{2,3},{3,2},{4,5},{5,4},{6,7},{7,6},{8,9},{9,8},{10,11... | collective-permute-start | bytes 196616 | tf_op jit(solution)/shard_map/ppermute | solution.py:370
  181.7 2.0 collective-permute-start.40
  183.7 1.3 collective-permute-start.41
  185.6 11.4 %product.6.refs_3_.refs_7_ = f32[1024,512]{1,0:T(8,128)} custom-call(s32[4]{0:T(128)} %copy-done.11, bf16[128,5120]{1,0:T(8,128)(2,1)} %bitcast.79, bf16[128,5120]{1,0:T(8,128)(2,1)} %collective-permute-done.refs_4_.refs_2_, bf16[128,5120]{1,0:T(8,128)(2,1)} %collective-permute-done.1.refs_5_.refs_3_, bf16[128,5120]{1,0:T(8,128)(2,1)} %copy-done.3, ...), custom_call_target="tpu_custom_call" | custom-call | tf_op jit(solution)/shard_map/product/pallas_call | solution.py:199
  197.1 11.5 %product.5.refs_2_.refs_6_ = f32[1024,512]{1,0:T(8,128)} custom-call(s32[4]{0:T(128)} %copy-done.11, bf16[128,5120]{1,0:T(8,128)(2,1)} %bitcast.80, bf16[128,5120]{1,0:T(8,128)(2,1)} %collective-permute-done.refs_4_.refs_2_, bf16[128,5120]{1,0:T(8,128)(2,1)} %collective-permute-done.1.refs_5_.refs_3_, bf16[128,5120]{1,0:T(8,128)(2,1)} %copy-done.3, ...), custom_call_target="tpu_custom_call" | custom-call | tf_op jit(solution)/shard_map/product/pallas_call | solution.py:199
  209.3 3.5 %collective-permute-start.36 = (f32[2,128,128]{1,2,0:T(8,128)S(1)}, f32[2,128,128]{1,2,0:T(8,128)S(1)}, u32[]{:S(2)}, u32[]{:S(2)}) collective-permute-start(f32[2,128,128]{1,2,0:T(8,128)S(1)} %pad_maximum_fusion.3), channel_id=1, source_target_pairs={{0,6},{1,7},{2,0},{3,1},{4,2},{5,3},{6,4},{7,5},{8,14},{9,15},{10,... | collective-permute-start | bytes 393224 | tf_op jit(solution)/shard_map/ppermute | solution.py:47
  213.1 4.1 %collective-permute-start.42 = (f32[4,2,128,128]{2,1,0,3:T(2,128)S(1)}, f32[4,2,128,128]{2,1,0,3:T(2,128)S(1)}, u32[]{:S(2)}, u32[]{:S(2)}) collective-permute-start(f32[4,2,128,128]{2,1,0,3:T(2,128)S(1)} %pad_maximum_fusion.2), channel_id=1, source_target_pairs={{0,8},{8,0},{16,24},{24,16},{32,40},{40,32},{48,56},{56,48},{64,72... | collective-permute-start | bytes 1572872 | tf_op jit(solution)/shard_map/ppermute | solution.py:374
  217.2 1.8 collective-permute-done.35
  219.1 1.0 copy.26
  221.9 1.3 pad_maximum_fusion.refs_9_.refs_10_
  223.2 11.1 %epilogue.2 = s16[8448,128]{1,0:T(8,128)(2,1)} custom-call(s32[57]{0:T(128)} %convert_element_type.36.refs_0_, f32[1024,16,128]{2,1,0:T(8,128)} %bitcast.71, f32[1024,512]{1,0:T(8,128)} %product.5.refs_2_.refs_6_, f32[1024,512]{1,0:T(8,128)} %product.6.refs_3_.refs_7_, f32[1024,128]{1,0:T(8,128)} %bitcast.83, f32[1024,16,128]{2,1,0:T(8,128)} %bitcast.72, ...), custom_call_target="tpu_custom_call" | custom-call | tf_op jit(solution)/shard_map/epilogue/pallas_call | solution.py:118
  234.3 7.8 %all-to-all-start.1 = ((s16[16,528,128]{2,1,0:T(8,128)(2,1)}), s16[16,528,128]{2,1,0:T(8,128)(2,1)S(1)}, u32[]{:S(2)}, u32[]{:S(2)}) async-start(s16[16,528,128]{2,1,0:T(8,128)(2,1)} %bitcast.87), calls=%async_computation.1 | async-start | bytes 4325376 | tf_op jit(solution)/shard_map/all_to_all | solution.py:405
  242.1 11.8 %product.4.refs_2_.refs_6_ = f32[1024,512]{1,0:T(8,128)} custom-call(s32[4]{0:T(128)} %copy-done.11, bf16[128,5120]{1,0:T(8,128)(2,1)} %bitcast.81, bf16[128,5120]{1,0:T(8,128)(2,1)} %collective-permute-done.refs_4_.refs_2_, bf16[128,5120]{1,0:T(8,128)(2,1)} %collective-permute-done.1.refs_5_.refs_3_, bf16[128,5120]{1,0:T(8,128)(2,1)} %copy-done.3, ...), custom_call_target="tpu_custom_call" | custom-call | tf_op jit(solution)/shard_map/product/pallas_call | solution.py:199
  253.9 11.5 %product.7.refs_3_.refs_7_ = f32[1024,512]{1,0:T(8,128)} custom-call(s32[4]{0:T(128)} %copy-done.11, bf16[128,5120]{1,0:T(8,128)(2,1)} %bitcast.82, bf16[128,5120]{1,0:T(8,128)(2,1)} %collective-permute-done.refs_4_.refs_2_, bf16[128,5120]{1,0:T(8,128)(2,1)} %collective-permute-done.1.refs_5_.refs_3_, bf16[128,5120]{1,0:T(8,128)(2,1)} %copy-done.3, ...), custom_call_target="tpu_custom_call" | custom-call | tf_op jit(solution)/shard_map/product/pallas_call | solution.py:199
  265.4 11.0 %epilogue.3 = s16[8448,128]{1,0:T(8,128)(2,1)} custom-call(s32[57]{0:T(128)} %convert_element_type.36.refs_0_, f32[1024,16,128]{2,1,0:T(8,128)} %bitcast.73, f32[1024,512]{1,0:T(8,128)} %product.4.refs_2_.refs_6_, f32[1024,512]{1,0:T(8,128)} %product.7.refs_3_.refs_7_, f32[1024,128]{1,0:T(8,128)} %bitcast.85, f32[1024,16,128]{2,1,0:T(8,128)} %bitcast.74, ...), custom_call_target="tpu_custom_call" | custom-call | tf_op jit(solution)/shard_map/epilogue/pallas_call | solution.py:118
  276.4 1.4 copy-done.10
  277.8 5.4 %all-to-all-start = ((s16[16,528,128]{2,1,0:T(8,128)(2,1)}), s16[16,528,128]{2,1,0:T(8,128)(2,1)}, u32[]{:S(2)}, u32[]{:S(2)}) async-start(s16[16,528,128]{2,1,0:T(8,128)(2,1)} %bitcast.88), calls=%async_computation | async-start | bytes 4325376 | tf_op jit(solution)/shard_map/all_to_all | solution.py:405
  283.2 4.3 %unpack.2.refs_0_ = f32[1024,16,128]{2,1,0:T(8,128)} custom-call(s16[16,528,128]{2,1,0:T(8,128)(2,1)} %copy-done.10), custom_call_target="tpu_custom_call" | custom-call | tf_op jit(solution)/shard_map/unpack/pallas_call | solution.py:286
  287.5 23.5 %all-to-all-done.coded = s16[16,528,128]{2,1,0:T(8,128)(2,1)} async-done(((s16[16,528,128]{2,1,0:T(8,128)(2,1)}), s16[16,528,128]{2,1,0:T(8,128)(2,1)}, u32[]{:S(2)}, u32[]{:S(2)}) %all-to-all-start) | async-done | bytes 2162720 | tf_op jit(solution)/shard_map/all_to_all | solution.py:405
  310.9 4.3 %unpack.3 = f32[1024,16,128]{2,1,0:T(8,128)} custom-call(s16[16,528,128]{2,1,0:T(8,128)(2,1)} %all-to-all-done.coded, f32[1024,16,128]{2,1,0:T(8,128)} %unpack.2.refs_0_), custom_call_target="tpu_custom_call", output_to_operand_aliasing={{}: (1, {})} | custom-call | tf_op jit(solution)/shard_map/unpack/pallas_call | solution.py:286
  (113 shorter events, 14.9 us)
Async XLA Ops:
  0.0 9.0 %copy-start = (bf16[5120,128]{1,0:T(8,128)(2,1)S(1)}, bf16[5120,128]{1,0:T(8,128)(2,1)}, u32[]{:S(2)}) copy-start(bf16[5120,128]{1,0:T(8,128)(2,1)} %refs_11_.7) | copy-start | bytes 3932164
  1.7 7.9 %copy-start.1 = (bf16[5120,128]{0,1:T(8,128)(2,1)}, bf16[5120,128]{0,1:T(8,128)(2,1)S(1)}, u32[]{:S(2)}) copy-start(bf16[5120,128]{0,1:T(8,128)(2,1)S(1)} %copy.19) | copy-start | bytes 3932164
  1.7 31.8 %collective-permute-start = (bf16[128,5120]{1,0:T(8,128)(2,1)S(1)}, bf16[128,5120]{1,0:T(8,128)(2,1)}, u32[]{:S(2)}, u32[]{:S(2)}) collective-permute-start(bf16[128,5120]{1,0:T(8,128)(2,1)S(1)} %bitcast.75), channel_id=1, source_target_pairs={{0,1},{1,0},{2,3},{3,2},{4,5},{5,4},{6,7},{7,6},{8,9},{9,8},{10,11... | collective-permute-start | bytes 3932168 | tf_op jit(solution)/shard_map/ppermute | solution.py:315
  5.4 52.4 %collective-permute-start.3 = (bf16[128,5120]{1,0:T(8,128)(2,1)S(1)}, bf16[128,5120]{1,0:T(8,128)(2,1)}, u32[]{:S(2)}, u32[]{:S(2)}) collective-permute-start(bf16[128,5120]{1,0:T(8,128)(2,1)S(1)} %bitcast.76), channel_id=1, source_target_pairs={{0,6},{1,7},{2,0},{3,1},{4,2},{5,3},{6,4},{7,5},{8,14},{9,15},{10,... | collective-permute-start | bytes 3932168 | tf_op jit(solution)/shard_map/ppermute | solution.py:36
  8.1 51.4 %collective-permute-start.1 = (bf16[128,5120]{1,0:T(8,128)(2,1)S(1)}, bf16[128,5120]{1,0:T(8,128)(2,1)}, u32[]{:S(2)}, u32[]{:S(2)}) collective-permute-start(bf16[128,5120]{1,0:T(8,128)(2,1)S(1)} %bitcast.77), channel_id=1, source_target_pairs={{0,2},{1,3},{2,4},{3,5},{4,6},{5,7},{6,0},{7,1},{8,10},{9,11},{10,... | collective-permute-start | bytes 3932168 | tf_op jit(solution)/shard_map/ppermute | solution.py:36
  22.8 162.1 %copy-start.11 = (s32[4]{0:T(128)}, s32[4]{0:T(128)S(1)}, u32[]{:S(2)}) copy-start(s32[4]{0:T(128)S(1)} %compare_select_fusion.2.refs_0_) | copy-start | bytes 52
  43.6 2.0 collective-permute-start.11
  44.3 5.5 %collective-permute-start.10 = (f32[128,128]{1,0:T(8,128)S(1)}, f32[128,128]{1,0:T(8,128)S(1)}, u32[]{:S(2)}, u32[]{:S(2)}) collective-permute-start(f32[128,128]{1,0:T(8,128)S(1)} %fusion.3), channel_id=1, source_target_pairs={{0,64},{1,65},{2,66},{3,67},{4,68},{5,69},{6,70},{7,71}} | collective-permute-start | bytes 196616 | tf_op jit(solution)/shard_map/ppermute | solution.py:341
  45.0 4.8 %collective-permute-start.9 = (f32[128,128]{1,0:T(8,128)S(1)}, f32[128,128]{1,0:T(8,128)S(1)}, u32[]{:S(2)}, u32[]{:S(2)}) collective-permute-start(f32[128,128]{1,0:T(8,128)S(1)} %fusion.3), channel_id=1, source_target_pairs={{0,32},{1,33},{2,34},{3,35},{4,36},{5,37},{6,38},{7,39}} | collective-permute-start | bytes 196616 | tf_op jit(solution)/shard_map/ppermute | solution.py:341
  45.7 26.2 %collective-permute-start.21 = (bf16[5120,128]{1,0:T(8,128)(2,1)S(1)}, bf16[5120,128]{1,0:T(8,128)(2,1)}, u32[]{:S(2)}, u32[]{:S(2)}) collective-permute-start(bf16[5120,128]{1,0:T(8,128)(2,1)S(1)} %copy-done), channel_id=1, source_target_pairs={{0,96},{8,104},{16,112},{24,120},{32,0},{40,8},{48,16},{56,24},{64... | collective-permute-start | bytes 3932168 | tf_op jit(solution)/shard_map/ppermute | solution.py:36
  49.8 24.5 %collective-permute-start.17 = (bf16[5120,128]{1,0:T(8,128)(2,1)S(1)}, bf16[5120,128]{1,0:T(8,128)(2,1)}, u32[]{:S(2)}, u32[]{:S(2)}) collective-permute-start(bf16[5120,128]{1,0:T(8,128)(2,1)S(1)} %copy-done), channel_id=1, source_target_pairs={{0,32},{8,40},{16,48},{24,56},{32,64},{40,72},{48,80},{56,88},{64,... | collective-permute-start | bytes 3932168 | tf_op jit(solution)/shard_map/ppermute | solution.py:36
  49.8 29.2 %collective-permute-start.15 = (bf16[5120,128]{1,0:T(8,128)(2,1)S(1)}, bf16[5120,128]{1,0:T(8,128)(2,1)}, u32[]{:S(2)}, u32[]{:S(2)}) collective-permute-start(bf16[5120,128]{1,0:T(8,128)(2,1)S(1)} %copy-done), channel_id=1, source_target_pairs={{0,8},{8,0},{16,24},{24,16},{32,40},{40,32},{48,56},{56,48},{64,72... | collective-permute-start | bytes 3932168 | tf_op jit(solution)/shard_map/ppermute | solution.py:312
  57.7 5.8 %collective-permute-start.12 = (f32[128,128]{1,0:T(8,128)S(1)}, f32[128,128]{1,0:T(8,128)S(1)}, u32[]{:S(2)}, u32[]{:S(2)}) collective-permute-start(f32[128,128]{1,0:T(8,128)S(1)} %add_select_fusion), channel_id=1, source_target_pairs={{0,16},{32,48},{64,80},{96,112},{1,17},{33,49},{65,81},{97,113},{2... | collective-permute-start | bytes 196616 | tf_op jit(solution)/shard_map/ppermute | solution.py:344
  59.5 25.4 %collective-permute-start.6 = (bf16[64,5120]{1,0:T(8,128)(2,1)S(1)}, bf16[64,5120]{1,0:T(8,128)(2,1)S(1)}, u32[]{:S(2)}, u32[]{:S(2)}) collective-permute-start(bf16[64,5120]{1,0:T(8,128)(2,1)S(1)} %slice.71), channel_id=1, source_target_pairs={{0,6},{1,7},{2,0},{3,1},{4,2},{5,3},{6,4},{7,5},{8,14},{9,15},{10,... | collective-permute-start | bytes 1966088 | tf_op jit(solution)/shard_map/ppermute | solution.py:42
  63.5 24.2 %collective-permute-start.5 = (bf16[64,5120]{1,0:T(8,128)(2,1)S(1)}, bf16[64,5120]{1,0:T(8,128)(2,1)}, u32[]{:S(2)}, u32[]{:S(2)}) collective-permute-start(bf16[64,5120]{1,0:T(8,128)(2,1)S(1)} %slice.70), channel_id=1, source_target_pairs={{0,2},{1,3},{2,4},{3,5},{4,6},{5,7},{6,0},{7,1},{8,10},{9,11},{10,... | collective-permute-start | bytes 1966088 | tf_op jit(solution)/shard_map/ppermute | solution.py:41
  71.9 10.4 %collective-permute-start.13 = (f32[128,128]{1,0:T(8,128)S(1)}, f32[128,128]{1,0:T(8,128)S(1)}, u32[]{:S(2)}, u32[]{:S(2)}) collective-permute-start(f32[128,128]{1,0:T(8,128)S(1)} %broadcast_select_fusion), channel_id=1, source_target_pairs={{0,8},{16,24},{32,40},{48,56},{64,72},{80,88},{96,104},{112,120},{... | collective-permute-start | bytes 196616 | tf_op jit(solution)/shard_map/ppermute | solution.py:349
  74.3 14.0 %collective-permute-start.26 = (bf16[2560,128]{1,0:T(8,128)(2,1)S(1)}, bf16[2560,128]{1,0:T(8,128)(2,1)S(1)}, u32[]{:S(2)}, u32[]{:S(2)}) collective-permute-start(bf16[2560,128]{1,0:T(8,128)(2,1)S(1)} %slice.75), channel_id=1, source_target_pairs={{0,96},{8,104},{16,112},{24,120},{32,0},{40,8},{48,16},{56,24},{64... | collective-permute-start | bytes 1966088 | tf_op jit(solution)/shard_map/ppermute | solution.py:42
  79.0 15.6 %collective-permute-start.25 = (bf16[2560,128]{1,0:T(8,128)(2,1)S(1)}, bf16[2560,128]{1,0:T(8,128)(2,1)S(1)}, u32[]{:S(2)}, u32[]{:S(2)}) collective-permute-start(bf16[2560,128]{1,0:T(8,128)(2,1)S(1)} %slice.74), channel_id=1, source_target_pairs={{0,32},{8,40},{16,48},{24,56},{32,64},{40,72},{48,80},{56,88},{64,... | collective-permute-start | bytes 1966088 | tf_op jit(solution)/shard_map/ppermute | solution.py:41
  82.3 28.2 %collective-permute-start.14 = (bf16[5120,128]{1,0:T(8,128)(2,1)S(1)}, bf16[5120,128]{1,0:T(8,128)(2,1)}, u32[]{:S(2)}, u32[]{:S(2)}) collective-permute-start(bf16[5120,128]{1,0:T(8,128)(2,1)S(1)} %copy-done), channel_id=1, source_target_pairs={{0,16},{8,24},{16,0},{24,8},{32,48},{40,56},{48,32},{56,40},{64,80... | collective-permute-start | bytes 3932168 | tf_op jit(solution)/shard_map/ppermute | solution.py:332
  85.0 31.1 %copy-start.7 = (bf16[64,5120]{1,0:T(8,128)(2,1)}, bf16[64,5120]{1,0:T(8,128)(2,1)S(1)}, u32[]{:S(2)}) copy-start(bf16[64,5120]{1,0:T(8,128)(2,1)S(1)} %collective-permute-done.6.refs_10_.refs_8_) | copy-start | bytes 1966084
  85.0 28.0 %collective-permute-start.4 = (bf16[128,5120]{1,0:T(8,128)(2,1)}, bf16[128,5120]{1,0:T(8,128)(2,1)S(1)}, u32[]{:S(2)}, u32[]{:S(2)}) collective-permute-start(bf16[128,5120]{1,0:T(8,128)(2,1)} %collective-permute-done.refs_4_.refs_2_), channel_id=1, source_target_pairs={{0,6},{1,7},{2,0},{3,1},{4,2},{5,3},{6,4},{7,5},{8,14},{9,15},{10,... | collective-permute-start | bytes 3932168 | tf_op jit(solution)/shard_map/ppermute | solution.py:36
  87.7 28.3 %collective-permute-start.2 = (bf16[128,5120]{1,0:T(8,128)(2,1)}, bf16[128,5120]{1,0:T(8,128)(2,1)S(1)}, u32[]{:S(2)}, u32[]{:S(2)}) collective-permute-start(bf16[128,5120]{1,0:T(8,128)(2,1)} %collective-permute-done.refs_4_.refs_2_), channel_id=1, source_target_pairs={{0,2},{1,3},{2,4},{3,5},{4,6},{5,7},{6,0},{7,1},{8,10},{9,11},{10,... | collective-permute-start | bytes 3932168 | tf_op jit(solution)/shard_map/ppermute | solution.py:36
  88.3 28.8 %collective-permute-start.23 = (bf16[5120,128]{1,0:T(8,128)(2,1)}, bf16[5120,128]{1,0:T(8,128)(2,1)S(1)}, u32[]{:S(2)}, u32[]{:S(2)}) collective-permute-start(bf16[5120,128]{1,0:T(8,128)(2,1)} %collective-permute-done.21.refs_21_.refs_19_), channel_id=1, source_target_pairs={{0,8},{8,0},{16,24},{24,16},{32,40},{40,32},{48,56},{56,48},{64,72... | collective-permute-start | bytes 3932168 | tf_op jit(solution)/shard_map/ppermute | solution.py:312
  94.7 26.1 %collective-permute-start.19 = (bf16[5120,128]{1,0:T(8,128)(2,1)}, bf16[5120,128]{1,0:T(8,128)(2,1)}, u32[]{:S(2)}, u32[]{:S(2)}) collective-permute-start(bf16[5120,128]{1,0:T(8,128)(2,1)} %collective-permute-done.17.refs_17_.refs_15_), channel_id=1, source_target_pairs={{0,8},{8,0},{16,24},{24,16},{32,40},{40,32},{48,56},{56,48},{64,72... | collective-permute-start | bytes 3932168 | tf_op jit(solution)/shard_map/ppermute | solution.py:312
  110.4 28.7 %collective-permute-start.27 = (bf16[5120,128]{1,0:T(8,128)(2,1)}, bf16[5120,128]{1,0:T(8,128)(2,1)S(1)}, u32[]{:S(2)}, u32[]{:S(2)}) collective-permute-start(bf16[5120,128]{1,0:T(8,128)(2,1)} %constant_dynamic-update-slice_fusion.refs_25_.refs_23_), channel_id=1, source_target_pairs={{0,16},{8,24},{16,0},{24,8},{32,48},{40,56},{48,32},{56,40},{64,80... | collective-permute-start | bytes 3932168 | tf_op jit(solution)/shard_map/ppermute | solution.py:347
  113.0 3.1 copy-start.2
  113.0 29.8 %collective-permute-start.22 = (bf16[5120,128]{1,0:T(8,128)(2,1)}, bf16[5120,128]{1,0:T(8,128)(2,1)}, u32[]{:S(2)}, u32[]{:S(2)}) collective-permute-start(bf16[5120,128]{1,0:T(8,128)(2,1)} %collective-permute-done.14.refs_14_.refs_12_), channel_id=1, source_target_pairs={{0,96},{8,104},{16,112},{24,120},{32,0},{40,8},{48,16},{56,24},{64... | collective-permute-start | bytes 3932168 | tf_op jit(solution)/shard_map/ppermute | solution.py:36
  116.0 1.1 copy-start.3
  116.0 28.6 %collective-permute-start.18 = (bf16[5120,128]{1,0:T(8,128)(2,1)}, bf16[5120,128]{1,0:T(8,128)(2,1)}, u32[]{:S(2)}, u32[]{:S(2)}) collective-permute-start(bf16[5120,128]{1,0:T(8,128)(2,1)} %collective-permute-done.14.refs_14_.refs_12_), channel_id=1, source_target_pairs={{0,32},{8,40},{16,48},{24,56},{32,64},{40,72},{48,80},{56,88},{64,... | collective-permute-start | bytes 3932168 | tf_op jit(solution)/shard_map/ppermute | solution.py:36
  117.1 1.1 copy-start.4
  118.2 12.1 %collective-permute-start.8 = (bf16[64,5120]{1,0:T(8,128)(2,1)S(1)}, bf16[64,5120]{1,0:T(8,128)(2,1)S(1)}, u32[]{:S(2)}, u32[]{:S(2)}) collective-permute-start(bf16[64,5120]{1,0:T(8,128)(2,1)S(1)} %slice.73), channel_id=1, source_target_pairs={{0,6},{1,7},{2,0},{3,1},{4,2},{5,3},{6,4},{7,5},{8,14},{9,15},{10,... | collective-permute-start | bytes 1966088 | tf_op jit(solution)/shard_map/ppermute | solution.py:42
  120.8 14.9 %collective-permute-start.7 = (bf16[64,5120]{1,0:T(8,128)(2,1)S(1)}, bf16[64,5120]{1,0:T(8,128)(2,1)S(1)}, u32[]{:S(2)}, u32[]{:S(2)}) collective-permute-start(bf16[64,5120]{1,0:T(8,128)(2,1)S(1)} %slice.72), channel_id=1, source_target_pairs={{0,2},{1,3},{2,4},{3,5},{4,6},{5,7},{6,0},{7,1},{8,10},{9,11},{10,... | collective-permute-start | bytes 1966088 | tf_op jit(solution)/shard_map/ppermute | solution.py:41
  130.3 21.4 %copy-start.8 = (bf16[64,5120]{1,0:T(8,128)(2,1)}, bf16[64,5120]{1,0:T(8,128)(2,1)S(1)}, u32[]{:S(2)}) copy-start(bf16[64,5120]{1,0:T(8,128)(2,1)S(1)} %collective-permute-done.8.refs_12_.refs_10_) | copy-start | bytes 1966084
  130.3 19.1 %collective-permute-start.28 = (bf16[5120,128]{1,0:T(8,128)(2,1)}, bf16[5120,128]{1,0:T(8,128)(2,1)S(1)}, u32[]{:S(2)}, u32[]{:S(2)}) collective-permute-start(bf16[5120,128]{1,0:T(8,128)(2,1)} %constant_dynamic-update-slice_fusion.refs_25_.refs_23_), channel_id=1, source_target_pairs={{0,8},{8,0},{16,24},{24,16},{32,40},{40,32},{48,56},{56,48},{64,72... | collective-permute-start | bytes 3932168 | tf_op jit(solution)/shard_map/ppermute | solution.py:312
  135.7 3.4 %copy-start.9 = (bf16[64,5120]{1,0:T(8,128)(2,1)}, bf16[64,5120]{1,0:T(8,128)(2,1)S(1)}, u32[]{:S(2)}) copy-start(bf16[64,5120]{1,0:T(8,128)(2,1)S(1)} %collective-permute-done.7.refs_11_.refs_9_) | copy-start | bytes 1966084
  135.7 13.6 %collective-permute-start.16 = (bf16[5120,128]{1,0:T(8,128)(2,1)}, bf16[5120,128]{1,0:T(8,128)(2,1)}, u32[]{:S(2)}, u32[]{:S(2)}) collective-permute-start(bf16[5120,128]{1,0:T(8,128)(2,1)} %collective-permute-done.14.refs_14_.refs_12_), channel_id=1, source_target_pairs={{0,8},{8,0},{16,24},{24,16},{32,40},{40,32},{48,56},{56,48},{64,72... | collective-permute-start | bytes 3932168 | tf_op jit(solution)/shard_map/ppermute | solution.py:312
  139.2 12.6 %copy-start.5 = (bf16[5120,128]{1,0:T(8,128)(2,1)}, bf16[5120,128]{1,0:T(8,128)(2,1)S(1)}, u32[]{:S(2)}) copy-start(bf16[5120,128]{1,0:T(8,128)(2,1)S(1)} %collective-permute-done.27.refs_26_.refs_24_) | copy-start | bytes 3932164
  139.2 10.2 %collective-permute-start.29 = (bf16[5120,128]{1,0:T(8,128)(2,1)S(1)}, bf16[5120,128]{1,0:T(8,128)(2,1)}, u32[]{:S(2)}, u32[]{:S(2)}) collective-permute-start(bf16[5120,128]{1,0:T(8,128)(2,1)S(1)} %collective-permute-done.27.refs_26_.refs_24_), channel_id=1, source_target_pairs={{0,8},{8,0},{16,24},{24,16},{32,40},{40,32},{48,56},{56,48},{64,72... | collective-permute-start | bytes 3932168 | tf_op jit(solution)/shard_map/ppermute | solution.py:312
  142.8 6.6 %collective-permute-start.24 = (bf16[5120,128]{1,0:T(8,128)(2,1)}, bf16[5120,128]{1,0:T(8,128)(2,1)}, u32[]{:S(2)}, u32[]{:S(2)}) collective-permute-start(bf16[5120,128]{1,0:T(8,128)(2,1)} %collective-permute-done.22.refs_22_.refs_20_), channel_id=1, source_target_pairs={{0,8},{8,0},{16,24},{24,16},{32,40},{40,32},{48,56},{56,48},{64,72... | collective-permute-start | bytes 3932168 | tf_op jit(solution)/shard_map/ppermute | solution.py:312
  144.6 7.1 %collective-permute-start.20 = (bf16[5120,128]{1,0:T(8,128)(2,1)}, bf16[5120,128]{1,0:T(8,128)(2,1)}, u32[]{:S(2)}, u32[]{:S(2)}) collective-permute-start(bf16[5120,128]{1,0:T(8,128)(2,1)} %collective-permute-done.18.refs_18_.refs_16_), channel_id=1, source_target_pairs={{0,8},{8,0},{16,24},{24,16},{32,40},{40,32},{48,56},{56,48},{64,72... | collective-permute-start | bytes 3932168 | tf_op jit(solution)/shard_map/ppermute | solution.py:312
  149.4 2.4 copy-start.6
  162.9 13.4 %copy-start.12 = (s32[16]{0:T(128)S(1)}, s32[16]{0:T(128)}, u32[]{:S(2)}) copy-start(s32[16]{0:T(128)} %param.5) | copy-start | bytes 196
  163.1 9.3 %collective-permute-start.30 = (f32[4,128,128]{1,2,0:T(8,128)S(1)}, f32[4,128,128]{1,2,0:T(8,128)S(1)}, u32[]{:S(2)}, u32[]{:S(2)}) collective-permute-start(f32[4,128,128]{1,2,0:T(8,128)S(1)} %bitcast.100), channel_id=1, source_target_pairs={{0,1},{8,9},{16,17},{24,25},{32,33},{40,41},{48,49},{56,57},{64,65... | collective-permute-start | bytes 786440 | tf_op jit(solution)/shard_map/ppermute | solution.py:364
  172.4 4.0 %collective-permute-start.32 = (f32[128,128]{0,1:T(8,128)S(1)}, f32[128,128]{0,1:T(8,128)S(1)}, u32[]{:S(2)}, u32[]{:S(2)}) collective-permute-start(f32[128,128]{0,1:T(8,128)S(1)} %get-tuple-element.65), channel_id=1, source_target_pairs={{0,4},{1,5},{8,12},{9,13},{16,20},{17,21},{24,28},{25,29},{32,36},... | collective-permute-start | bytes 196616 | tf_op jit(solution)/shard_map/ppermute | solution.py:367
  173.7 2.7 collective-permute-start.33
  175.0 2.6 collective-permute-start.31
  177.7 3.9 %collective-permute-start.38 = (f32[128,128]{0,1:T(8,128)S(1)}, f32[128,128]{0,1:T(8,128)S(1)}, u32[]{:S(2)}, u32[]{:S(2)}) collective-permute-start(f32[128,128]{0,1:T(8,128)S(1)} %get-tuple-element.60), channel_id=1, source_target_pairs={{0,16},{8,24},{16,0},{24,8},{32,48},{40,56},{48,32},{56,40},{64,80... | collective-permute-start | bytes 196616 | tf_op jit(solution)/shard_map/ppermute | solution.py:372
  177.8 30.8 %collective-permute-start.34 = (f32[128,128]{0,1:T(8,128)S(1)}, f32[128,128]{0,1:T(8,128)S(1)}, u32[]{:S(2)}, u32[]{:S(2)}) collective-permute-start(f32[128,128]{0,1:T(8,128)S(1)} %get-tuple-element.60), channel_id=1, source_target_pairs={{0,1},{1,0},{2,3},{3,2},{4,5},{5,4},{6,7},{7,6},{8,9},{9,8},{10,11... | collective-permute-start | bytes 196616 | tf_op jit(solution)/shard_map/ppermute | solution.py:370
  181.7 31.1 %collective-permute-start.40 = (f32[2,128,128]{1,0,2:T(2,128)S(1)}, f32[2,128,128]{1,0,2:T(2,128)S(1)}, u32[]{:S(2)}, u32[]{:S(2)}) collective-permute-start(f32[2,128,128]{1,0,2:T(2,128)S(1)} %get-tuple-element.69), channel_id=1, source_target_pairs={{0,96},{8,104},{16,112},{24,120},{32,0},{40,8},{48,16},{56,24},{64... | collective-permute-start | bytes 393224 | tf_op jit(solution)/shard_map/ppermute | solution.py:47
  183.7 29.2 %collective-permute-start.39 = (f32[2,128,128]{1,0,2:T(2,128)S(1)}, f32[2,128,128]{1,0,2:T(2,128)S(1)}, u32[]{:S(2)}, u32[]{:S(2)}) collective-permute-start(f32[2,128,128]{1,0,2:T(2,128)S(1)} %get-tuple-element.69), channel_id=1, source_target_pairs={{0,32},{8,40},{16,48},{24,56},{32,64},{40,72},{48,80},{56,88},{64,... | collective-permute-start | bytes 393224 | tf_op jit(solution)/shard_map/ppermute | solution.py:47
  183.7 29.2 %collective-permute-start.41 = (f32[2,128,128]{1,0,2:T(2,128)S(1)}, f32[2,128,128]{1,0,2:T(2,128)S(1)}, u32[]{:S(2)}, u32[]{:S(2)}) collective-permute-start(f32[2,128,128]{1,0,2:T(2,128)S(1)} %get-tuple-element.69), channel_id=1, source_target_pairs={{0,64},{8,72},{16,80},{24,88},{32,96},{40,104},{48,112},{56,120},{... | collective-permute-start | bytes 393224 | tf_op jit(solution)/shard_map/ppermute | solution.py:47
  208.6 10.5 %collective-permute-start.37 = (f32[2,128,128]{1,2,0:T(8,128)S(1)}, f32[2,128,128]{1,2,0:T(8,128)S(1)}, u32[]{:S(2)}, u32[]{:S(2)}) collective-permute-start(f32[2,128,128]{1,2,0:T(8,128)S(1)} %pad_maximum_fusion.3), channel_id=1, source_target_pairs={{0,4},{1,5},{2,6},{3,7},{4,0},{5,1},{6,2},{7,3},{8,12},{9,13},{10,... | collective-permute-start | bytes 393224 | tf_op jit(solution)/shard_map/ppermute | solution.py:47
  209.3 9.7 %collective-permute-start.36 = (f32[2,128,128]{1,2,0:T(8,128)S(1)}, f32[2,128,128]{1,2,0:T(8,128)S(1)}, u32[]{:S(2)}, u32[]{:S(2)}) collective-permute-start(f32[2,128,128]{1,2,0:T(8,128)S(1)} %pad_maximum_fusion.3), channel_id=1, source_target_pairs={{0,6},{1,7},{2,0},{3,1},{4,2},{5,3},{6,4},{7,5},{8,14},{9,15},{10,... | collective-permute-start | bytes 393224 | tf_op jit(solution)/shard_map/ppermute | solution.py:47
  212.8 6.2 %collective-permute-start.35 = (f32[2,128,128]{1,2,0:T(8,128)S(1)}, f32[2,128,128]{1,2,0:T(8,128)S(1)}, u32[]{:S(2)}, u32[]{:S(2)}) collective-permute-start(f32[2,128,128]{1,2,0:T(8,128)S(1)} %pad_maximum_fusion.3), channel_id=1, source_target_pairs={{0,2},{1,3},{2,4},{3,5},{4,6},{5,7},{6,0},{7,1},{8,10},{9,11},{10,... | collective-permute-start | bytes 393224 | tf_op jit(solution)/shard_map/ppermute | solution.py:47
  213.1 7.3 %collective-permute-start.42 = (f32[4,2,128,128]{2,1,0,3:T(2,128)S(1)}, f32[4,2,128,128]{2,1,0,3:T(2,128)S(1)}, u32[]{:S(2)}, u32[]{:S(2)}) collective-permute-start(f32[4,2,128,128]{2,1,0,3:T(2,128)S(1)} %pad_maximum_fusion.2), channel_id=1, source_target_pairs={{0,8},{8,0},{16,24},{24,16},{32,40},{40,32},{48,56},{56,48},{64,72... | collective-permute-start | bytes 1572872 | tf_op jit(solution)/shard_map/ppermute | solution.py:374
  234.3 42.2 %all-to-all-start.1 = ((s16[16,528,128]{2,1,0:T(8,128)(2,1)}), s16[16,528,128]{2,1,0:T(8,128)(2,1)S(1)}, u32[]{:S(2)}, u32[]{:S(2)}) async-start(s16[16,528,128]{2,1,0:T(8,128)(2,1)} %bitcast.87), calls=%async_computation.1 | async-start | bytes 4325376 | tf_op jit(solution)/shard_map/all_to_all | solution.py:405
  276.4 1.4 copy-start.10
  277.8 33.1 %all-to-all-start = ((s16[16,528,128]{2,1,0:T(8,128)(2,1)}), s16[16,528,128]{2,1,0:T(8,128)(2,1)}, u32[]{:S(2)}, u32[]{:S(2)}) async-start(s16[16,528,128]{2,1,0:T(8,128)(2,1)} %bitcast.88), calls=%async_computation | async-start | bytes 4325376 | tf_op jit(solution)/shard_map/all_to_all | solution.py:405

commit v5 on v4

--- a/solution.py
+++ b/solution.py
@@ -272,7 +272,7 @@
 
 def unpack_kernel(coded, *refs):
     out = refs[-1]
-    for source in range(4):
+    for source in range(8):
         code = coded[source, TILE_ROWS * HALF :, :].astype(jnp.float32)
         scale = jnp.exp(code * LOG_STEP) * (1.0 / LEVELS)
         for a in range(PAIRS):
@@ -285,12 +285,12 @@
     begun = [] if before is None else [before]
     return pl.pallas_call(
         unpack_kernel,
-        grid=(4,),
+        grid=(2,),
         in_specs=[
-            pl.BlockSpec((4, CODED_ROWS, 128), lambda i: (i, 0, 0)),
+            pl.BlockSpec((8, CODED_ROWS, 128), lambda i: (i, 0, 0)),
             *[pl.BlockSpec(memory_space=pl.ANY)] * len(begun),
         ],
-        out_specs=pl.BlockSpec((4 * TILE_ROWS, HALF, 128), lambda i: (i, part, 0)),
+        out_specs=pl.BlockSpec((8 * TILE_ROWS, HALF, 128), lambda i: (i, part, 0)),
         out_shape=jax.ShapeDtypeStruct((16 * TILE_ROWS, 2 * HALF, 128), jnp.float32),
         input_output_aliases={1: 0} if begun else {},
         name="unpack",

time: 317 us -> 316 us (level)
  transfers between devices with their start and end apart: 45 -> 45, of which waited for: 13 -> 13; matrix products, arithmetic and copies ran while one was open for 12% -> 12% of each run, Pallas kernels for 20% -> 19%
where the time goes in v5:
time: 316 us; the launch traced here: 314 us
  starting transfers between devices  109 us (34%)
  Pallas kernels  85.3 us (27%)
  waiting for transfers between devices  73.5 us (23%)
  other arithmetic  26.9 us (9%)
  local copies, waits for them, and re-layouts  18.5 us (6%)
    pallas_call x4, Pallas kernels, product(): pl.pallas_call(lambda *refs: product_kernel(*refs, plane=plane), grid_spe...  46.2 us
    ppermute x8, starting transfers between devices, twin(): return lax.ppermute(value, 'row', row_perm(0, 0, 1))  37.5 us
    all_to_all x2, waiting for transfers between devices, compute(): lax.all_to_all(packed.reshape(16, CODED_ROWS, 128), 'row', split_axis=0,...  24.3 us
    pallas_call x2, Pallas kernels, epilogue(): pl.pallas_call(lambda *refs: epilogue_kernel(*refs, part=part, inv_snp=1....  22.1 us
    all_to_all x2, starting transfers between devices, compute(): lax.all_to_all(packed.reshape(16, CODED_ROWS, 128), 'row', split_axis=0,...  13.2 us
    another operation x3, other arithmetic, compute(): lower = jnp.linalg.cholesky(leading)  12.4 us
    ppermute x4, starting transfers between devices, ring_sides(): lax.ppermute(shard, axis, perm(-1))  11.9 us
    ppermute x3, waiting for transfers between devices, ring_relay(): bottom = lax.ppermute(down[half:], axis, perm(-1))  10.1 us
  transfers between devices with their start and end apart: 45, of which 13 were waited for; matrix products, arithmetic and copies ran while one was open for 12% of the time, Pallas kernels for 19%

profile of v5, /device:TPU:1, one launch (start us, length us, event | category | flops | bytes accessed | tf_op | source)
XLA Modules:
  0.0 314.4 jit_solution(7422968606450507484)
XLA Ops:
  0.0 1.7 copy.19
  1.7 3.6 %collective-permute-start = (bf16[128,5120]{1,0:T(8,128)(2,1)S(1)}, bf16[128,5120]{1,0:T(8,128)(2,1)}, u32[]{:S(2)}, u32[]{:S(2)}) collective-permute-start(bf16[128,5120]{1,0:T(8,128)(2,1)S(1)} %bitcast.75), channel_id=1, source_target_pairs={{0,1},{1,0},{2,3},{3,2},{4,5},{5,4},{6,7},{7,6},{8,9},{9,8},{10,11... | collective-permute-start | bytes 3932168 | tf_op jit(solution)/shard_map/ppermute | solution.py:315
  5.4 2.7 collective-permute-start.3
  9.7 11.7 %cholesky.20 = f32[128,128]{1,0:T(8,128)S(1)} custom-call(f32[128,128]{1,0:T(8,128)S(1)} %fusion.5), custom_call_target="Cholesky" | custom-call | tf_op jit(solution)/shard_map/jit(cholesky)/cholesky | solution.py:321
  23.5 10.0 %collective-permute-done.refs_4_.refs_2_ = bf16[128,5120]{1,0:T(8,128)(2,1)} collective-permute-done((bf16[128,5120]{1,0:T(8,128)(2,1)S(1)}, bf16[128,5120]{1,0:T(8,128)(2,1)}, u32[]{:S(2)}, u32[]{:S(2)}) %collective-permute-start) | collective-permute-done | bytes 1310752 | tf_op jit(solution)/shard_map/ppermute | solution.py:315
  33.6 9.8 %custom-call.6 = f32[1,128,128]{1,2,0:T(8,128)S(1)} custom-call(f32[1,128,128]{2,1,0:T(8,128)S(1)} %select_bitcast_fusion), custom_call_target="InvertDiagBlocksLowerTriangular" | custom-call | tf_op jit(solution)/shard_map/triangular_solve | solution.py:338
  45.7 4.2 %collective-permute-start.21 = (bf16[5120,128]{1,0:T(8,128)(2,1)S(1)}, bf16[5120,128]{1,0:T(8,128)(2,1)}, u32[]{:S(2)}, u32[]{:S(2)}) collective-permute-start(bf16[5120,128]{1,0:T(8,128)(2,1)S(1)} %copy-done), channel_id=1, source_target_pairs={{0,96},{8,104},{16,112},{24,120},{32,0},{40,8},{48,16},{56,24},{64... | collective-permute-start | bytes 3932168 | tf_op jit(solution)/shard_map/ppermute | solution.py:36
  49.8 7.9 %collective-permute-start.15 = (bf16[5120,128]{1,0:T(8,128)(2,1)S(1)}, bf16[5120,128]{1,0:T(8,128)(2,1)}, u32[]{:S(2)}, u32[]{:S(2)}) collective-permute-start(bf16[5120,128]{1,0:T(8,128)(2,1)S(1)} %copy-done), channel_id=1, source_target_pairs={{0,8},{8,0},{16,24},{24,16},{32,40},{40,32},{48,56},{56,48},{64,72... | collective-permute-start | bytes 3932168 | tf_op jit(solution)/shard_map/ppermute | solution.py:312
  58.4 1.1 slice.71
  59.5 2.8 collective-permute-start.6
  62.3 1.1 slice.70
  63.6 1.9 slice.61
  65.5 6.4 %collective-permute-done.21.refs_21_.refs_19_ = bf16[5120,128]{1,0:T(8,128)(2,1)} collective-permute-done((bf16[5120,128]{1,0:T(8,128)(2,1)S(1)}, bf16[5120,128]{1,0:T(8,128)(2,1)}, u32[]{:S(2)}, u32[]{:S(2)}) %collective-permute-start.21) | collective-permute-done | bytes 1310752 | tf_op jit(solution)/shard_map/ppermute | solution.py:36
  71.9 1.3 collective-permute-start.13
  73.1 1.1 slice.75
  74.3 3.6 %collective-permute-start.26 = (bf16[2560,128]{1,0:T(8,128)(2,1)S(1)}, bf16[2560,128]{1,0:T(8,128)(2,1)S(1)}, u32[]{:S(2)}, u32[]{:S(2)}) collective-permute-start(bf16[2560,128]{1,0:T(8,128)(2,1)S(1)} %slice.75), channel_id=1, source_target_pairs={{0,96},{8,104},{16,112},{24,120},{32,0},{40,8},{48,16},{56,24},{64... | collective-permute-start | bytes 1966088 | tf_op jit(solution)/shard_map/ppermute | solution.py:42
  77.9 1.1 slice.74
  79.0 1.1 collective-permute-start.25
  80.1 2.2 collective-permute-done.13
  82.3 2.7 collective-permute-start.14
  85.0 2.7 collective-permute-start.4
  88.3 6.3 %collective-permute-start.23 = (bf16[5120,128]{1,0:T(8,128)(2,1)}, bf16[5120,128]{1,0:T(8,128)(2,1)S(1)}, u32[]{:S(2)}, u32[]{:S(2)}) collective-permute-start(bf16[5120,128]{1,0:T(8,128)(2,1)} %collective-permute-done.21.refs_21_.refs_19_), channel_id=1, source_target_pairs={{0,8},{8,0},{16,24},{24,16},{32,40},{40,32},{48,56},{56,48},{64,72... | collective-permute-start | bytes 3932168 | tf_op jit(solution)/shard_map/ppermute | solution.py:312
  94.7 4.9 %collective-permute-start.19 = (bf16[5120,128]{1,0:T(8,128)(2,1)}, bf16[5120,128]{1,0:T(8,128)(2,1)}, u32[]{:S(2)}, u32[]{:S(2)}) collective-permute-start(bf16[5120,128]{1,0:T(8,128)(2,1)} %collective-permute-done.17.refs_17_.refs_15_), channel_id=1, source_target_pairs={{0,8},{8,0},{16,24},{24,16},{32,40},{40,32},{48,56},{56,48},{64,72... | collective-permute-start | bytes 3932168 | tf_op jit(solution)/shard_map/ppermute | solution.py:312
  101.4 9.1 %collective-permute-done.14.refs_14_.refs_12_ = bf16[5120,128]{1,0:T(8,128)(2,1)} collective-permute-done((bf16[5120,128]{1,0:T(8,128)(2,1)S(1)}, bf16[5120,128]{1,0:T(8,128)(2,1)}, u32[]{:S(2)}, u32[]{:S(2)}) %collective-permute-start.14) | collective-permute-done | bytes 1310752 | tf_op jit(solution)/shard_map/ppermute | solution.py:332
  110.4 2.3 collective-permute-start.27
  113.0 2.3 collective-permute-start.22
  116.1 1.0 copy-done.3
  117.1 1.1 copy-done.4
  118.2 2.6 collective-permute-start.8
  120.8 9.5 %collective-permute-done.8.refs_12_.refs_10_ = bf16[64,5120]{1,0:T(8,128)(2,1)S(1)} collective-permute-done((bf16[64,5120]{1,0:T(8,128)(2,1)S(1)}, bf16[64,5120]{1,0:T(8,128)(2,1)S(1)}, u32[]{:S(2)}, u32[]{:S(2)}) %collective-permute-start.8) | collective-permute-done | bytes 655392 | tf_op jit(solution)/shard_map/ppermute | solution.py:42
  130.3 5.4 %collective-permute-start.28 = (bf16[5120,128]{1,0:T(8,128)(2,1)}, bf16[5120,128]{1,0:T(8,128)(2,1)S(1)}, u32[]{:S(2)}, u32[]{:S(2)}) collective-permute-start(bf16[5120,128]{1,0:T(8,128)(2,1)} %constant_dynamic-update-slice_fusion.refs_25_.refs_23_), channel_id=1, source_target_pairs={{0,8},{8,0},{16,24},{24,16},{32,40},{40,32},{48,56},{56,48},{64,72... | collective-permute-start | bytes 3932168 | tf_op jit(solution)/shard_map/ppermute | solution.py:312
  135.7 3.4 %collective-permute-start.16 = (bf16[5120,128]{1,0:T(8,128)(2,1)}, bf16[5120,128]{1,0:T(8,128)(2,1)}, u32[]{:S(2)}, u32[]{:S(2)}) collective-permute-start(bf16[5120,128]{1,0:T(8,128)(2,1)} %collective-permute-done.14.refs_14_.refs_12_), channel_id=1, source_target_pairs={{0,8},{8,0},{16,24},{24,16},{32,40},{40,32},{48,56},{56,48},{64,72... | collective-permute-start | bytes 3932168 | tf_op jit(solution)/shard_map/ppermute | solution.py:312
  139.2 3.6 %collective-permute-start.29 = (bf16[5120,128]{1,0:T(8,128)(2,1)S(1)}, bf16[5120,128]{1,0:T(8,128)(2,1)}, u32[]{:S(2)}, u32[]{:S(2)}) collective-permute-start(bf16[5120,128]{1,0:T(8,128)(2,1)S(1)} %collective-permute-done.27.refs_26_.refs_24_), channel_id=1, source_target_pairs={{0,8},{8,0},{16,24},{24,16},{32,40},{40,32},{48,56},{56,48},{64,72... | collective-permute-start | bytes 3932168 | tf_op jit(solution)/shard_map/ppermute | solution.py:312
  142.8 1.8 collective-permute-start.24
  144.6 4.1 %collective-permute-start.20 = (bf16[5120,128]{1,0:T(8,128)(2,1)}, bf16[5120,128]{1,0:T(8,128)(2,1)}, u32[]{:S(2)}, u32[]{:S(2)}) collective-permute-start(bf16[5120,128]{1,0:T(8,128)(2,1)} %collective-permute-done.18.refs_18_.refs_16_), channel_id=1, source_target_pairs={{0,8},{8,0},{16,24},{24,16},{32,40},{40,32},{48,56},{56,48},{64,72... | collective-permute-start | bytes 3932168 | tf_op jit(solution)/shard_map/ppermute | solution.py:312
  149.4 2.3 collective-permute-done.20.refs_20_.refs_18_
  151.8 10.1 %panel.1 = f32[1024,128]{1,0:T(8,128)} custom-call(s32[5]{0:T(128)} %stack.47.refs_0_, f32[1024,128]{1,0:T(8,128)} %bitcast.89, f32[128,128]{1,0:T(8,128)} %broadcast_select_fusion.1.refs_2_, bf16[128,5120]{1,0:T(8,128)(2,1)} %bitcast.78, bf16[128,5120]{1,0:T(8,128)(2,1)} %collective-permute-done.refs_4_.refs_2_, ...), custom_call_target="tpu_custom_call" | custom-call | tf_op jit(solution)/shard_map/panel/pallas_call | solution.py:250
  161.8 1.1 fusion.11
  163.1 4.1 %collective-permute-start.30 = (f32[4,128,128]{1,2,0:T(8,128)S(1)}, f32[4,128,128]{1,2,0:T(8,128)S(1)}, u32[]{:S(2)}, u32[]{:S(2)}) collective-permute-start(f32[4,128,128]{1,2,0:T(8,128)S(1)} %bitcast.100), channel_id=1, source_target_pairs={{0,1},{8,9},{16,17},{24,25},{32,33},{40,41},{48,49},{56,57},{64,65... | collective-permute-start | bytes 786440 | tf_op jit(solution)/shard_map/ppermute | solution.py:364
  167.3 5.1 %collective-permute-done.30 = f32[4,128,128]{1,2,0:T(8,128)S(1)} collective-permute-done((f32[4,128,128]{1,2,0:T(8,128)S(1)}, f32[4,128,128]{1,2,0:T(8,128)S(1)}, u32[]{:S(2)}, u32[]{:S(2)}) %collective-permute-start.30) | collective-permute-done | bytes 262176 | tf_op jit(solution)/shard_map/ppermute | solution.py:364
  172.4 1.3 collective-permute-start.32
  173.7 1.3 collective-permute-start.33
  175.0 1.3 collective-permute-start.31
  176.5 1.2 collective-permute-done.31
  177.8 3.8 %collective-permute-start.34 = (f32[128,128]{0,1:T(8,128)S(1)}, f32[128,128]{0,1:T(8,128)S(1)}, u32[]{:S(2)}, u32[]{:S(2)}) collective-permute-start(f32[128,128]{0,1:T(8,128)S(1)} %get-tuple-element.60), channel_id=1, source_target_pairs={{0,1},{1,0},{2,3},{3,2},{4,5},{5,4},{6,7},{7,6},{8,9},{9,8},{10,11... | collective-permute-start | bytes 196616 | tf_op jit(solution)/shard_map/ppermute | solution.py:370
  181.7 2.0 collective-permute-start.40
  183.7 1.3 collective-permute-start.41
  185.6 11.4 %product.6.refs_3_.refs_7_ = f32[1024,512]{1,0:T(8,128)} custom-call(s32[4]{0:T(128)} %copy-done.11, bf16[128,5120]{1,0:T(8,128)(2,1)} %bitcast.79, bf16[128,5120]{1,0:T(8,128)(2,1)} %collective-permute-done.refs_4_.refs_2_, bf16[128,5120]{1,0:T(8,128)(2,1)} %collective-permute-done.1.refs_5_.refs_3_, bf16[128,5120]{1,0:T(8,128)(2,1)} %copy-done.3, ...), custom_call_target="tpu_custom_call" | custom-call | tf_op jit(solution)/shard_map/product/pallas_call | solution.py:199
  197.1 11.5 %product.5.refs_2_.refs_6_ = f32[1024,512]{1,0:T(8,128)} custom-call(s32[4]{0:T(128)} %copy-done.11, bf16[128,5120]{1,0:T(8,128)(2,1)} %bitcast.80, bf16[128,5120]{1,0:T(8,128)(2,1)} %collective-permute-done.refs_4_.refs_2_, bf16[128,5120]{1,0:T(8,128)(2,1)} %collective-permute-done.1.refs_5_.refs_3_, bf16[128,5120]{1,0:T(8,128)(2,1)} %copy-done.3, ...), custom_call_target="tpu_custom_call" | custom-call | tf_op jit(solution)/shard_map/product/pallas_call | solution.py:199
  209.3 3.5 %collective-permute-start.36 = (f32[2,128,128]{1,2,0:T(8,128)S(1)}, f32[2,128,128]{1,2,0:T(8,128)S(1)}, u32[]{:S(2)}, u32[]{:S(2)}) collective-permute-start(f32[2,128,128]{1,2,0:T(8,128)S(1)} %pad_maximum_fusion.3), channel_id=1, source_target_pairs={{0,6},{1,7},{2,0},{3,1},{4,2},{5,3},{6,4},{7,5},{8,14},{9,15},{10,... | collective-permute-start | bytes 393224 | tf_op jit(solution)/shard_map/ppermute | solution.py:47
  213.1 4.1 %collective-permute-start.42 = (f32[4,2,128,128]{2,1,0,3:T(2,128)S(1)}, f32[4,2,128,128]{2,1,0,3:T(2,128)S(1)}, u32[]{:S(2)}, u32[]{:S(2)}) collective-permute-start(f32[4,2,128,128]{2,1,0,3:T(2,128)S(1)} %pad_maximum_fusion.2), channel_id=1, source_target_pairs={{0,8},{8,0},{16,24},{24,16},{32,40},{40,32},{48,56},{56,48},{64,72... | collective-permute-start | bytes 1572872 | tf_op jit(solution)/shard_map/ppermute | solution.py:374
  217.2 1.8 collective-permute-done.35
  219.1 1.0 copy.26
  221.9 1.3 pad_maximum_fusion.refs_9_.refs_10_
  223.2 11.1 %epilogue.2 = s16[8448,128]{1,0:T(8,128)(2,1)} custom-call(s32[57]{0:T(128)} %convert_element_type.36.refs_0_, f32[1024,16,128]{2,1,0:T(8,128)} %bitcast.71, f32[1024,512]{1,0:T(8,128)} %product.5.refs_2_.refs_6_, f32[1024,512]{1,0:T(8,128)} %product.6.refs_3_.refs_7_, f32[1024,128]{1,0:T(8,128)} %bitcast.83, f32[1024,16,128]{2,1,0:T(8,128)} %bitcast.72, ...), custom_call_target="tpu_custom_call" | custom-call | tf_op jit(solution)/shard_map/epilogue/pallas_call | solution.py:118
  234.3 7.8 %all-to-all-start.1 = ((s16[16,528,128]{2,1,0:T(8,128)(2,1)}), s16[16,528,128]{2,1,0:T(8,128)(2,1)S(1)}, u32[]{:S(2)}, u32[]{:S(2)}) async-start(s16[16,528,128]{2,1,0:T(8,128)(2,1)} %bitcast.87), calls=%async_computation.1 | async-start | bytes 4325376 | tf_op jit(solution)/shard_map/all_to_all | solution.py:405
  242.1 11.8 %product.4.refs_2_.refs_6_ = f32[1024,512]{1,0:T(8,128)} custom-call(s32[4]{0:T(128)} %copy-done.11, bf16[128,5120]{1,0:T(8,128)(2,1)} %bitcast.81, bf16[128,5120]{1,0:T(8,128)(2,1)} %collective-permute-done.refs_4_.refs_2_, bf16[128,5120]{1,0:T(8,128)(2,1)} %collective-permute-done.1.refs_5_.refs_3_, bf16[128,5120]{1,0:T(8,128)(2,1)} %copy-done.3, ...), custom_call_target="tpu_custom_call" | custom-call | tf_op jit(solution)/shard_map/product/pallas_call | solution.py:199
  253.9 11.5 %product.7.refs_3_.refs_7_ = f32[1024,512]{1,0:T(8,128)} custom-call(s32[4]{0:T(128)} %copy-done.11, bf16[128,5120]{1,0:T(8,128)(2,1)} %bitcast.82, bf16[128,5120]{1,0:T(8,128)(2,1)} %collective-permute-done.refs_4_.refs_2_, bf16[128,5120]{1,0:T(8,128)(2,1)} %collective-permute-done.1.refs_5_.refs_3_, bf16[128,5120]{1,0:T(8,128)(2,1)} %copy-done.3, ...), custom_call_target="tpu_custom_call" | custom-call | tf_op jit(solution)/shard_map/product/pallas_call | solution.py:199
  265.4 11.0 %epilogue.3 = s16[8448,128]{1,0:T(8,128)(2,1)} custom-call(s32[57]{0:T(128)} %convert_element_type.36.refs_0_, f32[1024,16,128]{2,1,0:T(8,128)} %bitcast.73, f32[1024,512]{1,0:T(8,128)} %product.4.refs_2_.refs_6_, f32[1024,512]{1,0:T(8,128)} %product.7.refs_3_.refs_7_, f32[1024,128]{1,0:T(8,128)} %bitcast.85, f32[1024,16,128]{2,1,0:T(8,128)} %bitcast.74, ...), custom_call_target="tpu_custom_call" | custom-call | tf_op jit(solution)/shard_map/epilogue/pallas_call | solution.py:118
  276.4 1.4 copy-done.10
  277.8 5.4 %all-to-all-start = ((s16[16,528,128]{2,1,0:T(8,128)(2,1)}), s16[16,528,128]{2,1,0:T(8,128)(2,1)}, u32[]{:S(2)}, u32[]{:S(2)}) async-start(s16[16,528,128]{2,1,0:T(8,128)(2,1)} %bitcast.88), calls=%async_computation | async-start | bytes 4325376 | tf_op jit(solution)/shard_map/all_to_all | solution.py:405
  283.2 3.5 %unpack.2.refs_0_ = f32[1024,16,128]{2,1,0:T(8,128)} custom-call(s16[16,528,128]{2,1,0:T(8,128)(2,1)} %copy-done.10), custom_call_target="tpu_custom_call" | custom-call | tf_op jit(solution)/shard_map/unpack/pallas_call | solution.py:286
  286.6 24.3 %all-to-all-done.coded = s16[16,528,128]{2,1,0:T(8,128)(2,1)} async-done(((s16[16,528,128]{2,1,0:T(8,128)(2,1)}), s16[16,528,128]{2,1,0:T(8,128)(2,1)}, u32[]{:S(2)}, u32[]{:S(2)}) %all-to-all-start) | async-done | bytes 2162720 | tf_op jit(solution)/shard_map/all_to_all | solution.py:405
  310.9 3.5 %unpack.3 = f32[1024,16,128]{2,1,0:T(8,128)} custom-call(s16[16,528,128]{2,1,0:T(8,128)(2,1)} %all-to-all-done.coded, f32[1024,16,128]{2,1,0:T(8,128)} %unpack.2.refs_0_), custom_call_target="tpu_custom_call", output_to_operand_aliasing={{}: (1, {})} | custom-call | tf_op jit(solution)/shard_map/unpack/pallas_call | solution.py:286
  (113 shorter events, 14.9 us)
Async XLA Ops:
  0.0 9.0 %copy-start = (bf16[5120,128]{1,0:T(8,128)(2,1)S(1)}, bf16[5120,128]{1,0:T(8,128)(2,1)}, u32[]{:S(2)}) copy-start(bf16[5120,128]{1,0:T(8,128)(2,1)} %refs_11_.7) | copy-start | bytes 3932164
  1.7 7.9 %copy-start.1 = (bf16[5120,128]{0,1:T(8,128)(2,1)}, bf16[5120,128]{0,1:T(8,128)(2,1)S(1)}, u32[]{:S(2)}) copy-start(bf16[5120,128]{0,1:T(8,128)(2,1)S(1)} %copy.19) | copy-start | bytes 3932164
  1.7 31.8 %collective-permute-start = (bf16[128,5120]{1,0:T(8,128)(2,1)S(1)}, bf16[128,5120]{1,0:T(8,128)(2,1)}, u32[]{:S(2)}, u32[]{:S(2)}) collective-permute-start(bf16[128,5120]{1,0:T(8,128)(2,1)S(1)} %bitcast.75), channel_id=1, source_target_pairs={{0,1},{1,0},{2,3},{3,2},{4,5},{5,4},{6,7},{7,6},{8,9},{9,8},{10,11... | collective-permute-start | bytes 3932168 | tf_op jit(solution)/shard_map/ppermute | solution.py:315
  5.4 52.4 %collective-permute-start.3 = (bf16[128,5120]{1,0:T(8,128)(2,1)S(1)}, bf16[128,5120]{1,0:T(8,128)(2,1)}, u32[]{:S(2)}, u32[]{:S(2)}) collective-permute-start(bf16[128,5120]{1,0:T(8,128)(2,1)S(1)} %bitcast.76), channel_id=1, source_target_pairs={{0,6},{1,7},{2,0},{3,1},{4,2},{5,3},{6,4},{7,5},{8,14},{9,15},{10,... | collective-permute-start | bytes 3932168 | tf_op jit(solution)/shard_map/ppermute | solution.py:36
  8.1 51.4 %collective-permute-start.1 = (bf16[128,5120]{1,0:T(8,128)(2,1)S(1)}, bf16[128,5120]{1,0:T(8,128)(2,1)}, u32[]{:S(2)}, u32[]{:S(2)}) collective-permute-start(bf16[128,5120]{1,0:T(8,128)(2,1)S(1)} %bitcast.77), channel_id=1, source_target_pairs={{0,2},{1,3},{2,4},{3,5},{4,6},{5,7},{6,0},{7,1},{8,10},{9,11},{10,... | collective-permute-start | bytes 3932168 | tf_op jit(solution)/shard_map/ppermute | solution.py:36
  22.8 162.1 %copy-start.11 = (s32[4]{0:T(128)}, s32[4]{0:T(128)S(1)}, u32[]{:S(2)}) copy-start(s32[4]{0:T(128)S(1)} %compare_select_fusion.2.refs_0_) | copy-start | bytes 52
  43.6 2.0 collective-permute-start.11
  44.3 5.5 %collective-permute-start.10 = (f32[128,128]{1,0:T(8,128)S(1)}, f32[128,128]{1,0:T(8,128)S(1)}, u32[]{:S(2)}, u32[]{:S(2)}) collective-permute-start(f32[128,128]{1,0:T(8,128)S(1)} %fusion.3), channel_id=1, source_target_pairs={{0,64},{1,65},{2,66},{3,67},{4,68},{5,69},{6,70},{7,71}} | collective-permute-start | bytes 196616 | tf_op jit(solution)/shard_map/ppermute | solution.py:341
  45.0 4.8 %collective-permute-start.9 = (f32[128,128]{1,0:T(8,128)S(1)}, f32[128,128]{1,0:T(8,128)S(1)}, u32[]{:S(2)}, u32[]{:S(2)}) collective-permute-start(f32[128,128]{1,0:T(8,128)S(1)} %fusion.3), channel_id=1, source_target_pairs={{0,32},{1,33},{2,34},{3,35},{4,36},{5,37},{6,38},{7,39}} | collective-permute-start | bytes 196616 | tf_op jit(solution)/shard_map/ppermute | solution.py:341
  45.7 26.2 %collective-permute-start.21 = (bf16[5120,128]{1,0:T(8,128)(2,1)S(1)}, bf16[5120,128]{1,0:T(8,128)(2,1)}, u32[]{:S(2)}, u32[]{:S(2)}) collective-permute-start(bf16[5120,128]{1,0:T(8,128)(2,1)S(1)} %copy-done), channel_id=1, source_target_pairs={{0,96},{8,104},{16,112},{24,120},{32,0},{40,8},{48,16},{56,24},{64... | collective-permute-start | bytes 3932168 | tf_op jit(solution)/shard_map/ppermute | solution.py:36
  49.8 24.5 %collective-permute-start.17 = (bf16[5120,128]{1,0:T(8,128)(2,1)S(1)}, bf16[5120,128]{1,0:T(8,128)(2,1)}, u32[]{:S(2)}, u32[]{:S(2)}) collective-permute-start(bf16[5120,128]{1,0:T(8,128)(2,1)S(1)} %copy-done), channel_id=1, source_target_pairs={{0,32},{8,40},{16,48},{24,56},{32,64},{40,72},{48,80},{56,88},{64,... | collective-permute-start | bytes 3932168 | tf_op jit(solution)/shard_map/ppermute | solution.py:36
  49.8 29.2 %collective-permute-start.15 = (bf16[5120,128]{1,0:T(8,128)(2,1)S(1)}, bf16[5120,128]{1,0:T(8,128)(2,1)}, u32[]{:S(2)}, u32[]{:S(2)}) collective-permute-start(bf16[5120,128]{1,0:T(8,128)(2,1)S(1)} %copy-done), channel_id=1, source_target_pairs={{0,8},{8,0},{16,24},{24,16},{32,40},{40,32},{48,56},{56,48},{64,72... | collective-permute-start | bytes 3932168 | tf_op jit(solution)/shard_map/ppermute | solution.py:312
  57.7 5.8 %collective-permute-start.12 = (f32[128,128]{1,0:T(8,128)S(1)}, f32[128,128]{1,0:T(8,128)S(1)}, u32[]{:S(2)}, u32[]{:S(2)}) collective-permute-start(f32[128,128]{1,0:T(8,128)S(1)} %add_select_fusion), channel_id=1, source_target_pairs={{0,16},{32,48},{64,80},{96,112},{1,17},{33,49},{65,81},{97,113},{2... | collective-permute-start | bytes 196616 | tf_op jit(solution)/shard_map/ppermute | solution.py:344
  59.5 25.4 %collective-permute-start.6 = (bf16[64,5120]{1,0:T(8,128)(2,1)S(1)}, bf16[64,5120]{1,0:T(8,128)(2,1)S(1)}, u32[]{:S(2)}, u32[]{:S(2)}) collective-permute-start(bf16[64,5120]{1,0:T(8,128)(2,1)S(1)} %slice.71), channel_id=1, source_target_pairs={{0,6},{1,7},{2,0},{3,1},{4,2},{5,3},{6,4},{7,5},{8,14},{9,15},{10,... | collective-permute-start | bytes 1966088 | tf_op jit(solution)/shard_map/ppermute | solution.py:42
  63.5 24.2 %collective-permute-start.5 = (bf16[64,5120]{1,0:T(8,128)(2,1)S(1)}, bf16[64,5120]{1,0:T(8,128)(2,1)}, u32[]{:S(2)}, u32[]{:S(2)}) collective-permute-start(bf16[64,5120]{1,0:T(8,128)(2,1)S(1)} %slice.70), channel_id=1, source_target_pairs={{0,2},{1,3},{2,4},{3,5},{4,6},{5,7},{6,0},{7,1},{8,10},{9,11},{10,... | collective-permute-start | bytes 1966088 | tf_op jit(solution)/shard_map/ppermute | solution.py:41
  71.9 10.4 %collective-permute-start.13 = (f32[128,128]{1,0:T(8,128)S(1)}, f32[128,128]{1,0:T(8,128)S(1)}, u32[]{:S(2)}, u32[]{:S(2)}) collective-permute-start(f32[128,128]{1,0:T(8,128)S(1)} %broadcast_select_fusion), channel_id=1, source_target_pairs={{0,8},{16,24},{32,40},{48,56},{64,72},{80,88},{96,104},{112,120},{... | collective-permute-start | bytes 196616 | tf_op jit(solution)/shard_map/ppermute | solution.py:349
  74.3 14.0 %collective-permute-start.26 = (bf16[2560,128]{1,0:T(8,128)(2,1)S(1)}, bf16[2560,128]{1,0:T(8,128)(2,1)S(1)}, u32[]{:S(2)}, u32[]{:S(2)}) collective-permute-start(bf16[2560,128]{1,0:T(8,128)(2,1)S(1)} %slice.75), channel_id=1, source_target_pairs={{0,96},{8,104},{16,112},{24,120},{32,0},{40,8},{48,16},{56,24},{64... | collective-permute-start | bytes 1966088 | tf_op jit(solution)/shard_map/ppermute | solution.py:42
  79.0 15.6 %collective-permute-start.25 = (bf16[2560,128]{1,0:T(8,128)(2,1)S(1)}, bf16[2560,128]{1,0:T(8,128)(2,1)S(1)}, u32[]{:S(2)}, u32[]{:S(2)}) collective-permute-start(bf16[2560,128]{1,0:T(8,128)(2,1)S(1)} %slice.74), channel_id=1, source_target_pairs={{0,32},{8,40},{16,48},{24,56},{32,64},{40,72},{48,80},{56,88},{64,... | collective-permute-start | bytes 1966088 | tf_op jit(solution)/shard_map/ppermute | solution.py:41
  82.3 28.2 %collective-permute-start.14 = (bf16[5120,128]{1,0:T(8,128)(2,1)S(1)}, bf16[5120,128]{1,0:T(8,128)(2,1)}, u32[]{:S(2)}, u32[]{:S(2)}) collective-permute-start(bf16[5120,128]{1,0:T(8,128)(2,1)S(1)} %copy-done), channel_id=1, source_target_pairs={{0,16},{8,24},{16,0},{24,8},{32,48},{40,56},{48,32},{56,40},{64,80... | collective-permute-start | bytes 3932168 | tf_op jit(solution)/shard_map/ppermute | solution.py:332
  85.0 31.1 %copy-start.7 = (bf16[64,5120]{1,0:T(8,128)(2,1)}, bf16[64,5120]{1,0:T(8,128)(2,1)S(1)}, u32[]{:S(2)}) copy-start(bf16[64,5120]{1,0:T(8,128)(2,1)S(1)} %collective-permute-done.6.refs_10_.refs_8_) | copy-start | bytes 1966084
  85.0 28.0 %collective-permute-start.4 = (bf16[128,5120]{1,0:T(8,128)(2,1)}, bf16[128,5120]{1,0:T(8,128)(2,1)S(1)}, u32[]{:S(2)}, u32[]{:S(2)}) collective-permute-start(bf16[128,5120]{1,0:T(8,128)(2,1)} %collective-permute-done.refs_4_.refs_2_), channel_id=1, source_target_pairs={{0,6},{1,7},{2,0},{3,1},{4,2},{5,3},{6,4},{7,5},{8,14},{9,15},{10,... | collective-permute-start | bytes 3932168 | tf_op jit(solution)/shard_map/ppermute | solution.py:36
  87.7 28.3 %collective-permute-start.2 = (bf16[128,5120]{1,0:T(8,128)(2,1)}, bf16[128,5120]{1,0:T(8,128)(2,1)S(1)}, u32[]{:S(2)}, u32[]{:S(2)}) collective-permute-start(bf16[128,5120]{1,0:T(8,128)(2,1)} %collective-permute-done.refs_4_.refs_2_), channel_id=1, source_target_pairs={{0,2},{1,3},{2,4},{3,5},{4,6},{5,7},{6,0},{7,1},{8,10},{9,11},{10,... | collective-permute-start | bytes 3932168 | tf_op jit(solution)/shard_map/ppermute | solution.py:36
  88.3 28.8 %collective-permute-start.23 = (bf16[5120,128]{1,0:T(8,128)(2,1)}, bf16[5120,128]{1,0:T(8,128)(2,1)S(1)}, u32[]{:S(2)}, u32[]{:S(2)}) collective-permute-start(bf16[5120,128]{1,0:T(8,128)(2,1)} %collective-permute-done.21.refs_21_.refs_19_), channel_id=1, source_target_pairs={{0,8},{8,0},{16,24},{24,16},{32,40},{40,32},{48,56},{56,48},{64,72... | collective-permute-start | bytes 3932168 | tf_op jit(solution)/shard_map/ppermute | solution.py:312
  94.7 26.1 %collective-permute-start.19 = (bf16[5120,128]{1,0:T(8,128)(2,1)}, bf16[5120,128]{1,0:T(8,128)(2,1)}, u32[]{:S(2)}, u32[]{:S(2)}) collective-permute-start(bf16[5120,128]{1,0:T(8,128)(2,1)} %collective-permute-done.17.refs_17_.refs_15_), channel_id=1, source_target_pairs={{0,8},{8,0},{16,24},{24,16},{32,40},{40,32},{48,56},{56,48},{64,72... | collective-permute-start | bytes 3932168 | tf_op jit(solution)/shard_map/ppermute | solution.py:312
  110.4 28.7 %collective-permute-start.27 = (bf16[5120,128]{1,0:T(8,128)(2,1)}, bf16[5120,128]{1,0:T(8,128)(2,1)S(1)}, u32[]{:S(2)}, u32[]{:S(2)}) collective-permute-start(bf16[5120,128]{1,0:T(8,128)(2,1)} %constant_dynamic-update-slice_fusion.refs_25_.refs_23_), channel_id=1, source_target_pairs={{0,16},{8,24},{16,0},{24,8},{32,48},{40,56},{48,32},{56,40},{64,80... | collective-permute-start | bytes 3932168 | tf_op jit(solution)/shard_map/ppermute | solution.py:347
  113.0 3.1 copy-start.2
  113.0 29.8 %collective-permute-start.22 = (bf16[5120,128]{1,0:T(8,128)(2,1)}, bf16[5120,128]{1,0:T(8,128)(2,1)}, u32[]{:S(2)}, u32[]{:S(2)}) collective-permute-start(bf16[5120,128]{1,0:T(8,128)(2,1)} %collective-permute-done.14.refs_14_.refs_12_), channel_id=1, source_target_pairs={{0,96},{8,104},{16,112},{24,120},{32,0},{40,8},{48,16},{56,24},{64... | collective-permute-start | bytes 3932168 | tf_op jit(solution)/shard_map/ppermute | solution.py:36
  116.0 1.1 copy-start.3
  116.0 28.6 %collective-permute-start.18 = (bf16[5120,128]{1,0:T(8,128)(2,1)}, bf16[5120,128]{1,0:T(8,128)(2,1)}, u32[]{:S(2)}, u32[]{:S(2)}) collective-permute-start(bf16[5120,128]{1,0:T(8,128)(2,1)} %collective-permute-done.14.refs_14_.refs_12_), channel_id=1, source_target_pairs={{0,32},{8,40},{16,48},{24,56},{32,64},{40,72},{48,80},{56,88},{64,... | collective-permute-start | bytes 3932168 | tf_op jit(solution)/shard_map/ppermute | solution.py:36
  117.1 1.1 copy-start.4
  118.2 12.1 %collective-permute-start.8 = (bf16[64,5120]{1,0:T(8,128)(2,1)S(1)}, bf16[64,5120]{1,0:T(8,128)(2,1)S(1)}, u32[]{:S(2)}, u32[]{:S(2)}) collective-permute-start(bf16[64,5120]{1,0:T(8,128)(2,1)S(1)} %slice.73), channel_id=1, source_target_pairs={{0,6},{1,7},{2,0},{3,1},{4,2},{5,3},{6,4},{7,5},{8,14},{9,15},{10,... | collective-permute-start | bytes 1966088 | tf_op jit(solution)/shard_map/ppermute | solution.py:42
  120.8 14.9 %collective-permute-start.7 = (bf16[64,5120]{1,0:T(8,128)(2,1)S(1)}, bf16[64,5120]{1,0:T(8,128)(2,1)S(1)}, u32[]{:S(2)}, u32[]{:S(2)}) collective-permute-start(bf16[64,5120]{1,0:T(8,128)(2,1)S(1)} %slice.72), channel_id=1, source_target_pairs={{0,2},{1,3},{2,4},{3,5},{4,6},{5,7},{6,0},{7,1},{8,10},{9,11},{10,... | collective-permute-start | bytes 1966088 | tf_op jit(solution)/shard_map/ppermute | solution.py:41
  130.3 21.4 %copy-start.8 = (bf16[64,5120]{1,0:T(8,128)(2,1)}, bf16[64,5120]{1,0:T(8,128)(2,1)S(1)}, u32[]{:S(2)}) copy-start(bf16[64,5120]{1,0:T(8,128)(2,1)S(1)} %collective-permute-done.8.refs_12_.refs_10_) | copy-start | bytes 1966084
  130.3 19.1 %collective-permute-start.28 = (bf16[5120,128]{1,0:T(8,128)(2,1)}, bf16[5120,128]{1,0:T(8,128)(2,1)S(1)}, u32[]{:S(2)}, u32[]{:S(2)}) collective-permute-start(bf16[5120,128]{1,0:T(8,128)(2,1)} %constant_dynamic-update-slice_fusion.refs_25_.refs_23_), channel_id=1, source_target_pairs={{0,8},{8,0},{16,24},{24,16},{32,40},{40,32},{48,56},{56,48},{64,72... | collective-permute-start | bytes 3932168 | tf_op jit(solution)/shard_map/ppermute | solution.py:312
  135.7 3.4 %copy-start.9 = (bf16[64,5120]{1,0:T(8,128)(2,1)}, bf16[64,5120]{1,0:T(8,128)(2,1)S(1)}, u32[]{:S(2)}) copy-start(bf16[64,5120]{1,0:T(8,128)(2,1)S(1)} %collective-permute-done.7.refs_11_.refs_9_) | copy-start | bytes 1966084
  135.7 13.6 %collective-permute-start.16 = (bf16[5120,128]{1,0:T(8,128)(2,1)}, bf16[5120,128]{1,0:T(8,128)(2,1)}, u32[]{:S(2)}, u32[]{:S(2)}) collective-permute-start(bf16[5120,128]{1,0:T(8,128)(2,1)} %collective-permute-done.14.refs_14_.refs_12_), channel_id=1, source_target_pairs={{0,8},{8,0},{16,24},{24,16},{32,40},{40,32},{48,56},{56,48},{64,72... | collective-permute-start | bytes 3932168 | tf_op jit(solution)/shard_map/ppermute | solution.py:312
  139.2 12.6 %copy-start.5 = (bf16[5120,128]{1,0:T(8,128)(2,1)}, bf16[5120,128]{1,0:T(8,128)(2,1)S(1)}, u32[]{:S(2)}) copy-start(bf16[5120,128]{1,0:T(8,128)(2,1)S(1)} %collective-permute-done.27.refs_26_.refs_24_) | copy-start | bytes 3932164
  139.2 10.2 %collective-permute-start.29 = (bf16[5120,128]{1,0:T(8,128)(2,1)S(1)}, bf16[5120,128]{1,0:T(8,128)(2,1)}, u32[]{:S(2)}, u32[]{:S(2)}) collective-permute-start(bf16[5120,128]{1,0:T(8,128)(2,1)S(1)} %collective-permute-done.27.refs_26_.refs_24_), channel_id=1, source_target_pairs={{0,8},{8,0},{16,24},{24,16},{32,40},{40,32},{48,56},{56,48},{64,72... | collective-permute-start | bytes 3932168 | tf_op jit(solution)/shard_map/ppermute | solution.py:312
  142.8 6.6 %collective-permute-start.24 = (bf16[5120,128]{1,0:T(8,128)(2,1)}, bf16[5120,128]{1,0:T(8,128)(2,1)}, u32[]{:S(2)}, u32[]{:S(2)}) collective-permute-start(bf16[5120,128]{1,0:T(8,128)(2,1)} %collective-permute-done.22.refs_22_.refs_20_), channel_id=1, source_target_pairs={{0,8},{8,0},{16,24},{24,16},{32,40},{40,32},{48,56},{56,48},{64,72... | collective-permute-start | bytes 3932168 | tf_op jit(solution)/shard_map/ppermute | solution.py:312
  144.6 7.1 %collective-permute-start.20 = (bf16[5120,128]{1,0:T(8,128)(2,1)}, bf16[5120,128]{1,0:T(8,128)(2,1)}, u32[]{:S(2)}, u32[]{:S(2)}) collective-permute-start(bf16[5120,128]{1,0:T(8,128)(2,1)} %collective-permute-done.18.refs_18_.refs_16_), channel_id=1, source_target_pairs={{0,8},{8,0},{16,24},{24,16},{32,40},{40,32},{48,56},{56,48},{64,72... | collective-permute-start | bytes 3932168 | tf_op jit(solution)/shard_map/ppermute | solution.py:312
  149.4 2.4 copy-start.6
  162.9 13.4 %copy-start.12 = (s32[16]{0:T(128)S(1)}, s32[16]{0:T(128)}, u32[]{:S(2)}) copy-start(s32[16]{0:T(128)} %param.5) | copy-start | bytes 196
  163.1 9.3 %collective-permute-start.30 = (f32[4,128,128]{1,2,0:T(8,128)S(1)}, f32[4,128,128]{1,2,0:T(8,128)S(1)}, u32[]{:S(2)}, u32[]{:S(2)}) collective-permute-start(f32[4,128,128]{1,2,0:T(8,128)S(1)} %bitcast.100), channel_id=1, source_target_pairs={{0,1},{8,9},{16,17},{24,25},{32,33},{40,41},{48,49},{56,57},{64,65... | collective-permute-start | bytes 786440 | tf_op jit(solution)/shard_map/ppermute | solution.py:364
  172.4 4.0 %collective-permute-start.32 = (f32[128,128]{0,1:T(8,128)S(1)}, f32[128,128]{0,1:T(8,128)S(1)}, u32[]{:S(2)}, u32[]{:S(2)}) collective-permute-start(f32[128,128]{0,1:T(8,128)S(1)} %get-tuple-element.65), channel_id=1, source_target_pairs={{0,4},{1,5},{8,12},{9,13},{16,20},{17,21},{24,28},{25,29},{32,36},... | collective-permute-start | bytes 196616 | tf_op jit(solution)/shard_map/ppermute | solution.py:367
  173.7 2.7 collective-permute-start.33
  175.0 2.6 collective-permute-start.31
  177.7 3.9 %collective-permute-start.38 = (f32[128,128]{0,1:T(8,128)S(1)}, f32[128,128]{0,1:T(8,128)S(1)}, u32[]{:S(2)}, u32[]{:S(2)}) collective-permute-start(f32[128,128]{0,1:T(8,128)S(1)} %get-tuple-element.60), channel_id=1, source_target_pairs={{0,16},{8,24},{16,0},{24,8},{32,48},{40,56},{48,32},{56,40},{64,80... | collective-permute-start | bytes 196616 | tf_op jit(solution)/shard_map/ppermute | solution.py:372
  177.8 30.8 %collective-permute-start.34 = (f32[128,128]{0,1:T(8,128)S(1)}, f32[128,128]{0,1:T(8,128)S(1)}, u32[]{:S(2)}, u32[]{:S(2)}) collective-permute-start(f32[128,128]{0,1:T(8,128)S(1)} %get-tuple-element.60), channel_id=1, source_target_pairs={{0,1},{1,0},{2,3},{3,2},{4,5},{5,4},{6,7},{7,6},{8,9},{9,8},{10,11... | collective-permute-start | bytes 196616 | tf_op jit(solution)/shard_map/ppermute | solution.py:370
  181.7 31.1 %collective-permute-start.40 = (f32[2,128,128]{1,0,2:T(2,128)S(1)}, f32[2,128,128]{1,0,2:T(2,128)S(1)}, u32[]{:S(2)}, u32[]{:S(2)}) collective-permute-start(f32[2,128,128]{1,0,2:T(2,128)S(1)} %get-tuple-element.69), channel_id=1, source_target_pairs={{0,96},{8,104},{16,112},{24,120},{32,0},{40,8},{48,16},{56,24},{64... | collective-permute-start | bytes 393224 | tf_op jit(solution)/shard_map/ppermute | solution.py:47
  183.7 29.2 %collective-permute-start.39 = (f32[2,128,128]{1,0,2:T(2,128)S(1)}, f32[2,128,128]{1,0,2:T(2,128)S(1)}, u32[]{:S(2)}, u32[]{:S(2)}) collective-permute-start(f32[2,128,128]{1,0,2:T(2,128)S(1)} %get-tuple-element.69), channel_id=1, source_target_pairs={{0,32},{8,40},{16,48},{24,56},{32,64},{40,72},{48,80},{56,88},{64,... | collective-permute-start | bytes 393224 | tf_op jit(solution)/shard_map/ppermute | solution.py:47
  183.7 29.2 %collective-permute-start.41 = (f32[2,128,128]{1,0,2:T(2,128)S(1)}, f32[2,128,128]{1,0,2:T(2,128)S(1)}, u32[]{:S(2)}, u32[]{:S(2)}) collective-permute-start(f32[2,128,128]{1,0,2:T(2,128)S(1)} %get-tuple-element.69), channel_id=1, source_target_pairs={{0,64},{8,72},{16,80},{24,88},{32,96},{40,104},{48,112},{56,120},{... | collective-permute-start | bytes 393224 | tf_op jit(solution)/shard_map/ppermute | solution.py:47
  208.6 10.5 %collective-permute-start.37 = (f32[2,128,128]{1,2,0:T(8,128)S(1)}, f32[2,128,128]{1,2,0:T(8,128)S(1)}, u32[]{:S(2)}, u32[]{:S(2)}) collective-permute-start(f32[2,128,128]{1,2,0:T(8,128)S(1)} %pad_maximum_fusion.3), channel_id=1, source_target_pairs={{0,4},{1,5},{2,6},{3,7},{4,0},{5,1},{6,2},{7,3},{8,12},{9,13},{10,... | collective-permute-start | bytes 393224 | tf_op jit(solution)/shard_map/ppermute | solution.py:47
  209.3 9.7 %collective-permute-start.36 = (f32[2,128,128]{1,2,0:T(8,128)S(1)}, f32[2,128,128]{1,2,0:T(8,128)S(1)}, u32[]{:S(2)}, u32[]{:S(2)}) collective-permute-start(f32[2,128,128]{1,2,0:T(8,128)S(1)} %pad_maximum_fusion.3), channel_id=1, source_target_pairs={{0,6},{1,7},{2,0},{3,1},{4,2},{5,3},{6,4},{7,5},{8,14},{9,15},{10,... | collective-permute-start | bytes 393224 | tf_op jit(solution)/shard_map/ppermute | solution.py:47
  212.8 6.2 %collective-permute-start.35 = (f32[2,128,128]{1,2,0:T(8,128)S(1)}, f32[2,128,128]{1,2,0:T(8,128)S(1)}, u32[]{:S(2)}, u32[]{:S(2)}) collective-permute-start(f32[2,128,128]{1,2,0:T(8,128)S(1)} %pad_maximum_fusion.3), channel_id=1, source_target_pairs={{0,2},{1,3},{2,4},{3,5},{4,6},{5,7},{6,0},{7,1},{8,10},{9,11},{10,... | collective-permute-start | bytes 393224 | tf_op jit(solution)/shard_map/ppermute | solution.py:47
  213.1 7.3 %collective-permute-start.42 = (f32[4,2,128,128]{2,1,0,3:T(2,128)S(1)}, f32[4,2,128,128]{2,1,0,3:T(2,128)S(1)}, u32[]{:S(2)}, u32[]{:S(2)}) collective-permute-start(f32[4,2,128,128]{2,1,0,3:T(2,128)S(1)} %pad_maximum_fusion.2), channel_id=1, source_target_pairs={{0,8},{8,0},{16,24},{24,16},{32,40},{40,32},{48,56},{56,48},{64,72... | collective-permute-start | bytes 1572872 | tf_op jit(solution)/shard_map/ppermute | solution.py:374
  234.3 42.2 %all-to-all-start.1 = ((s16[16,528,128]{2,1,0:T(8,128)(2,1)}), s16[16,528,128]{2,1,0:T(8,128)(2,1)S(1)}, u32[]{:S(2)}, u32[]{:S(2)}) async-start(s16[16,528,128]{2,1,0:T(8,128)(2,1)} %bitcast.87), calls=%async_computation.1 | async-start | bytes 4325376 | tf_op jit(solution)/shard_map/all_to_all | solution.py:405
  276.4 1.4 copy-start.10
  277.8 33.1 %all-to-all-start = ((s16[16,528,128]{2,1,0:T(8,128)(2,1)}), s16[16,528,128]{2,1,0:T(8,128)(2,1)}, u32[]{:S(2)}, u32[]{:S(2)}) async-start(s16[16,528,128]{2,1,0:T(8,128)(2,1)} %bitcast.88), calls=%async_computation | async-start | bytes 4325376 | tf_op jit(solution)/shard_map/all_to_all | solution.py:405
